TPU v7x, 256 devices: a whole 4x4x8 slice. The times are simulated.
256 devices in a mesh: seq: 32 (over z_lo, x, core), tp: 8 (over y, z_hi).
Axes of the slice: x: 4, y: 4, z: 8 (z_hi: 2, z_lo: 4; z = z_hi * 4 + z_lo), core: 2. Of those that a mesh axis runs over, the one named last changes fastest.
Arguments:
- hidden: bfloat16 [8192, 7168], P('seq', 'tp'), may hold values from -6 to 6
- norm_gain: bfloat16 [7168], replicated, may hold values from 0.5 to 1.5
- w_query: bfloat16 [7168, 4096], P(None, 'tp'), may hold values from -0.0625 to 0.0625
- w_key: bfloat16 [7168, 1024], P(None, 'tp'), may hold values from -0.0625 to 0.0625
- w_value: bfloat16 [7168, 1024], P(None, 'tp'), may hold values from -0.0625 to 0.0625
- prefix_keys: bfloat16 [8192, 1024], P('seq', 'tp'), may hold values from -64 to 64
- prefix_values: bfloat16 [8192, 1024], P('seq', 'tp'), may hold values from -6 to 6
- page_prefix: int32 [64], replicated, may hold values from 0 to 3, as said below
- request_prefix: int32 [32], replicated, may hold values from 0 to 3
- suffix_lengths: int32 [32], replicated, may hold values from 1 to 1024, 8192 in all
- row_order: int32 [8192], replicated, may hold values from 0 to 8191, as said below
Outputs:
- attended: bfloat16 [8192, 4096], P('seq', 'tp')
- suffix_keys: bfloat16 [8192, 1024], P('seq', 'tp')
- suffix_values: bfloat16 [8192, 1024], P('seq', 'tp')
Inputs may be any that keep to these rules, and one draw needn't show every extreme that they name: `page_prefix`: each of the 4 prefixes owns exactly 16 pages. `suffix_lengths`: the lengths sum to 8192; the longest is exactly 1024. `row_order`: a permutation of 0 to 8191 made of aligned runs of 128 consecutive values.
All inputs are finite; a program needn't handle non-finite values.
Results may differ from a plain program's by a relative error of at most 0.0075.
The roundings to bfloat16 on the way count: a program that leaves them out, or rounds other values in their place, can miss the bound.
Values may be sent and summed in bfloat16 or wider, within the bound.
A program may use at most 128 MiB of HBM per device.

v0:
```python
import math

import jax
import jax.numpy as jnp
from jax import lax
from jax.sharding import PartitionSpec as P

HEAD = 128
PAGE = 128
PREFIXES = 4


ROPE_BASE = 5000000.0


def rotate(tensor_in, positions):
    head_dim = tensor_in.shape[-1]
    half_dim = head_dim // 2
    frequency = ROPE_BASE ** (-(jnp.arange(half_dim, dtype=jnp.float32) * 2.0 / head_dim))
    angles = positions.astype(jnp.float32)[:, None] * frequency[None, :]
    cosine = jnp.cos(angles)[:, None, :]
    sine_part = jnp.sin(angles)[:, None, :]
    first_half = tensor_in[..., :half_dim]
    second_half = tensor_in[..., half_dim:]
    return jnp.concatenate(
        [
            first_half * cosine - second_half * sine_part,
            second_half * cosine + first_half * sine_part,
        ],
        axis=-1,
    )


def locate(row_order, suffix_lengths, request_prefix):
    end_rows = jnp.cumsum(suffix_lengths)
    starts = end_rows - suffix_lengths
    numbers = jnp.arange(suffix_lengths.shape[0], dtype=jnp.int32)
    request = jnp.sum((row_order[:, None] >= end_rows[None, :]).astype(jnp.int32), axis=1)
    chosen = request[:, None] == numbers[None, :]
    position = row_order - jnp.sum(jnp.where(chosen, starts[None, :], 0), axis=1)
    wanted = jnp.sum(jnp.where(chosen, request_prefix[None, :], 0), axis=1)
    return (request, position, wanted)


def body(
    hidden,
    norm_gain,
    w_query,
    w_key,
    w_value,
    prefix_keys,
    prefix_values,
    page_prefix,
    request_prefix,
    suffix_lengths,
    row_order,
):
    gathered = lax.all_gather(hidden, "tp", axis=1, tiled=True)
    local_rows = gathered.shape[0]
    hidden_f = gathered.astype(jnp.float32)
    mean_sq = jnp.mean(hidden_f * hidden_f, axis=1, keepdims=True)
    normed = (
        hidden_f * lax.rsqrt(mean_sq + 1e-05) * norm_gain.astype(jnp.float32)[None, :]
    ).astype(jnp.bfloat16)
    request_all, position_all, wanted_all = locate(row_order, suffix_lengths, request_prefix)
    offset = lax.axis_index("seq") * local_rows
    request = lax.dynamic_slice_in_dim(request_all, offset, local_rows)
    position = lax.dynamic_slice_in_dim(position_all, offset, local_rows)
    wanted = lax.dynamic_slice_in_dim(wanted_all, offset, local_rows)
    prefix_len = page_prefix.shape[0] * PAGE // PREFIXES
    rope_at = prefix_len + position
    q_heads = w_query.shape[1] // HEAD
    kv_heads = w_key.shape[1] // HEAD
    group_size = q_heads // kv_heads
    queries = rotate(
        jnp.dot(normed, w_query, preferred_element_type=jnp.float32).reshape(
            local_rows, q_heads, HEAD
        ),
        rope_at,
    ).astype(jnp.bfloat16)
    queries = queries.reshape(local_rows, kv_heads, group_size, HEAD)
    new_keys = rotate(
        jnp.dot(normed, w_key, preferred_element_type=jnp.float32).reshape(
            local_rows, kv_heads, HEAD
        ),
        rope_at,
    ).astype(jnp.bfloat16)
    new_keys = new_keys.reshape(local_rows, kv_heads * HEAD)
    new_values = jnp.dot(normed, w_value, preferred_element_type=jnp.float32).astype(jnp.bfloat16)
    row_pages = jnp.repeat(page_prefix, PAGE)
    score_scale = 1.0 / math.sqrt(HEAD)
    initial = (
        jnp.full((kv_heads, local_rows, group_size), -1e30, jnp.float32),
        jnp.zeros((kv_heads, local_rows, group_size), jnp.float32),
        jnp.zeros((kv_heads, local_rows, group_size, HEAD), jnp.float32),
    )

    def attend(state, key_rows, value_rows, visible):
        row_count = key_rows.shape[0]
        block_width = math.gcd(row_count, 512)
        block_count = row_count // block_width
        key_blocks = key_rows.reshape(block_count, block_width, kv_heads, HEAD)
        value_blocks = value_rows.reshape(block_count, block_width, kv_heads, HEAD)
        mask_blocks = visible.reshape(local_rows, block_count, block_width).transpose(1, 0, 2)

        def step(carry_in, inputs):
            run_max, run_sum, run_acc = carry_in
            key_block, value_block, mask_block = inputs
            scores = (
                jnp.einsum("tngd,knd->ntgk", queries, key_block, preferred_element_type=jnp.float32)
                * score_scale
            )
            seen = mask_block[None, :, None, :]
            new_max = jnp.maximum(run_max, jnp.max(jnp.where(seen, scores, -1e30), axis=-1))
            weights = jnp.where(seen, jnp.exp(scores - new_max[..., None]), 0.0)
            fade = jnp.exp(run_max - new_max)
            run_sum = run_sum * fade + jnp.sum(weights, axis=-1)
            run_acc = run_acc * fade[..., None] + jnp.einsum(
                "ntgk,knd->ntgd",
                weights.astype(jnp.bfloat16),
                value_block,
                preferred_element_type=jnp.float32,
            )
            return ((new_max, run_sum, run_acc), None)

        result, unused = lax.scan(step, state, (key_blocks, value_blocks, mask_blocks))
        return result

    key_rows = lax.all_gather(prefix_keys, "seq", axis=0, tiled=True)
    value_rows = lax.all_gather(prefix_values, "seq", axis=0, tiled=True)
    visible = wanted[:, None] == row_pages[None, :]
    state = attend(initial, key_rows, value_rows, visible)
    key_rows = lax.all_gather(new_keys, "seq", axis=0, tiled=True)
    value_rows = lax.all_gather(new_values, "seq", axis=0, tiled=True)
    visible = (request[:, None] == request_all[None, :]) & (
        position_all[None, :] <= position[:, None]
    )
    state = attend(state, key_rows, value_rows, visible)
    run_max, run_sum, run_acc = state
    attended = (
        (run_acc / run_sum[..., None])
        .transpose(1, 0, 2, 3)
        .reshape(local_rows, q_heads * HEAD)
        .astype(jnp.bfloat16)
    )
    return (attended, new_keys, new_values)


def solution(mesh):
    return jax.shard_map(
        body,
        mesh=mesh,
        in_specs=(
            P("seq", "tp"),
            P(),
            P(None, "tp"),
            P(None, "tp"),
            P(None, "tp"),
            P("seq", "tp"),
            P("seq", "tp"),
            P(),
            P(),
            P(),
            P(),
        ),
        out_specs=(P("seq", "tp"), P("seq", "tp"), P("seq", "tp")),
        check_vma=False,
    )
```

profile of v0, /device:TPU:165, one launch (start us, length us, event | category | flops | bytes accessed | tf_op | source)
XLA Modules:
  0.0 433.1 jit_solution(14165126439068676029)
XLA Ops:
  14.6 90.8 %all-gather.8.cloned.1.call-done = bf16[256,7168]{1,0:T(8,128)(2,1)} async-done(((bf16[256,896]{1,0:T(8,128)(2,1)}), bf16[256,7168]{1,0:T(8,128)(2,1)}) %all-gather.8.cloned.1.call-update) | async-done | bytes 3670032 | tf_op jit(solution)/shard_map/all_gather | solution.py:58
  105.4 3.0 fusion.44
  112.2 2.8 broadcast_compare_fusion
  115.0 4.7 %compare_and_fusion = pred[16,256,512]{1,2,0:T(8,128)(4,1)} fusion(s32[256]{0:T(256)S(1)} %get-tuple-element.194, s32[16,512]{1,0:T(8,128)S(1)} %le.17, s32[16,512]{1,0:T(8,128)S(1)} %eq.52, s32[256]{0:T(256)S(1)} %dynamic_slice.31), kind=kLoop, calls=%fused_computation.60 | loop fusion | flops 6291456 | bytes 2164736 | tf_op jit(solution)/shard_map/and | solution.py:135
  119.7 6.0 %fusion.61 = f32[256,512]{1,0:T(8,128)} fusion(bf16[7168,512]{1,0:T(8,128)(2,1)} %param.17, bf16[256,7168]{1,0:T(8,128)(2,1)S(1)} %copy-done.3, f32[7168]{0:T(1024)S(1)} %convert_element_type.47, f32[256]{0:T(256)S(1)} %add_rsqrt_fusion), kind=kOutput, calls=%fused_computation.97 | convolution fusion | flops 1886388224 | bytes 11564032 | tf_op jit(solution)/shard_map/dot_general | solution.py:76
  129.0 3.5 convolution_convert_fusion
  132.5 33.1 %all-gather.6.cloned.1.call-done = bf16[8192,128]{1,0:T(8,128)(2,1)} async-done(((bf16[256,128]{1,0:T(8,128)(2,1)}), bf16[8192,128]{1,0:T(8,128)(2,1)}) %all-gather.6.cloned.1.call-update) | async-done | bytes 2097168 | tf_op jit(solution)/shard_map/all_gather | solution.py:129
  165.6 61.0 %all-gather.10.cloned.1.call-done = bf16[8192,128]{1,0:T(8,128)(2,1)} async-done(((bf16[256,128]{1,0:T(8,128)(2,1)}), bf16[8192,128]{1,0:T(8,128)(2,1)}) %all-gather.10.cloned.1.call-update) | async-done | bytes 2097168 | tf_op jit(solution)/shard_map/all_gather | solution.py:130
  226.5 107.5 %while.30 = (s32[]{:T(128)}, f32[1,256,4]{1,2,0:T(4,128)S(1)}, f32[1,256,4]{1,2,0:T(4,128)S(1)}, f32[1,256,4,128]{3,1,2,0:T(8,128)S(1)}, pred[16,256,512]{1,2,0:...) while((s32[]{:T(128)}, f32[1,256,4]{1,2,0:T(4,128)S(1)}, ...), condition=%wide.region_8.9_spmd.clone, body=%wide.region_5.8_spmd.clone.sunk | while | flops 274601984 | bytes 16974992 | solution.py:126
  234.2 2.7 fusion.87
  240.9 2.7 fusion.87
  254.3 2.7 fusion.87
  261.0 2.7 fusion.87
  267.8 2.7 fusion.87
  274.5 2.7 fusion.87
  281.2 2.7 fusion.87
  287.9 2.7 fusion.87
  301.3 2.7 fusion.87
  308.0 2.7 fusion.87
  314.7 2.7 fusion.87
  321.5 2.7 fusion.87
  334.7 4.1 copy.43
  338.8 14.0 %all-gather.14.cloned.1.call-done = bf16[8192,128]{1,0:T(8,128)(2,1)} async-done(((bf16[256,128]{1,0:T(8,128)(2,1)}), bf16[8192,128]{1,0:T(8,128)(2,1)}) %all-gather.14.cloned.1.call-update) | async-done | bytes 2097168 | tf_op jit(solution)/shard_map/all_gather | solution.py:134
  352.8 72.6 %while.29 = (s32[]{:T(128)}, f32[1,256,4]{1,2,0:T(4,128)S(1)}, f32[1,256,4]{1,2,0:T(4,128)S(1)}, f32[1,256,4,128]{3,1,2,0:T(8,128)S(1)}, pred[16,256,512]{1,2,0:...) while((s32[]{:T(128)}, f32[1,256,4]{1,2,0:T(4,128)S(1)}, ...), condition=%wide.region_12.13_spmd, body=%wide.region_9.12_spmd.sunk | while | flops 274467840 | bytes 8586337 | solution.py:126
  (300 shorter events, 162.4 us)
Async XLA Ops:
  7.2 101.2 %copy-start = (bf16[7168,128]{1,0:T(8,128)(2,1)S(1)}, bf16[7168,128]{1,0:T(8,128)(2,1)}, u32[]{:S(2)}) copy-start(bf16[7168,128]{1,0:T(8,128)(2,1)} %param.18) | copy-start | bytes 5505028
  7.2 98.2 %all-gather.8.cloned.1.call-start = ((), (), s32[]{:S(2)}) async-start(), calls=%async_computation.1 | async-start | bytes 4128768 | tf_op jit(solution)/shard_map/all_gather | solution.py:58
  7.9 157.6 %all-gather.6.cloned.1.call-start = ((), (), s32[]{:S(2)}) async-start(), calls=%async_computation | async-start | bytes 2162688 | tf_op jit(solution)/shard_map/all_gather | solution.py:129
  8.7 217.8 %all-gather.10.cloned.1.call-start = ((), (), s32[]{:S(2)}) async-start(), calls=%async_computation.2 | async-start | bytes 2162688 | tf_op jit(solution)/shard_map/all_gather | solution.py:130
  9.4 325.3 %all-gather.12.cloned.1.call-start = ((), (), s32[]{:S(2)}) async-start(), calls=%async_computation.3 | async-start | bytes 2162688 | tf_op jit(solution)/shard_map/all_gather | solution.py:133
  105.4 3.1 copy-start.2
  108.5 3.0 copy-start.6
  111.1 241.7 %all-gather.14.cloned.1.call-start = ((), (), s32[]{:S(2)}) async-start(), calls=%async_computation.4 | async-start | bytes 2162688 | tf_op jit(solution)/shard_map/all_gather | solution.py:134
  112.2 7.5 %copy-start.3 = (bf16[256,7168]{1,0:T(8,128)(2,1)S(1)}, bf16[256,7168]{1,0:T(8,128)(2,1)}, u32[]{:S(2)}) copy-start(bf16[256,7168]{1,0:T(8,128)(2,1)} %all-gather.8.cloned.1.call-done) | copy-start | bytes 11010052
  226.5 107.5 %copy-start.5 = (bf16[256,128]{0,1:T(8,128)(2,1)S(1)}, bf16[256,128]{0,1:T(8,128)(2,1)}, u32[]{:S(2)}) copy-start(bf16[256,128]{0,1:T(8,128)(2,1)} %pad_maximum_fusion.1) | copy-start | bytes 196612
  230.2 2.6 copy-start.1
  236.9 2.6 copy-start.1
  243.6 2.6 copy-start.1
  250.3 2.6 copy-start.1
  257.0 2.6 copy-start.1
  263.7 2.6 copy-start.1
  270.5 2.6 copy-start.1
  277.2 2.6 copy-start.1
  290.6 2.6 copy-start.1
  297.3 2.6 copy-start.1
  310.7 2.6 copy-start.1
  317.5 2.6 copy-start.1
  324.2 2.6 copy-start.1
  330.9 2.6 copy-start.1
  (3 other events, 7.1 us)
Sparse Core Ops, SparseCore 0:
  10.6 94.6 all-gather.7
  107.2 58.2 all-gather.5
  167.4 59.0 all-gather.9
  228.7 62.8 all-gather.11
  293.9 58.8 all-gather.13
where the time goes:
time: 440 us; the launch traced here: 433 us
  waiting for transfers between devices  201 us (46%)
  matrix products  144 us (33%)
  local copies, waits for them, and re-layouts  39.5 us (9%)
  other arithmetic  32.5 us (7%)
  between operations  13.9 us (3%)
    all_gather x1, waiting for transfers between devices, body(): gathered = lax.all_gather(hidden, 'tp', axis=1, tiled=True)  90.8 us
    dot_general x32, matrix products, step(): jnp.einsum('ntgk,knd->ntgd', weights.astype(jnp.bfloat16), value_block, p...  67.8 us
    dot_general x32, matrix products, step(): jnp.einsum('tngd,knd->ntgk', queries, key_block, preferred_element_type=j...  65.6 us
    all_gather x1, waiting for transfers between devices, body(): value_rows = lax.all_gather(prefix_values, 'seq', axis=0, tiled=True)  61 us
    all_gather x1, waiting for transfers between devices, body(): key_rows = lax.all_gather(prefix_keys, 'seq', axis=0, tiled=True)  33.1 us
    broadcast_in_dim x32, local copies, waits for them, and re-layouts, step(): jnp.where(seen, scores, -1e+30)  29.4 us
    reduce_sum x32, other arithmetic, step(): run_sum = run_sum * fade + jnp.sum(weights, axis=-1)  14.8 us
    all_gather x1, waiting for transfers between devices, body(): value_rows = lax.all_gather(new_values, 'seq', axis=0, tiled=True)  14 us
  transfers between devices with their start and end apart: 5, of which 4 were waited for; matrix products, arithmetic and copies ran while one was open for 33% of the time, Pallas kernels for 0%

commit v1 on v0

--- a/solution.py
+++ b/solution.py
@@ -1,9 +1,12 @@
+import functools
 import math
 
 import jax
 import jax.numpy as jnp
 from jax import lax
 from jax.sharding import PartitionSpec as P
+from jax.experimental import pallas as pl
+from jax.experimental.pallas import tpu as pltpu
 
 HEAD = 128
 PAGE = 128
@@ -42,7 +45,72 @@
     return (request, position, wanted)
 
 
+def seq_gather_kernel(n, x_ref, o_ref, send_sem, recv_sem, local_sem):
+    me = lax.axis_index("seq")
+    parts = x_ref.shape[0]
+    mesh_id = pl.DeviceIdType.MESH
+    barrier = pltpu.get_barrier_semaphore()
+
+    def greet(k, carry):
+        peer = lax.rem(me + k, n)
+        pl.semaphore_signal(barrier, inc=1, device_id={"seq": peer}, device_id_type=mesh_id)
+        return carry
+
+    lax.fori_loop(1, n, greet, 0)
+    pl.semaphore_wait(barrier, n - 1)
+    local = pltpu.make_async_copy(x_ref, o_ref.at[:, me], local_sem)
+    local.start()
+
+    def push(peer, sender, receiver):
+        return [
+            pltpu.make_async_remote_copy(
+                src_ref=x_ref.at[a],
+                dst_ref=o_ref.at[a, receiver],
+                send_sem=send_sem.at[a, sender],
+                recv_sem=recv_sem.at[a, receiver],
+                device_id={"seq": peer},
+                device_id_type=mesh_id,
+            )
+            for a in range(parts)
+        ]
+
+    def send(k, carry):
+        peer = lax.rem(me + k, n)
+        for copy in push(peer, peer, me):
+            copy.start()
+        return carry
+
+    lax.fori_loop(1, n, send, 0)
+
+    def finish(k, carry):
+        peer = lax.rem(me + k, n)
+        for copy in push(peer, peer, peer):
+            copy.wait_send()
+            copy.wait_recv()
+        return carry
+
+    lax.fori_loop(1, n, finish, 0)
+    local.wait()
+
+
+def seq_gather(stacked, n, cid):
+    parts, rows, cols = stacked.shape
+    return pl.pallas_call(
+        functools.partial(seq_gather_kernel, n),
+        out_shape=jax.ShapeDtypeStruct((parts, n, rows, cols), stacked.dtype),
+        in_specs=[pl.BlockSpec(memory_space=pl.ANY)],
+        out_specs=pl.BlockSpec(memory_space=pl.ANY),
+        scratch_shapes=[
+            pltpu.SemaphoreType.DMA((parts, n)),
+            pltpu.SemaphoreType.DMA((parts, n)),
+            pltpu.SemaphoreType.DMA,
+        ],
+        compiler_params=pltpu.CompilerParams(collective_id=cid, has_side_effects=True),
+    )(stacked)
+
+
 def body(
+    seq_n,
     hidden,
     norm_gain,
     w_query,
@@ -126,12 +194,14 @@
         result, unused = lax.scan(step, state, (key_blocks, value_blocks, mask_blocks))
         return result
 
-    key_rows = lax.all_gather(prefix_keys, "seq", axis=0, tiled=True)
-    value_rows = lax.all_gather(prefix_values, "seq", axis=0, tiled=True)
+    gathered_prefix = seq_gather(jnp.stack([prefix_keys, prefix_values]), seq_n, 0)
+    key_rows = gathered_prefix[0].reshape(-1, kv_heads * HEAD)
+    value_rows = gathered_prefix[1].reshape(-1, kv_heads * HEAD)
     visible = wanted[:, None] == row_pages[None, :]
     state = attend(initial, key_rows, value_rows, visible)
-    key_rows = lax.all_gather(new_keys, "seq", axis=0, tiled=True)
-    value_rows = lax.all_gather(new_values, "seq", axis=0, tiled=True)
+    gathered_suffix = seq_gather(jnp.stack([new_keys, new_values]), seq_n, 1)
+    key_rows = gathered_suffix[0].reshape(-1, kv_heads * HEAD)
+    value_rows = gathered_suffix[1].reshape(-1, kv_heads * HEAD)
     visible = (request[:, None] == request_all[None, :]) & (
         position_all[None, :] <= position[:, None]
     )
@@ -148,7 +218,7 @@
 
 def solution(mesh):
     return jax.shard_map(
-        body,
+        functools.partial(body, mesh.shape["seq"]),
         mesh=mesh,
         in_specs=(
             P("seq", "tp"),

time: 440 us -> 533 us (1.21)
  the two profiles are of different devices: /device:TPU:165 before, /device:TPU:63 now
where the time goes in v1:
time: 533 us; the launch traced here: 531 us
  Pallas kernels  279 us (52%)
  matrix products  130 us (24%)
  other arithmetic  61.3 us (12%)
  local copies, waits for them, and re-layouts  43.4 us (8%)
  between operations  14.3 us (3%)
    pallas_call x2, Pallas kernels, seq_gather(): pl.pallas_call(functools.partial(seq_gather_kernel, n), out_shape=jax.Sha...  279 us
    dot_general x32, matrix products, step(): jnp.einsum('tngd,knd->ntgk', queries, key_block, preferred_element_type=j...  65.1 us
    dot_general x32, matrix products, step(): jnp.einsum('ntgk,knd->ntgd', weights.astype(jnp.bfloat16), value_block, p...  54.6 us
    reduce_sum x32, other arithmetic, step(): run_sum = run_sum * fade + jnp.sum(weights, axis=-1)  42.6 us
    broadcast_in_dim x32, local copies, waits for them, and re-layouts, step(): jnp.where(seen, scores, -1e+30)  29.4 us
  transfers between devices with their start and end apart: 1, of which 0 were waited for; matrix products, arithmetic and copies ran while one was open for 4% of the time, Pallas kernels for 30%

profile of v1, /device:TPU:63, one launch (start us, length us, event | category | flops | bytes accessed | tf_op | source)
XLA Modules:
  0.0 530.7 jit_solution(723003541956796206)
XLA Ops:
  14.1 160.0 %shard_map.130 = bf16[2,32,256,128]{3,2,1,0:T(8,128)(2,1)} custom-call(bf16[2,256,128]{2,1,0:T(8,128)(2,1)} %pad_maximum_fusion.1.x_ref), custom_call_target="tpu_custom_call" | custom-call | tf_op jit(solution)/shard_map/pallas_call | solution.py:98
  174.8 4.8 fusion.62
  179.6 2.7 broadcast_compare_fusion
  182.3 4.6 compare_and_fusion
  186.9 3.0 fusion.44
  190.0 6.0 %fusion.59 = f32[256,512]{1,0:T(8,128)} fusion(bf16[7168,512]{1,0:T(8,128)(2,1)} %param.17, bf16[256,7168]{1,0:T(8,128)(2,1)S(1)} %copy-done.2, f32[7168]{0:T(1024)S(1)} %convert_element_type.54, f32[256]{0:T(256)S(1)} %add_rsqrt_fusion), kind=kOutput, calls=%fused_computation.97 | convolution fusion | flops 1886388224 | bytes 11564032 | tf_op jit(solution)/shard_map/dot_general | solution.py:144
  197.8 121.5 %while.30 = (s32[]{:T(128)}, f32[1,256,4]{1,2,0:T(4,128)S(1)}, f32[1,256,4]{1,2,0:T(4,128)S(1)}, f32[1,256,4,128]{3,1,2,0:T(8,128)S(1)}, pred[16,256,512]{1,2,0:...) while((s32[]{:T(128)}, f32[1,256,4]{1,2,0:T(4,128)S(1)}, ...), condition=%wide.region_8.9_spmd.clone, body=%wide.region_5.8_spmd.clone.sunk | while | flops 274601984 | bytes 16973984 | solution.py:194
  198.8 2.7 fusion.87
  214.0 2.7 fusion.87
  221.5 2.7 fusion.87
  229.1 2.7 fusion.87
  236.7 2.7 fusion.87
  244.3 2.7 fusion.87
  251.9 2.7 fusion.87
  259.5 2.7 fusion.87
  267.1 2.7 fusion.87
  274.7 2.7 fusion.87
  282.3 2.7 fusion.87
  297.5 2.7 fusion.87
  312.7 2.7 fusion.87
  319.4 3.4 convolution_bitcast_fusion.2
  325.6 119.0 %shard_map.131 = bf16[2,32,256,128]{3,2,1,0:T(8,128)(2,1)} custom-call(bf16[2,256,128]{2,1,0:T(8,128)(2,1)} %pad_maximum_fusion.2.x_ref), custom_call_target="tpu_custom_call" | custom-call | tf_op jit(solution)/shard_map/pallas_call | solution.py:98
  444.6 4.7 fusion.61
  449.4 72.6 %while.29 = (s32[]{:T(128)}, f32[1,256,4]{1,2,0:T(4,128)S(1)}, f32[1,256,4]{1,2,0:T(4,128)S(1)}, f32[1,256,4,128]{3,1,2,0:T(8,128)S(1)}, pred[16,256,512]{1,2,0:...) while((s32[]{:T(128)}, f32[1,256,4]{1,2,0:T(4,128)S(1)}, ...), condition=%wide.region_12.13_spmd, body=%wide.region_9.12_spmd.sunk | while | flops 274467840 | bytes 8585329 | solution.py:194
  (294 shorter events, 171.9 us)
Async XLA Ops:
  7.2 312.2 %copy-start = (bf16[7168,128]{1,0:T(8,128)(2,1)S(1)}, bf16[7168,128]{1,0:T(8,128)(2,1)}, u32[]{:S(2)}) copy-start(bf16[7168,128]{1,0:T(8,128)(2,1)} %param.18) | copy-start | bytes 5505028
  7.2 179.7 %all-gather.2.cloned.1.call-start = ((), (), s32[]{:S(2)}) async-start(), calls=%async_computation | async-start | bytes 4128768 | tf_op jit(solution)/shard_map/all_gather | solution.py:126
  14.1 160.0 %copy-start.6 = (bf16[7168]{0:T(1024)(128)(2,1)S(1)}, bf16[7168]{0:T(1024)(128)(2,1)}, u32[]{:S(2)}) copy-start(bf16[7168]{0:T(1024)(128)(2,1)} %param.16) | copy-start | bytes 43012
  14.1 160.0 %copy-start.4 = (s32[8192]{0:T(1024)S(1)}, s32[8192]{0:T(1024)}, u32[]{:S(2)}) copy-start(s32[8192]{0:T(1024)} %param.25) | copy-start | bytes 98308
  186.9 3.1 copy-start.2
  201.4 2.2 copy-start.1
  209.0 2.2 copy-start.1
  216.6 2.2 copy-start.1
  224.2 2.2 copy-start.1
  231.8 2.2 copy-start.1
  239.4 2.2 copy-start.1
  247.0 2.2 copy-start.1
  254.6 2.2 copy-start.1
  262.2 2.2 copy-start.1
  269.8 2.2 copy-start.1
  277.4 2.2 copy-start.1
  285.0 2.2 copy-start.1
  292.6 2.2 copy-start.1
  300.2 2.2 copy-start.1
  307.8 2.2 copy-start.1
  315.4 2.2 copy-start.1
  319.4 4.1 copy-start.3
  319.4 4.1 copy-start.7
  324.8 119.8 %copy-start.5 = (bf16[256,128]{1,0:T(8,128)(2,1)}, bf16[256,128]{1,0:T(8,128)(2,1)S(1)}, u32[]{:S(2)}) copy-start(bf16[256,128]{1,0:T(8,128)(2,1)S(1)} %convolution_convert_fusion) | copy-start | bytes 196612
Sparse Core Ops, SparseCore 0:
  10.6 145.6 all-gather.1

commit v2 on v1

--- a/solution.py
+++ b/solution.py
@@ -45,64 +45,87 @@
     return (request, position, wanted)
 
 
-def seq_gather_kernel(n, x_ref, o_ref, send_sem, recv_sem, local_sem):
+def seq_gather_kernel(chips, x_ref, o_ref, send_sem, recv_sem, fwd_send, fwd_recv, local_sem):
     me = lax.axis_index("seq")
+    chip = me // 2
+    core = me % 2
+    partner = chip * 2 + (1 - core)
     parts = x_ref.shape[0]
     mesh_id = pl.DeviceIdType.MESH
     barrier = pltpu.get_barrier_semaphore()
 
     def greet(k, carry):
-        peer = lax.rem(me + k, n)
+        peer = lax.rem(chip + k, chips) * 2 + core
         pl.semaphore_signal(barrier, inc=1, device_id={"seq": peer}, device_id_type=mesh_id)
         return carry
 
-    lax.fori_loop(1, n, greet, 0)
-    pl.semaphore_wait(barrier, n - 1)
-    local = pltpu.make_async_copy(x_ref, o_ref.at[:, me], local_sem)
+    lax.fori_loop(1, chips, greet, 0)
+    pl.semaphore_signal(barrier, inc=1, device_id={"seq": partner}, device_id_type=mesh_id)
+    pl.semaphore_wait(barrier, chips)
+    local = pltpu.make_async_copy(x_ref, o_ref.at[:, chip, core], local_sem)
     local.start()
 
-    def push(peer, sender, receiver):
+    def push(peer_chip, sender, receiver):
         return [
             pltpu.make_async_remote_copy(
                 src_ref=x_ref.at[a],
-                dst_ref=o_ref.at[a, receiver],
+                dst_ref=o_ref.at[a, receiver, core],
                 send_sem=send_sem.at[a, sender],
                 recv_sem=recv_sem.at[a, receiver],
-                device_id={"seq": peer},
+                device_id={"seq": peer_chip * 2 + core},
                 device_id_type=mesh_id,
             )
             for a in range(parts)
         ]
 
     def send(k, carry):
-        peer = lax.rem(me + k, n)
-        for copy in push(peer, peer, me):
+        peer_chip = lax.rem(chip + k, chips)
+        for copy in push(peer_chip, peer_chip, chip):
             copy.start()
         return carry
 
-    lax.fori_loop(1, n, send, 0)
+    lax.fori_loop(1, chips, send, 0)
 
     def finish(k, carry):
-        peer = lax.rem(me + k, n)
-        for copy in push(peer, peer, peer):
+        peer_chip = lax.rem(chip + k, chips)
+        for copy in push(peer_chip, peer_chip, peer_chip):
             copy.wait_send()
             copy.wait_recv()
         return carry
 
-    lax.fori_loop(1, n, finish, 0)
+    lax.fori_loop(1, chips, finish, 0)
     local.wait()
+    forward = [
+        pltpu.make_async_remote_copy(
+            src_ref=o_ref.at[a, :, core],
+            dst_ref=o_ref.at[a, :, core],
+            send_sem=fwd_send.at[a],
+            recv_sem=fwd_recv.at[a],
+            device_id={"seq": partner},
+            device_id_type=mesh_id,
+        )
+        for a in range(parts)
+    ]
+    for copy in forward:
+        copy.start()
+    for copy in forward:
+        copy.wait_send()
+        copy.wait_recv()
 
 
 def seq_gather(stacked, n, cid):
     parts, rows, cols = stacked.shape
+    chips = n // 2
     return pl.pallas_call(
-        functools.partial(seq_gather_kernel, n),
-        out_shape=jax.ShapeDtypeStruct((parts, n, rows, cols), stacked.dtype),
+        functools.partial(seq_gather_kernel, chips),
+        out_shape=jax.ShapeDtypeStruct((parts, chips, 2, rows, cols), stacked.dtype),
         in_specs=[pl.BlockSpec(memory_space=pl.ANY)],
         out_specs=pl.BlockSpec(memory_space=pl.ANY),
         scratch_shapes=[
-            pltpu.SemaphoreType.DMA((parts, n)),
-            pltpu.SemaphoreType.DMA((parts, n)),
+            pltpu.SemaphoreType.DMA((parts, chips)),
+            pltpu.SemaphoreType.DMA((parts, chips)),
+            pltpu.SemaphoreType.DMA((parts,)),
+            pltpu.SemaphoreType.DMA((parts,)),
             pltpu.SemaphoreType.DMA,
         ],
         compiler_params=pltpu.CompilerParams(collective_id=cid, has_side_effects=True),

time: 533 us -> 423 us (0.79)
  the two profiles are of different devices: /device:TPU:63 before, /device:TPU:165 now
where the time goes in v2:
time: 423 us; the launch traced here: 418 us
  Pallas kernels  167 us (39%)
  matrix products  130 us (31%)
  other arithmetic  61.3 us (14%)
  local copies, waits for them, and re-layouts  43.4 us (10%)
  between operations  14.3 us (3%)
    pallas_call x2, Pallas kernels, seq_gather(): pl.pallas_call(functools.partial(seq_gather_kernel, chips), out_shape=jax...  167 us
    dot_general x32, matrix products, step(): jnp.einsum('tngd,knd->ntgk', queries, key_block, preferred_element_type=j...  65.1 us
    dot_general x32, matrix products, step(): jnp.einsum('ntgk,knd->ntgd', weights.astype(jnp.bfloat16), value_block, p...  54.6 us
    reduce_sum x32, other arithmetic, step(): run_sum = run_sum * fade + jnp.sum(weights, axis=-1)  42.6 us
    broadcast_in_dim x32, local copies, waits for them, and re-layouts, step(): jnp.where(seen, scores, -1e+30)  29.4 us
  transfers between devices with their start and end apart: 1, of which 0 were waited for; matrix products, arithmetic and copies ran while one was open for 5% of the time, Pallas kernels for 25%

profile of v2, /device:TPU:165, one launch (start us, length us, event | category | flops | bytes accessed | tf_op | source)
XLA Modules:
  0.0 418.3 jit_solution(13331677341459025418)
XLA Ops:
  14.1 106.2 %shard_map.130 = bf16[2,16,2,256,128]{4,3,2,1,0:T(8,128)(2,1)} custom-call(bf16[2,256,128]{2,1,0:T(8,128)(2,1)} %pad_maximum_fusion.1.x_ref), custom_call_target="tpu_custom_call" | custom-call | tf_op jit(solution)/shard_map/pallas_call | solution.py:119
  121.1 4.8 %fusion.62 = (bf16[1,16,2,256,128]{4,3,2,1,0:T(8,128)(2,1)}, bf16[1,16,2,256,128]{4,3,2,1,0:T(8,128)(2,1)}) fusion(bf16[2,16,2,256,128]{4,3,2,1,0:T(8,128)(2,1)} %shard_map.130), kind=kLoop, calls=%fused_computation.99 | loop fusion | bytes 8388608 | tf_op jit(solution)/shard_map/slice | solution.py:222
  125.9 2.7 broadcast_compare_fusion
  128.6 4.6 %compare_and_fusion = pred[16,256,512]{1,2,0:T(8,128)(4,1)} fusion(s32[256]{0:T(256)S(1)} %get-tuple-element.209, s32[16,512]{1,0:T(8,128)S(1)} %le.17, s32[16,512]{1,0:T(8,128)S(1)} %eq.52, s32[256]{0:T(256)S(1)} %dynamic_slice.31), kind=kLoop, calls=%fused_computation.60 | loop fusion | flops 6291456 | bytes 2164736 | tf_op jit(solution)/shard_map/and | solution.py:228
  133.2 3.0 fusion.44
  136.3 6.0 %fusion.59 = f32[256,512]{1,0:T(8,128)} fusion(bf16[7168,512]{1,0:T(8,128)(2,1)} %param.17, bf16[256,7168]{1,0:T(8,128)(2,1)S(1)} %copy-done.2, f32[7168]{0:T(1024)S(1)} %convert_element_type.54, f32[256]{0:T(256)S(1)} %add_rsqrt_fusion), kind=kOutput, calls=%fused_computation.97 | convolution fusion | flops 1886388224 | bytes 11564032 | tf_op jit(solution)/shard_map/dot_general | solution.py:167
  144.1 121.5 %while.30 = (s32[]{:T(128)}, f32[1,256,4]{1,2,0:T(4,128)S(1)}, f32[1,256,4]{1,2,0:T(4,128)S(1)}, f32[1,256,4,128]{3,1,2,0:T(8,128)S(1)}, pred[16,256,512]{1,2,0:...) while((s32[]{:T(128)}, f32[1,256,4]{1,2,0:T(4,128)S(1)}, ...), condition=%wide.region_8.9_spmd.clone, body=%wide.region_5.8_spmd.clone.sunk | while | flops 274601984 | bytes 16973984 | solution.py:217
  152.7 2.7 fusion.87
  160.2 2.7 fusion.87
  167.8 2.7 fusion.87
  175.4 2.7 fusion.87
  183.0 2.7 fusion.87
  198.2 2.7 fusion.87
  213.4 2.7 fusion.87
  221.0 2.7 fusion.87
  228.6 2.7 fusion.87
  236.2 2.7 fusion.87
  243.8 2.7 fusion.87
  251.4 2.7 fusion.87
  259.0 2.7 fusion.87
  265.7 3.4 convolution_bitcast_fusion.2
  271.9 60.4 %shard_map.131 = bf16[2,16,2,256,128]{4,3,2,1,0:T(8,128)(2,1)} custom-call(bf16[2,256,128]{2,1,0:T(8,128)(2,1)} %pad_maximum_fusion.2.x_ref), custom_call_target="tpu_custom_call" | custom-call | tf_op jit(solution)/shard_map/pallas_call | solution.py:119
  332.3 4.7 %fusion.61 = (bf16[1,16,2,256,128]{4,3,2,1,0:T(8,128)(2,1)}, bf16[1,16,2,256,128]{4,3,2,1,0:T(8,128)(2,1)}) fusion(bf16[2,16,2,256,128]{4,3,2,1,0:T(8,128)(2,1)} %shard_map.131), kind=kLoop, calls=%fused_computation.98 | loop fusion | bytes 8388608 | tf_op jit(solution)/shard_map/slice | solution.py:227
  337.0 72.6 %while.29 = (s32[]{:T(128)}, f32[1,256,4]{1,2,0:T(4,128)S(1)}, f32[1,256,4]{1,2,0:T(4,128)S(1)}, f32[1,256,4,128]{3,1,2,0:T(8,128)S(1)}, pred[16,256,512]{1,2,0:...) while((s32[]{:T(128)}, f32[1,256,4]{1,2,0:T(4,128)S(1)}, ...), condition=%wide.region_12.13_spmd, body=%wide.region_9.12_spmd.sunk | while | flops 274467840 | bytes 8585329 | solution.py:217
  (294 shorter events, 171.9 us)
Async XLA Ops:
  7.2 258.5 %copy-start = (bf16[7168,128]{1,0:T(8,128)(2,1)S(1)}, bf16[7168,128]{1,0:T(8,128)(2,1)}, u32[]{:S(2)}) copy-start(bf16[7168,128]{1,0:T(8,128)(2,1)} %param.18) | copy-start | bytes 5505028
  7.2 126.0 %all-gather.2.cloned.1.call-start = ((), (), s32[]{:S(2)}) async-start(), calls=%async_computation | async-start | bytes 4128768 | tf_op jit(solution)/shard_map/all_gather | solution.py:149
  14.1 106.3 %copy-start.6 = (bf16[7168]{0:T(1024)(128)(2,1)S(1)}, bf16[7168]{0:T(1024)(128)(2,1)}, u32[]{:S(2)}) copy-start(bf16[7168]{0:T(1024)(128)(2,1)} %param.16) | copy-start | bytes 43012
  14.1 106.3 %copy-start.4 = (s32[8192]{0:T(1024)S(1)}, s32[8192]{0:T(1024)}, u32[]{:S(2)}) copy-start(s32[8192]{0:T(1024)} %param.25) | copy-start | bytes 98308
  133.2 3.1 copy-start.2
  147.7 2.2 copy-start.1
  155.3 2.2 copy-start.1
  162.9 2.2 copy-start.1
  170.5 2.2 copy-start.1
  178.1 2.2 copy-start.1
  185.7 2.2 copy-start.1
  193.3 2.2 copy-start.1
  200.9 2.2 copy-start.1
  208.5 2.2 copy-start.1
  216.1 2.2 copy-start.1
  223.7 2.2 copy-start.1
  231.3 2.2 copy-start.1
  238.9 2.2 copy-start.1
  246.5 2.2 copy-start.1
  254.1 2.2 copy-start.1
  261.7 2.2 copy-start.1
  265.7 4.1 copy-start.3
  265.7 4.1 copy-start.7
  271.1 61.2 %copy-start.5 = (bf16[256,128]{1,0:T(8,128)(2,1)}, bf16[256,128]{1,0:T(8,128)(2,1)S(1)}, u32[]{:S(2)}) copy-start(bf16[256,128]{1,0:T(8,128)(2,1)S(1)} %convolution_convert_fusion) | copy-start | bytes 196612
Sparse Core Ops, SparseCore 0:
  10.6 107.3 all-gather.1

commit v3 on v2

--- a/solution.py
+++ b/solution.py
@@ -130,6 +130,76 @@
         ],
         compiler_params=pltpu.CompilerParams(collective_id=cid, has_side_effects=True),
     )(stacked)
+
+
+def attention_kernel(
+    scale,
+    p_idx, p_cnt, s_idx, s_cnt,
+    q_ref, q_want, q_req, q_pos,
+    pk_ref, pv_ref, p_tag, p_bound,
+    sk_ref, sv_ref, s_tag, s_bound,
+    o_ref, m_sc, l_sc, acc_sc,
+):
+    for i in range(q_ref.shape[0]):
+        m_sc[...] = jnp.full(m_sc.shape, -1e30, jnp.float32)
+        l_sc[...] = jnp.zeros(l_sc.shape, jnp.float32)
+        acc_sc[...] = jnp.zeros(acc_sc.shape, jnp.float32)
+        query = q_ref[i]
+        want = q_want[i]
+        req = q_req[i]
+        pos = q_pos[i]
+
+        def sweep(idx, cnt, k_ref, v_ref, tag_ref, bound_ref):
+            def step(n, carry):
+                b = idx[i, n]
+                scores = lax.dot_general(
+                    query, k_ref[b], (((1,), (1,)), ((), ())),
+                    preferred_element_type=jnp.float32,
+                ) * scale
+                tag = tag_ref[b]
+                seen = ((tag == want) | (tag == req)) & (bound_ref[b] <= pos)
+                run_max = m_sc[...]
+                new_max = jnp.maximum(
+                    run_max, jnp.max(jnp.where(seen, scores, -1e30), axis=1, keepdims=True)
+                )
+                weights = jnp.where(seen, jnp.exp(scores - new_max), 0.0)
+                fade = jnp.exp(run_max - new_max)
+                l_sc[...] = l_sc[...] * fade + jnp.sum(weights, axis=1, keepdims=True)
+                acc_sc[...] = acc_sc[...] * fade + jnp.dot(
+                    weights.astype(jnp.bfloat16), v_ref[b],
+                    preferred_element_type=jnp.float32,
+                )
+                m_sc[...] = new_max
+                return carry
+
+            lax.fori_loop(0, cnt[i], step, 0)
+
+        sweep(p_idx, p_cnt, pk_ref, pv_ref, p_tag, p_bound)
+        sweep(s_idx, s_cnt, sk_ref, sv_ref, s_tag, s_bound)
+        o_ref[i] = (acc_sc[...] / l_sc[...]).astype(o_ref.dtype)
+
+
+def block_attention(scale, lists, queries, query_meta, prefix_parts, suffix_parts):
+    q_blocks, q_rows, width = queries.shape
+    smem = pl.BlockSpec(memory_space=pltpu.SMEM)
+    vmem = pl.BlockSpec(memory_space=pltpu.VMEM)
+    return pl.pallas_call(
+        functools.partial(attention_kernel, scale),
+        out_shape=jax.ShapeDtypeStruct((q_blocks, q_rows, width), jnp.bfloat16),
+        in_specs=[smem] * 4 + [vmem] * 12,
+        out_specs=vmem,
+        scratch_shapes=[
+            pltpu.VMEM((q_rows, 1), jnp.float32),
+            pltpu.VMEM((q_rows, 1), jnp.float32),
+            pltpu.VMEM((q_rows, width), jnp.float32),
+        ],
+        compiler_params=pltpu.CompilerParams(vmem_limit_bytes=48 * 1024 * 1024),
+    )(*lists, queries, *query_meta, *prefix_parts, *suffix_parts)
+
+
+def visible_list(visible):
+    order = jnp.argsort(jnp.logical_not(visible), axis=1, stable=True).astype(jnp.int32)
+    return order, jnp.sum(visible.astype(jnp.int32), axis=1)
 
 
 def body(
@@ -178,63 +248,59 @@
     ).astype(jnp.bfloat16)
     new_keys = new_keys.reshape(local_rows, kv_heads * HEAD)
     new_values = jnp.dot(normed, w_value, preferred_element_type=jnp.float32).astype(jnp.bfloat16)
-    row_pages = jnp.repeat(page_prefix, PAGE)
     score_scale = 1.0 / math.sqrt(HEAD)
-    initial = (
-        jnp.full((kv_heads, local_rows, group_size), -1e30, jnp.float32),
-        jnp.zeros((kv_heads, local_rows, group_size), jnp.float32),
-        jnp.zeros((kv_heads, local_rows, group_size, HEAD), jnp.float32),
-    )
-
-    def attend(state, key_rows, value_rows, visible):
-        row_count = key_rows.shape[0]
-        block_width = math.gcd(row_count, 512)
-        block_count = row_count // block_width
-        key_blocks = key_rows.reshape(block_count, block_width, kv_heads, HEAD)
-        value_blocks = value_rows.reshape(block_count, block_width, kv_heads, HEAD)
-        mask_blocks = visible.reshape(local_rows, block_count, block_width).transpose(1, 0, 2)
-
-        def step(carry_in, inputs):
-            run_max, run_sum, run_acc = carry_in
-            key_block, value_block, mask_block = inputs
-            scores = (
-                jnp.einsum("tngd,knd->ntgk", queries, key_block, preferred_element_type=jnp.float32)
-                * score_scale
-            )
-            seen = mask_block[None, :, None, :]
-            new_max = jnp.maximum(run_max, jnp.max(jnp.where(seen, scores, -1e30), axis=-1))
-            weights = jnp.where(seen, jnp.exp(scores - new_max[..., None]), 0.0)
-            fade = jnp.exp(run_max - new_max)
-            run_sum = run_sum * fade + jnp.sum(weights, axis=-1)
-            run_acc = run_acc * fade[..., None] + jnp.einsum(
-                "ntgk,knd->ntgd",
-                weights.astype(jnp.bfloat16),
-                value_block,
-                preferred_element_type=jnp.float32,
-            )
-            return ((new_max, run_sum, run_acc), None)
-
-        result, unused = lax.scan(step, state, (key_blocks, value_blocks, mask_blocks))
-        return result
-
-    gathered_prefix = seq_gather(jnp.stack([prefix_keys, prefix_values]), seq_n, 0)
-    key_rows = gathered_prefix[0].reshape(-1, kv_heads * HEAD)
-    value_rows = gathered_prefix[1].reshape(-1, kv_heads * HEAD)
-    visible = wanted[:, None] == row_pages[None, :]
-    state = attend(initial, key_rows, value_rows, visible)
-    gathered_suffix = seq_gather(jnp.stack([new_keys, new_values]), seq_n, 1)
-    key_rows = gathered_suffix[0].reshape(-1, kv_heads * HEAD)
-    value_rows = gathered_suffix[1].reshape(-1, kv_heads * HEAD)
-    visible = (request[:, None] == request_all[None, :]) & (
-        position_all[None, :] <= position[:, None]
-    )
-    state = attend(state, key_rows, value_rows, visible)
-    run_max, run_sum, run_acc = state
+    block = PAGE
+    q_blocks = local_rows // block
+    pages = page_prefix.shape[0]
+    runs = row_order.shape[0] // block
+    stacked_q = (
+        queries.reshape(q_blocks, block, group_size, HEAD)
+        .transpose(0, 2, 1, 3)
+        .reshape(q_blocks, group_size * block, HEAD)
+    )
+
+    def per_query(values):
+        spread = jnp.broadcast_to(values.reshape(q_blocks, 1, block), (q_blocks, group_size, block))
+        return spread.reshape(q_blocks, group_size * block, 1).astype(jnp.int32)
+
+    query_meta = (per_query(wanted), per_query(request + PREFIXES), per_query(position))
+    want_blocks = wanted.reshape(q_blocks, block)
+    block_wants = jnp.any(
+        want_blocks[:, :, None] == jnp.arange(PREFIXES, dtype=jnp.int32)[None, None, :], axis=1
+    )
+    page_visible = jnp.take(block_wants, page_prefix, axis=1)
+    local_place = lax.dynamic_slice_in_dim(row_order, offset, local_rows).reshape(q_blocks, block)
+    first_seen = jnp.min(local_place - position.reshape(q_blocks, block), axis=1)
+    last_seen = jnp.max(local_place, axis=1)
+    run_place = row_order.reshape(runs, block)
+    run_low = jnp.min(run_place, axis=1)
+    run_high = jnp.max(run_place, axis=1)
+    run_visible = (run_low[None, :] <= last_seen[:, None]) & (run_high[None, :] >= first_seen[:, None])
+    p_idx, p_cnt = visible_list(page_visible)
+    s_idx, s_cnt = visible_list(run_visible)
+
+    seq_n_blocks = seq_n
+    gathered_prefix = seq_gather(jnp.stack([prefix_keys, prefix_values]), seq_n_blocks, 0)
+    prefix_parts = (
+        gathered_prefix[0].reshape(pages, block, HEAD),
+        gathered_prefix[1].reshape(pages, block, HEAD),
+        jnp.broadcast_to(page_prefix.reshape(pages, 1, 1), (pages, 1, block)).astype(jnp.int32),
+        jnp.full((pages, 1, block), -1, jnp.int32),
+    )
+    gathered_suffix = seq_gather(jnp.stack([new_keys, new_values]), seq_n_blocks, 1)
+    suffix_parts = (
+        gathered_suffix[0].reshape(runs, block, HEAD),
+        gathered_suffix[1].reshape(runs, block, HEAD),
+        (request_all + PREFIXES).reshape(runs, 1, block).astype(jnp.int32),
+        position_all.reshape(runs, 1, block).astype(jnp.int32),
+    )
+    out = block_attention(
+        score_scale, (p_idx, p_cnt, s_idx, s_cnt), stacked_q, query_meta, prefix_parts, suffix_parts
+    )
     attended = (
-        (run_acc / run_sum[..., None])
-        .transpose(1, 0, 2, 3)
-        .reshape(local_rows, q_heads * HEAD)
-        .astype(jnp.bfloat16)
+        out.reshape(q_blocks, group_size, block, HEAD)
+        .transpose(0, 2, 1, 3)
+        .reshape(local_rows, group_size * HEAD)
     )
     return (attended, new_keys, new_values)
 

time: 423 us -> 288 us (0.68)
  the two profiles are of different devices: /device:TPU:165 before, /device:TPU:167 now
where the time goes in v3:
time: 288 us; the launch traced here: 287 us
  Pallas kernels  220 us (76%)
  other arithmetic  21.1 us (7%)
  local copies, waits for them, and re-layouts  19.8 us (7%)
  between operations  14.3 us (5%)
  matrix products  11.4 us (4%)
    pallas_call x2, Pallas kernels, seq_gather(): pl.pallas_call(functools.partial(seq_gather_kernel, chips), out_shape=jax...  169 us
    pallas_call x1, Pallas kernels, block_attention(): pl.pallas_call(functools.partial(attention_kernel, scale), out_shape=jax....  50.6 us
    reshape x1, matrix products, body(): jnp.dot(normed, w_query, preferred_element_type=jnp.float32)  6.26 us
  transfers between devices with their start and end apart: 1, of which 0 were waited for; matrix products, arithmetic and copies ran while one was open for 7% of the time, Pallas kernels for 38%

profile of v3, /device:TPU:167, one launch (start us, length us, event | category | flops | bytes accessed | tf_op | source)
XLA Modules:
  0.0 287.1 jit_solution(5062443605348377618)
XLA Ops:
  10.2 1.0 convert_reduce_fusion
  11.2 1.0 select_reduce_fusion
  12.2 0.8 sub.16
  13.3 0.9 bitcast_reduce_fusion.2
  14.3 0.9 bitcast_reduce_fusion.1
  17.4 1.0 sort.31
  18.6 1.0 sort.32
  20.8 1.5 pad_maximum_fusion.x_ref
  22.3 108.3 %shard_map.130 = bf16[2,16,2,256,128]{4,3,2,1,0:T(8,128)(2,1)} custom-call(bf16[2,256,128]{2,1,0:T(8,128)(2,1)} %pad_maximum_fusion.x_ref), custom_call_target="tpu_custom_call" | custom-call | tf_op jit(solution)/shard_map/pallas_call | solution.py:119
  131.4 1.0 multiply_cosine_fusion.1
  132.3 4.8 %fusion.18 = (bf16[1,16,2,256,128]{4,3,2,1,0:T(8,128)(2,1)}, bf16[1,16,2,256,128]{4,3,2,1,0:T(8,128)(2,1)}) fusion(bf16[2,16,2,256,128]{4,3,2,1,0:T(8,128)(2,1)} %shard_map.130), kind=kLoop, calls=%fused_computation.54 | loop fusion | bytes 8388608 | tf_op jit(solution)/shard_map/slice | solution.py:286
  137.1 3.0 %fusion = f32[256]{0:T(256)S(1)} fusion(bf16[256,7168]{1,0:T(8,128)(2,1)} %all-gather.2.cloned.1.call-done), kind=kLoop, calls=%fused_computation.3 | loop fusion | flops 5504768 | bytes 3671040 | tf_op jit(solution)/shard_map/reduce_sum | solution.py:222
  140.2 1.3 convolution_bitcast_fusion
  141.5 1.2 fusion.8
  142.7 6.3 %fusion.15 = f32[256,512]{0,1:T(8,128)S(1)} fusion(bf16[7168,512]{1,0:T(8,128)(2,1)} %param.13, bf16[256,7168]{1,0:T(8,128)(2,1)S(1)} %copy-done.3, f32[7168]{0:T(1024)} %copy-done.9, f32[256]{0:T(256)S(1)} %add_rsqrt_fusion), kind=kOutput, calls=%fused_computation.52 | convolution fusion | flops 1886388224 | bytes 11564032 | tf_op jit(solution)/shard_map/reshape | solution.py:237
  149.0 0.7 subtract_convert_fusion
  149.8 1.6 concatenate.34
  151.4 1.6 concatenate.35
  152.9 2.0 maximum_bitcast_fusion
  155.0 1.8 copy.45
  156.8 3.9 %convolution_convert_fusion = bf16[256,128]{1,0:T(8,128)(2,1)S(1)} fusion(bf16[7168,128]{1,0:T(8,128)(2,1)} %param.15, bf16[256,7168]{1,0:T(8,128)(2,1)} %all-gather.2.cloned.1.call-done, f32[7168]{0:T(1024)} %copy-done.9, f32[256]{0:T(256)} %copy-done.14), kind=kOutput, calls=%fused_computation.7 | convolution fusion | flops 477134848 | bytes 5600256 | tf_op jit(solution)/shard_map/dot_general | solution.py:250
  162.1 60.8 %shard_map.131 = bf16[2,16,2,256,128]{4,3,2,1,0:T(8,128)(2,1)} custom-call(bf16[2,256,128]{2,1,0:T(8,128)(2,1)} %pad_maximum_fusion.1.x_ref), custom_call_target="tpu_custom_call" | custom-call | tf_op jit(solution)/shard_map/pallas_call | solution.py:119
  222.9 4.9 %fusion.17 = (bf16[1,16,2,256,128]{4,3,2,1,0:T(8,128)(2,1)}, bf16[1,16,2,256,128]{4,3,2,1,0:T(8,128)(2,1)}) fusion(bf16[2,16,2,256,128]{4,3,2,1,0:T(8,128)(2,1)} %shard_map.131), kind=kLoop, calls=%fused_computation.53 | loop fusion | bytes 8388608 | tf_op jit(solution)/shard_map/slice | solution.py:293
  228.0 50.6 %shard_map.132 = bf16[2,512,128]{2,1,0:T(8,128)(2,1)S(1)} custom-call(s32[2,64]{1,0:T(2,128)S(1)} %copy.47.p_idx, s32[2]{0:T(128)S(1)} %convert_reduce_fusion.1.p_cnt, s32[2,64]{1,0:T(2,128)S(1)} %copy.48.s_idx, s32[2]{0:T(128)S(1)} %get-tuple-element.13.s_cnt, bf16[2,512,128]{2,1,0:T(8,128)(2,1)S(1)} %bitcast.53, s32[2,512,1]{2,1,0:T(8,128)S(1)} %reshape.280.q_want, ...), custom_call_target="tpu_custom_call" | custom-call | tf_op jit(solution)/shard_map/pallas_call | solution.py:186
  (72 shorter events, 10.9 us)
Async XLA Ops:
  7.2 132.9 %copy-start = (bf16[7168,128]{1,0:T(8,128)(2,1)S(1)}, bf16[7168,128]{1,0:T(8,128)(2,1)}, u32[]{:S(2)}) copy-start(bf16[7168,128]{1,0:T(8,128)(2,1)} %param.14) | copy-start | bytes 5505028
  7.2 129.9 %all-gather.2.cloned.1.call-start = ((), (), s32[]{:S(2)}) async-start(), calls=%async_computation | async-start | bytes 4128768 | tf_op jit(solution)/shard_map/all_gather | solution.py:219
  10.2 129.9 %copy-start.9 = (f32[7168]{0:T(1024)}, f32[7168]{0:T(1024)S(1)}, u32[]{:S(2)}) copy-start(f32[7168]{0:T(1024)S(1)} %convert_element_type.42) | copy-start | bytes 86020
  130.7 0.5 copy-start.12
  130.8 0.6 copy-start.10
  137.1 3.1 %copy-start.3 = (bf16[256,7168]{1,0:T(8,128)(2,1)S(1)}, bf16[256,7168]{1,0:T(8,128)(2,1)}, u32[]{:S(2)}) copy-start(bf16[256,7168]{1,0:T(8,128)(2,1)} %all-gather.2.cloned.1.call-done) | copy-start | bytes 11010052
  140.2 2.5 copy-start.14
  140.2 1.3 copy-start.11
  140.2 1.3 copy-start.13
  142.7 6.3 %copy-start.6 = (f32[256,64]{0,1:T(8,128)S(1)}, f32[256,64]{0,1:T(8,128)}, u32[]{:S(2)}) copy-start(f32[256,64]{0,1:T(8,128)} %get-tuple-element.24) | copy-start | bytes 196612
  142.7 6.3 %copy-start.7 = (f32[256,64]{0,1:T(8,128)S(1)}, f32[256,64]{0,1:T(8,128)}, u32[]{:S(2)}) copy-start(f32[256,64]{0,1:T(8,128)} %get-tuple-element.25) | copy-start | bytes 196612
  156.8 4.6 %copy-start.4 = (bf16[256,1,64]{2,0,1:T(8,128)(2,1)S(1)}, bf16[256,1,64]{2,0,1:T(8,128)(2,1)}, u32[]{:S(2)}) copy-start(bf16[256,1,64]{2,0,1:T(8,128)(2,1)} %get-tuple-element.23) | copy-start | bytes 98308
  160.7 0.6 copy-start.8
  222.8 4.9 %copy-start.15 = (s32[64]{0:T(128)S(1)}, s32[64]{0:T(128)}, u32[]{:S(2)}) copy-start(s32[64]{0:T(128)} %param.18) | copy-start | bytes 772
  222.9 5.1 %copy-start.1 = (bf16[1,16,2,256,128]{4,3,2,1,0:T(8,128)(2,1)S(1)}, bf16[1,16,2,256,128]{4,3,2,1,0:T(8,128)(2,1)}, u32[]{:S(2)}) copy-start(bf16[1,16,2,256,128]{4,3,2,1,0:T(8,128)(2,1)} %get-tuple-element.19) | copy-start | bytes 6291460
  222.9 5.1 %copy-start.2 = (bf16[2,4,128,128]{3,2,1,0:T(8,128)(2,1)S(1)}, bf16[2,4,128,128]{3,2,1,0:T(8,128)(2,1)}, u32[]{:S(2)}) copy-start(bf16[2,4,128,128]{3,2,1,0:T(8,128)(2,1)} %copy.45) | copy-start | bytes 786436
  228.0 51.6 %copy-start.5 = (bf16[256,1,64]{2,0,1:T(8,128)(2,1)S(1)}, bf16[256,1,64]{2,0,1:T(8,128)(2,1)}, u32[]{:S(2)}) copy-start(bf16[256,1,64]{2,0,1:T(8,128)(2,1)} %get-tuple-element.23) | copy-start | bytes 98308
Sparse Core Ops, SparseCore 0:
  10.6 111.1 all-gather.1

commit v4 on v3

--- a/solution.py
+++ b/solution.py
@@ -133,13 +133,31 @@
 
 
 def attention_kernel(
-    scale,
-    p_idx, p_cnt, s_idx, s_cnt,
+    scale, group_pages,
+    wants, page_order, s_idx, s_cnt,
     q_ref, q_want, q_req, q_pos,
-    pk_ref, pv_ref, p_tag, p_bound,
+    pk_ref, pv_ref,
     sk_ref, sv_ref, s_tag, s_bound,
-    o_ref, m_sc, l_sc, acc_sc,
+    o_ref, m_sc, l_sc, acc_sc, pm_sc, pl_sc, pacc_sc,
 ):
+    prefixes, per_prefix = page_order.shape
+
+    def update(m_ref, l_ref, acc_ref, score_list, value_list):
+        run_max = m_ref[...]
+        new_max = run_max
+        for scores in score_list:
+            new_max = jnp.maximum(new_max, jnp.max(scores, axis=1, keepdims=True))
+        fade = jnp.exp(run_max - new_max)
+        total = l_ref[...] * fade
+        acc = acc_ref[...] * fade
+        for scores, values in zip(score_list, value_list):
+            weights = jnp.exp(scores - new_max)
+            total = total + jnp.sum(weights, axis=1, keepdims=True)
+            acc = acc + jnp.dot(weights.astype(jnp.bfloat16), values, preferred_element_type=jnp.float32)
+        l_ref[...] = total
+        acc_ref[...] = acc
+        m_ref[...] = new_max
+
     for i in range(q_ref.shape[0]):
         m_sc[...] = jnp.full(m_sc.shape, -1e30, jnp.float32)
         l_sc[...] = jnp.zeros(l_sc.shape, jnp.float32)
@@ -149,33 +167,47 @@
         req = q_req[i]
         pos = q_pos[i]
 
-        def sweep(idx, cnt, k_ref, v_ref, tag_ref, bound_ref):
-            def step(n, carry):
-                b = idx[i, n]
-                scores = lax.dot_general(
-                    query, k_ref[b], (((1,), (1,)), ((), ())),
-                    preferred_element_type=jnp.float32,
-                ) * scale
-                tag = tag_ref[b]
-                seen = ((tag == want) | (tag == req)) & (bound_ref[b] <= pos)
-                run_max = m_sc[...]
-                new_max = jnp.maximum(
-                    run_max, jnp.max(jnp.where(seen, scores, -1e30), axis=1, keepdims=True)
-                )
-                weights = jnp.where(seen, jnp.exp(scores - new_max), 0.0)
-                fade = jnp.exp(run_max - new_max)
-                l_sc[...] = l_sc[...] * fade + jnp.sum(weights, axis=1, keepdims=True)
-                acc_sc[...] = acc_sc[...] * fade + jnp.dot(
-                    weights.astype(jnp.bfloat16), v_ref[b],
-                    preferred_element_type=jnp.float32,
-                )
-                m_sc[...] = new_max
-                return carry
-
-            lax.fori_loop(0, cnt[i], step, 0)
-
-        sweep(p_idx, p_cnt, pk_ref, pv_ref, p_tag, p_bound)
-        sweep(s_idx, s_cnt, sk_ref, sv_ref, s_tag, s_bound)
+        def score(keys):
+            return lax.dot_general(
+                query, keys, (((1,), (1,)), ((), ())), preferred_element_type=jnp.float32
+            ) * scale
+
+        for p in range(prefixes):
+            @pl.when(wants[i, p] > 0)
+            def _():
+                pm_sc[...] = jnp.full(pm_sc.shape, -1e30, jnp.float32)
+                pl_sc[...] = jnp.zeros(pl_sc.shape, jnp.float32)
+                pacc_sc[...] = jnp.zeros(pacc_sc.shape, jnp.float32)
+
+                def page_step(g, carry):
+                    pages = [page_order[p, g * group_pages + j] for j in range(group_pages)]
+                    update(pm_sc, pl_sc, pacc_sc, [score(pk_ref[b]) for b in pages], [pv_ref[b] for b in pages])
+                    return carry
+
+                lax.fori_loop(0, per_prefix // group_pages, page_step, 0)
+                mine = want == p
+                m_sc[...] = jnp.where(mine, pm_sc[...], m_sc[...])
+                l_sc[...] = jnp.where(mine, pl_sc[...], l_sc[...])
+                acc_sc[...] = jnp.where(mine, pacc_sc[...], acc_sc[...])
+
+        def step(n, carry):
+            b = s_idx[i, n]
+            scores = score(sk_ref[b])
+            seen = (s_tag[b] == req) & (s_bound[b] <= pos)
+            run_max = m_sc[...]
+            new_max = jnp.maximum(
+                run_max, jnp.max(jnp.where(seen, scores, -1e30), axis=1, keepdims=True)
+            )
+            weights = jnp.where(seen, jnp.exp(scores - new_max), 0.0)
+            fade = jnp.exp(run_max - new_max)
+            l_sc[...] = l_sc[...] * fade + jnp.sum(weights, axis=1, keepdims=True)
+            acc_sc[...] = acc_sc[...] * fade + jnp.dot(
+                weights.astype(jnp.bfloat16), sv_ref[b], preferred_element_type=jnp.float32
+            )
+            m_sc[...] = new_max
+            return carry
+
+        lax.fori_loop(0, s_cnt[i], step, 0)
         o_ref[i] = (acc_sc[...] / l_sc[...]).astype(o_ref.dtype)
 
 
@@ -183,16 +215,17 @@
     q_blocks, q_rows, width = queries.shape
     smem = pl.BlockSpec(memory_space=pltpu.SMEM)
     vmem = pl.BlockSpec(memory_space=pltpu.VMEM)
+    state = [
+        pltpu.VMEM((q_rows, 1), jnp.float32),
+        pltpu.VMEM((q_rows, 1), jnp.float32),
+        pltpu.VMEM((q_rows, width), jnp.float32),
+    ]
     return pl.pallas_call(
-        functools.partial(attention_kernel, scale),
+        functools.partial(attention_kernel, scale, 4),
         out_shape=jax.ShapeDtypeStruct((q_blocks, q_rows, width), jnp.bfloat16),
-        in_specs=[smem] * 4 + [vmem] * 12,
+        in_specs=[smem] * 4 + [vmem] * 10,
         out_specs=vmem,
-        scratch_shapes=[
-            pltpu.VMEM((q_rows, 1), jnp.float32),
-            pltpu.VMEM((q_rows, 1), jnp.float32),
-            pltpu.VMEM((q_rows, width), jnp.float32),
-        ],
+        scratch_shapes=state + state,
         compiler_params=pltpu.CompilerParams(vmem_limit_bytes=48 * 1024 * 1024),
     )(*lists, queries, *query_meta, *prefix_parts, *suffix_parts)
 
@@ -268,7 +301,7 @@
     block_wants = jnp.any(
         want_blocks[:, :, None] == jnp.arange(PREFIXES, dtype=jnp.int32)[None, None, :], axis=1
     )
-    page_visible = jnp.take(block_wants, page_prefix, axis=1)
+    page_order = jnp.argsort(page_prefix, stable=True).astype(jnp.int32).reshape(PREFIXES, -1)
     local_place = lax.dynamic_slice_in_dim(row_order, offset, local_rows).reshape(q_blocks, block)
     first_seen = jnp.min(local_place - position.reshape(q_blocks, block), axis=1)
     last_seen = jnp.max(local_place, axis=1)
@@ -276,7 +309,6 @@
     run_low = jnp.min(run_place, axis=1)
     run_high = jnp.max(run_place, axis=1)
     run_visible = (run_low[None, :] <= last_seen[:, None]) & (run_high[None, :] >= first_seen[:, None])
-    p_idx, p_cnt = visible_list(page_visible)
     s_idx, s_cnt = visible_list(run_visible)
 
     seq_n_blocks = seq_n
@@ -284,8 +316,6 @@
     prefix_parts = (
         gathered_prefix[0].reshape(pages, block, HEAD),
         gathered_prefix[1].reshape(pages, block, HEAD),
-        jnp.broadcast_to(page_prefix.reshape(pages, 1, 1), (pages, 1, block)).astype(jnp.int32),
-        jnp.full((pages, 1, block), -1, jnp.int32),
     )
     gathered_suffix = seq_gather(jnp.stack([new_keys, new_values]), seq_n_blocks, 1)
     suffix_parts = (
@@ -295,7 +325,7 @@
         position_all.reshape(runs, 1, block).astype(jnp.int32),
     )
     out = block_attention(
-        score_scale, (p_idx, p_cnt, s_idx, s_cnt), stacked_q, query_meta, prefix_parts, suffix_parts
+        score_scale, (block_wants.astype(jnp.int32), page_order, s_idx, s_cnt), stacked_q, query_meta, prefix_parts, suffix_parts
     )
     attended = (
         out.reshape(q_blocks, group_size, block, HEAD)

time: 288 us -> 258 us (0.90)
  the two profiles are of different devices: /device:TPU:167 before, /device:TPU:165 now
where the time goes in v4:
time: 258 us; the launch traced here: 253 us
  Pallas kernels  186 us (72%)
  other arithmetic  21.3 us (8%)
  local copies, waits for them, and re-layouts  19 us (7%)
  between operations  14.3 us (6%)
  matrix products  11.6 us (4%)
    pallas_call x2, Pallas kernels, seq_gather(): pl.pallas_call(functools.partial(seq_gather_kernel, chips), out_shape=jax...  167 us
    pallas_call x1, Pallas kernels, block_attention(): pl.pallas_call(functools.partial(attention_kernel, scale, 4), out_shape=j...  19.3 us
    reshape x1, matrix products, body(): jnp.dot(normed, w_query, preferred_element_type=jnp.float32)  6.37 us
  transfers between devices with their start and end apart: 1, of which 0 were waited for; matrix products, arithmetic and copies ran while one was open for 8% of the time, Pallas kernels for 42%

profile of v4, /device:TPU:165, one launch (start us, length us, event | category | flops | bytes accessed | tf_op | source)
XLA Modules:
  0.0 253.2 jit_solution(3683427363167794505)
XLA Ops:
  7.9 2.7 %sort.34 = (s32[64]{0:T(128)}, s32[64]{0:T(128)S(1)}) sort(s32[64]{0:T(128)} %param.18, s32[64]{0:T(128)S(1)} %iota.27), dimensions={0}, to_apply=%region_4.5 | sort | flops 384 | bytes 1024 | tf_op jit(solution)/shard_map/jit(argsort)/sort | solution.py:304
  13.0 1.0 convert_reduce_fusion
  14.0 1.0 select_reduce_fusion
  15.0 0.8 sub.16
  16.0 0.9 bitcast_reduce_fusion.2
  16.9 0.9 bitcast_reduce_fusion.1
  18.1 1.0 sort.35
  20.3 1.5 pad_maximum_fusion.x_ref
  21.9 105.6 %shard_map.130 = bf16[2,16,2,256,128]{4,3,2,1,0:T(8,128)(2,1)} custom-call(bf16[2,256,128]{2,1,0:T(8,128)(2,1)} %pad_maximum_fusion.x_ref), custom_call_target="tpu_custom_call" | custom-call | tf_op jit(solution)/shard_map/pallas_call | solution.py:119
  128.1 1.0 multiply_cosine_fusion.1
  129.1 4.8 %fusion.18 = (bf16[1,16,2,256,128]{4,3,2,1,0:T(8,128)(2,1)}, bf16[1,16,2,256,128]{4,3,2,1,0:T(8,128)(2,1)}) fusion(bf16[2,16,2,256,128]{4,3,2,1,0:T(8,128)(2,1)} %shard_map.130), kind=kLoop, calls=%fused_computation.48 | loop fusion | bytes 8388608 | tf_op jit(solution)/shard_map/slice | solution.py:318
  133.9 3.0 %fusion = f32[256]{0:T(256)S(1)} fusion(bf16[256,7168]{1,0:T(8,128)(2,1)} %all-gather.2.cloned.1.call-done), kind=kLoop, calls=%fused_computation.2 | loop fusion | flops 5504768 | bytes 3671040 | tf_op jit(solution)/shard_map/reduce_sum | solution.py:255
  137.0 1.3 convolution_bitcast_fusion
  138.3 1.2 fusion.8
  139.5 6.4 %fusion.15 = f32[256,512]{0,1:T(8,128)S(1)} fusion(bf16[7168,512]{1,0:T(8,128)(2,1)} %param.13, bf16[256,7168]{1,0:T(8,128)(2,1)S(1)} %copy-done.3, f32[7168]{0:T(1024)} %copy-done.9, f32[256]{0:T(256)S(1)} %add_rsqrt_fusion), kind=kOutput, calls=%fused_computation.46 | convolution fusion | flops 1886388224 | bytes 11564032 | tf_op jit(solution)/shard_map/reshape | solution.py:270
  145.9 0.8 subtract_convert_fusion
  146.7 1.6 concatenate.34
  148.3 1.6 concatenate.35
  149.9 2.0 maximum_bitcast_fusion
  151.9 1.8 copy.41
  153.7 3.9 %convolution_convert_fusion = bf16[256,128]{1,0:T(8,128)(2,1)S(1)} fusion(bf16[7168,128]{1,0:T(8,128)(2,1)} %param.15, bf16[256,7168]{1,0:T(8,128)(2,1)} %all-gather.2.cloned.1.call-done, f32[7168]{0:T(1024)} %copy-done.9, f32[256]{0:T(256)} %copy-done.14), kind=kOutput, calls=%fused_computation.6 | convolution fusion | flops 477134848 | bytes 5600256 | tf_op jit(solution)/shard_map/dot_general | solution.py:283
  159.0 61.4 %shard_map.131 = bf16[2,16,2,256,128]{4,3,2,1,0:T(8,128)(2,1)} custom-call(bf16[2,256,128]{2,1,0:T(8,128)(2,1)} %pad_maximum_fusion.1.x_ref), custom_call_target="tpu_custom_call" | custom-call | tf_op jit(solution)/shard_map/pallas_call | solution.py:119
  220.5 4.9 %fusion.17 = (bf16[1,16,2,256,128]{4,3,2,1,0:T(8,128)(2,1)}, bf16[1,16,2,256,128]{4,3,2,1,0:T(8,128)(2,1)}) fusion(bf16[2,16,2,256,128]{4,3,2,1,0:T(8,128)(2,1)} %shard_map.131), kind=kLoop, calls=%fused_computation.47 | loop fusion | bytes 8388608 | tf_op jit(solution)/shard_map/slice | solution.py:323
  225.4 19.3 %shard_map.132 = bf16[2,512,128]{2,1,0:T(8,128)(2,1)S(1)} custom-call(s32[2,4]{1,0:T(2,128)S(1)} %convert_element_type.39.wants, s32[4,16]{1,0:T(4,128)S(1)} %reshape.253.page_order, s32[2,64]{1,0:T(2,128)S(1)} %copy.43.s_idx, s32[2]{0:T(128)S(1)} %get-tuple-element.13.s_cnt, bf16[2,512,128]{2,1,0:T(8,128)(2,1)S(1)} %bitcast.51, ...), custom_call_target="tpu_custom_call" | custom-call | tf_op jit(solution)/shard_map/pallas_call | solution.py:223
  (62 shorter events, 8.6 us)
Async XLA Ops:
  7.2 129.7 %copy-start = (bf16[7168,128]{1,0:T(8,128)(2,1)S(1)}, bf16[7168,128]{1,0:T(8,128)(2,1)}, u32[]{:S(2)}) copy-start(bf16[7168,128]{1,0:T(8,128)(2,1)} %param.14) | copy-start | bytes 5505028
  7.2 126.7 %all-gather.2.cloned.1.call-start = ((), (), s32[]{:S(2)}) async-start(), calls=%async_computation | async-start | bytes 4128768 | tf_op jit(solution)/shard_map/all_gather | solution.py:252
  13.0 123.9 %copy-start.9 = (f32[7168]{0:T(1024)}, f32[7168]{0:T(1024)S(1)}, u32[]{:S(2)}) copy-start(f32[7168]{0:T(1024)S(1)} %convert_element_type.42) | copy-start | bytes 86020
  127.5 0.5 copy-start.12
  127.6 0.6 copy-start.10
  133.9 3.1 %copy-start.3 = (bf16[256,7168]{1,0:T(8,128)(2,1)S(1)}, bf16[256,7168]{1,0:T(8,128)(2,1)}, u32[]{:S(2)}) copy-start(bf16[256,7168]{1,0:T(8,128)(2,1)} %all-gather.2.cloned.1.call-done) | copy-start | bytes 11010052
  137.0 2.5 copy-start.14
  137.0 1.3 copy-start.11
  137.0 1.3 copy-start.13
  139.5 6.4 %copy-start.6 = (f32[256,64]{0,1:T(8,128)S(1)}, f32[256,64]{0,1:T(8,128)}, u32[]{:S(2)}) copy-start(f32[256,64]{0,1:T(8,128)} %get-tuple-element.24) | copy-start | bytes 196612
  139.5 6.4 %copy-start.7 = (f32[256,64]{0,1:T(8,128)S(1)}, f32[256,64]{0,1:T(8,128)}, u32[]{:S(2)}) copy-start(f32[256,64]{0,1:T(8,128)} %get-tuple-element.25) | copy-start | bytes 196612
  153.7 4.6 %copy-start.4 = (bf16[256,1,64]{2,0,1:T(8,128)(2,1)S(1)}, bf16[256,1,64]{2,0,1:T(8,128)(2,1)}, u32[]{:S(2)}) copy-start(bf16[256,1,64]{2,0,1:T(8,128)(2,1)} %get-tuple-element.23) | copy-start | bytes 98308
  157.6 0.6 copy-start.8
  220.5 4.9 %copy-start.1 = (bf16[1,16,2,256,128]{4,3,2,1,0:T(8,128)(2,1)S(1)}, bf16[1,16,2,256,128]{4,3,2,1,0:T(8,128)(2,1)}, u32[]{:S(2)}) copy-start(bf16[1,16,2,256,128]{4,3,2,1,0:T(8,128)(2,1)} %get-tuple-element.19) | copy-start | bytes 6291460
  220.5 4.9 %copy-start.2 = (bf16[2,4,128,128]{3,2,1,0:T(8,128)(2,1)S(1)}, bf16[2,4,128,128]{3,2,1,0:T(8,128)(2,1)}, u32[]{:S(2)}) copy-start(bf16[2,4,128,128]{3,2,1,0:T(8,128)(2,1)} %copy.41) | copy-start | bytes 786436
  225.4 20.3 %copy-start.5 = (bf16[256,1,64]{2,0,1:T(8,128)(2,1)S(1)}, bf16[256,1,64]{2,0,1:T(8,128)(2,1)}, u32[]{:S(2)}) copy-start(bf16[256,1,64]{2,0,1:T(8,128)(2,1)} %get-tuple-element.23) | copy-start | bytes 98308
Sparse Core Ops, SparseCore 0:
  10.6 109.2 all-gather.1

commit v5 on v4

--- a/solution.py
+++ b/solution.py
@@ -45,70 +45,143 @@
     return (request, position, wanted)
 
 
-def seq_gather_kernel(chips, x_ref, o_ref, send_sem, recv_sem, fwd_send, fwd_recv, local_sem):
+def seq_gather_kernel(
+    zs, xs, x_ref, o_ref, z_send, z_recv, r_send, r_recv, f_send, f_recv, c_send, c_recv, local_sem
+):
     me = lax.axis_index("seq")
+    core = me % 2
     chip = me // 2
-    core = me % 2
-    partner = chip * 2 + (1 - core)
+    za = chip // xs
+    xb = chip % xs
+    right = lax.rem(xb + 1, xs)
+    left = lax.rem(xb + xs - 1, xs)
     parts = x_ref.shape[0]
     mesh_id = pl.DeviceIdType.MESH
+
+    def seq_of(z, x, c):
+        return (z * xs + x) * 2 + c
+
+    def signal(sem, target):
+        pl.semaphore_signal(sem, inc=1, device_id={"seq": target}, device_id_type=mesh_id)
+
     barrier = pltpu.get_barrier_semaphore()
 
     def greet(k, carry):
-        peer = lax.rem(chip + k, chips) * 2 + core
-        pl.semaphore_signal(barrier, inc=1, device_id={"seq": peer}, device_id_type=mesh_id)
+        signal(barrier, seq_of(lax.rem(za + k, zs), xb, core))
         return carry
 
-    lax.fori_loop(1, chips, greet, 0)
-    pl.semaphore_signal(barrier, inc=1, device_id={"seq": partner}, device_id_type=mesh_id)
-    pl.semaphore_wait(barrier, chips)
-    local = pltpu.make_async_copy(x_ref, o_ref.at[:, chip, core], local_sem)
+    lax.fori_loop(1, zs, greet, 0)
+    signal(barrier, seq_of(za, right, core))
+    signal(barrier, seq_of(za, left, core))
+    signal(barrier, seq_of(za, xb, 1 - core))
+    pl.semaphore_wait(barrier, zs + 2)
+
+    local = pltpu.make_async_copy(x_ref, o_ref.at[:, za, xb, core], local_sem)
     local.start()
 
-    def push(peer_chip, sender, receiver):
-        return [
-            pltpu.make_async_remote_copy(
-                src_ref=x_ref.at[a],
-                dst_ref=o_ref.at[a, receiver, core],
-                send_sem=send_sem.at[a, sender],
-                recv_sem=recv_sem.at[a, receiver],
-                device_id={"seq": peer_chip * 2 + core},
-                device_id_type=mesh_id,
-            )
-            for a in range(parts)
-        ]
-
-    def send(k, carry):
-        peer_chip = lax.rem(chip + k, chips)
-        for copy in push(peer_chip, peer_chip, chip):
-            copy.start()
+    def z_copy(a, peer_z, slot_z):
+        return pltpu.make_async_remote_copy(
+            src_ref=x_ref.at[a],
+            dst_ref=o_ref.at[a, slot_z, xb, core],
+            send_sem=z_send.at[a, peer_z],
+            recv_sem=z_recv.at[a, slot_z],
+            device_id={"seq": seq_of(peer_z, xb, core)},
+            device_id_type=mesh_id,
+        )
+
+    def z_start(k, carry):
+        peer_z = lax.rem(za + k, zs)
+        for a in range(parts):
+            z_copy(a, peer_z, za).start()
         return carry
 
-    lax.fori_loop(1, chips, send, 0)
-
-    def finish(k, carry):
-        peer_chip = lax.rem(chip + k, chips)
-        for copy in push(peer_chip, peer_chip, peer_chip):
+    lax.fori_loop(1, zs, z_start, 0)
+
+    def z_finish(k, carry):
+        peer_z = lax.rem(za + k, zs)
+        for a in range(parts):
+            copy = z_copy(a, peer_z, peer_z)
             copy.wait_send()
             copy.wait_recv()
         return carry
 
-    lax.fori_loop(1, chips, finish, 0)
+    lax.fori_loop(1, zs, z_finish, 0)
     local.wait()
-    forward = [
+
+    def ring_copy(a, side, group, target_x, sem_side):
+        return pltpu.make_async_remote_copy(
+            src_ref=o_ref.at[a, :, group, core],
+            dst_ref=o_ref.at[a, :, group, core],
+            send_sem=r_send.at[a, side],
+            recv_sem=r_recv.at[a, sem_side],
+            device_id={"seq": seq_of(za, target_x, core)},
+            device_id_type=mesh_id,
+        )
+
+    outgoing = []
+    for a in range(parts):
+        outgoing.append(ring_copy(a, 0, xb, right, 0))
+        outgoing.append(ring_copy(a, 1, xb, left, 1))
+    for copy in outgoing:
+        copy.start()
+    for a in range(parts):
+        ring_copy(a, 0, left, right, 0).wait_recv()
+        ring_copy(a, 1, right, left, 1).wait_recv()
+    for copy in outgoing:
+        copy.wait_send()
+
+    far = lax.rem(xb + 2, xs)
+    relay_k = pltpu.make_async_remote_copy(
+        src_ref=o_ref.at[0, :, left, core],
+        dst_ref=o_ref.at[0, :, left, core],
+        send_sem=f_send.at[0],
+        recv_sem=f_recv.at[0],
+        device_id={"seq": seq_of(za, right, core)},
+        device_id_type=mesh_id,
+    )
+    relay_v = pltpu.make_async_remote_copy(
+        src_ref=o_ref.at[1, :, right, core],
+        dst_ref=o_ref.at[1, :, right, core],
+        send_sem=f_send.at[1],
+        recv_sem=f_recv.at[1],
+        device_id={"seq": seq_of(za, left, core)},
+        device_id_type=mesh_id,
+    )
+    relay_k.start()
+    relay_v.start()
+    pltpu.make_async_remote_copy(
+        src_ref=o_ref.at[0, :, far, core],
+        dst_ref=o_ref.at[0, :, far, core],
+        send_sem=f_send.at[0],
+        recv_sem=f_recv.at[0],
+        device_id={"seq": seq_of(za, right, core)},
+        device_id_type=mesh_id,
+    ).wait_recv()
+    pltpu.make_async_remote_copy(
+        src_ref=o_ref.at[1, :, far, core],
+        dst_ref=o_ref.at[1, :, far, core],
+        send_sem=f_send.at[1],
+        recv_sem=f_recv.at[1],
+        device_id={"seq": seq_of(za, left, core)},
+        device_id_type=mesh_id,
+    ).wait_recv()
+    relay_k.wait_send()
+    relay_v.wait_send()
+
+    across = [
         pltpu.make_async_remote_copy(
-            src_ref=o_ref.at[a, :, core],
-            dst_ref=o_ref.at[a, :, core],
-            send_sem=fwd_send.at[a],
-            recv_sem=fwd_recv.at[a],
-            device_id={"seq": partner},
+            src_ref=o_ref.at[a, :, :, core],
+            dst_ref=o_ref.at[a, :, :, core],
+            send_sem=c_send.at[a],
+            recv_sem=c_recv.at[a],
+            device_id={"seq": seq_of(za, xb, 1 - core)},
             device_id_type=mesh_id,
         )
         for a in range(parts)
     ]
-    for copy in forward:
+    for copy in across:
         copy.start()
-    for copy in forward:
+    for copy in across:
         copy.wait_send()
         copy.wait_recv()
 
@@ -116,14 +189,20 @@
 def seq_gather(stacked, n, cid):
     parts, rows, cols = stacked.shape
     chips = n // 2
+    xs = 4
+    zs = chips // xs
     return pl.pallas_call(
-        functools.partial(seq_gather_kernel, chips),
-        out_shape=jax.ShapeDtypeStruct((parts, chips, 2, rows, cols), stacked.dtype),
+        functools.partial(seq_gather_kernel, zs, xs),
+        out_shape=jax.ShapeDtypeStruct((parts, zs, xs, 2, rows, cols), stacked.dtype),
         in_specs=[pl.BlockSpec(memory_space=pl.ANY)],
         out_specs=pl.BlockSpec(memory_space=pl.ANY),
         scratch_shapes=[
-            pltpu.SemaphoreType.DMA((parts, chips)),
-            pltpu.SemaphoreType.DMA((parts, chips)),
+            pltpu.SemaphoreType.DMA((parts, zs)),
+            pltpu.SemaphoreType.DMA((parts, zs)),
+            pltpu.SemaphoreType.DMA((parts, 2)),
+            pltpu.SemaphoreType.DMA((parts, 2)),
+            pltpu.SemaphoreType.DMA((parts,)),
+            pltpu.SemaphoreType.DMA((parts,)),
             pltpu.SemaphoreType.DMA((parts,)),
             pltpu.SemaphoreType.DMA((parts,)),
             pltpu.SemaphoreType.DMA,

time: 258 us -> 222 us (0.86)
  the two profiles are of different devices: /device:TPU:165 before, /device:TPU:68 now
where the time goes in v5:
time: 222 us
  Pallas kernels  112 us (50%)
  waiting for transfers between devices  43.8 us (20%)
  other arithmetic  21.3 us (10%)
  local copies, waits for them, and re-layouts  19 us (9%)
  between operations  14.3 us (6%)
  matrix products  11.6 us (5%)
    pallas_call x2, Pallas kernels, seq_gather(): pl.pallas_call(functools.partial(seq_gather_kernel, zs, xs), out_shape=ja...  82.1 us
    all_gather x1, waiting for transfers between devices, body(): gathered = lax.all_gather(hidden, 'tp', axis=1, tiled=True)  43.1 us
    pallas_call x1, Pallas kernels, block_attention(): pl.pallas_call(functools.partial(attention_kernel, scale, 4), out_shape=j...  29.4 us
    reshape x1, matrix products, body(): jnp.dot(normed, w_query, preferred_element_type=jnp.float32)  6.37 us
    slice x1, local copies, waits for them, and re-layouts, body(): gathered_suffix[1].reshape(runs, block, HEAD)  4.9 us
    slice x1, local copies, waits for them, and re-layouts, body(): gathered_prefix[1].reshape(pages, block, HEAD)  4.76 us
  transfers between devices with their start and end apart: 1, of which 1 were waited for; matrix products, arithmetic and copies ran while one was open for 9% of the time, Pallas kernels for 20%

profile of v5, /device:TPU:68, one launch (start us, length us, event | category | flops | bytes accessed | tf_op | source)
XLA Modules:
  0.0 221.5 jit_solution(173450543468322364)
XLA Ops:
  7.9 2.7 %sort.34 = (s32[64]{0:T(128)}, s32[64]{0:T(128)S(1)}) sort(s32[64]{0:T(128)} %param.18, s32[64]{0:T(128)S(1)} %iota.27), dimensions={0}, to_apply=%region_4.5 | sort | flops 384 | bytes 1024 | tf_op jit(solution)/shard_map/jit(argsort)/sort | solution.py:383
  13.0 1.0 convert_reduce_fusion
  14.0 1.0 select_reduce_fusion
  15.0 0.8 sub.16
  16.0 0.9 bitcast_reduce_fusion.2
  16.9 0.9 bitcast_reduce_fusion.1
  18.1 1.0 sort.35
  20.3 1.5 pad_maximum_fusion.x_ref
  21.9 45.0 %shard_map.130 = bf16[2,4,4,2,256,128]{5,4,3,2,1,0:T(8,128)(2,1)} custom-call(bf16[2,256,128]{2,1,0:T(8,128)(2,1)} %pad_maximum_fusion.x_ref), custom_call_target="tpu_custom_call" | custom-call | tf_op jit(solution)/shard_map/pallas_call | solution.py:194
  67.6 1.0 multiply_cosine_fusion.1
  68.5 4.8 %fusion.18 = (bf16[1,4,4,2,256,128]{5,4,3,2,1,0:T(8,128)(2,1)}, bf16[1,4,4,2,256,128]{5,4,3,2,1,0:T(8,128)(2,1)}) fusion(bf16[2,4,4,2,256,128]{5,4,3,2,1,0:T(8,128)(2,1)} %shard_map.130), kind=kLoop, calls=%fused_computation.48 | loop fusion | bytes 8388608 | tf_op jit(solution)/shard_map/slice | solution.py:397
  73.3 43.1 %all-gather.2.cloned.1.call-done = bf16[256,7168]{1,0:T(8,128)(2,1)} async-done(((bf16[256,896]{1,0:T(8,128)(2,1)}), bf16[256,7168]{1,0:T(8,128)(2,1)}) %all-gather.2.cloned.1.call-update) | async-done | bytes 3670032 | tf_op jit(solution)/shard_map/all_gather | solution.py:331
  116.4 3.0 %fusion = f32[256]{0:T(256)S(1)} fusion(bf16[256,7168]{1,0:T(8,128)(2,1)} %all-gather.2.cloned.1.call-done), kind=kLoop, calls=%fused_computation.2 | loop fusion | flops 5504768 | bytes 3671040 | tf_op jit(solution)/shard_map/reduce_sum | solution.py:334
  119.5 1.3 convolution_bitcast_fusion
  120.9 1.2 fusion.8
  122.1 6.4 %fusion.15 = f32[256,512]{0,1:T(8,128)S(1)} fusion(bf16[7168,512]{1,0:T(8,128)(2,1)} %param.13, bf16[256,7168]{1,0:T(8,128)(2,1)S(1)} %copy-done.3, f32[7168]{0:T(1024)} %copy-done.9, f32[256]{0:T(256)S(1)} %add_rsqrt_fusion), kind=kOutput, calls=%fused_computation.46 | convolution fusion | flops 1886388224 | bytes 11564032 | tf_op jit(solution)/shard_map/reshape | solution.py:349
  129.2 1.6 concatenate.34
  130.8 1.6 concatenate.35
  132.4 2.0 maximum_bitcast_fusion
  134.4 1.8 copy.41
  136.2 3.9 %convolution_convert_fusion = bf16[256,128]{1,0:T(8,128)(2,1)S(1)} fusion(bf16[7168,128]{1,0:T(8,128)(2,1)} %param.15, bf16[256,7168]{1,0:T(8,128)(2,1)} %all-gather.2.cloned.1.call-done, f32[7168]{0:T(1024)} %copy-done.9, f32[256]{0:T(256)} %copy-done.14), kind=kOutput, calls=%fused_computation.6 | convolution fusion | flops 477134848 | bytes 5600256 | tf_op jit(solution)/shard_map/dot_general | solution.py:362
  141.5 37.1 %shard_map.131 = bf16[2,4,4,2,256,128]{5,4,3,2,1,0:T(8,128)(2,1)} custom-call(bf16[2,256,128]{2,1,0:T(8,128)(2,1)} %pad_maximum_fusion.1.x_ref), custom_call_target="tpu_custom_call" | custom-call | tf_op jit(solution)/shard_map/pallas_call | solution.py:194
  178.7 4.9 %fusion.17 = (bf16[1,4,4,2,256,128]{5,4,3,2,1,0:T(8,128)(2,1)}, bf16[1,4,4,2,256,128]{5,4,3,2,1,0:T(8,128)(2,1)}) fusion(bf16[2,4,4,2,256,128]{5,4,3,2,1,0:T(8,128)(2,1)} %shard_map.131), kind=kLoop, calls=%fused_computation.47 | loop fusion | bytes 8388608 | tf_op jit(solution)/shard_map/slice | solution.py:402
  183.6 29.4 %shard_map.132 = bf16[2,512,128]{2,1,0:T(8,128)(2,1)S(1)} custom-call(s32[2,4]{1,0:T(2,128)S(1)} %convert_element_type.39.wants, s32[4,16]{1,0:T(4,128)S(1)} %reshape.253.page_order, s32[2,64]{1,0:T(2,128)S(1)} %copy.43.s_idx, s32[2]{0:T(128)S(1)} %get-tuple-element.13.s_cnt, bf16[2,512,128]{2,1,0:T(8,128)(2,1)S(1)} %bitcast.51, ...), custom_call_target="tpu_custom_call" | custom-call | tf_op jit(solution)/shard_map/pallas_call | solution.py:302
  (62 shorter events, 9.4 us)
Async XLA Ops:
  7.2 112.2 %copy-start = (bf16[7168,128]{1,0:T(8,128)(2,1)S(1)}, bf16[7168,128]{1,0:T(8,128)(2,1)}, u32[]{:S(2)}) copy-start(bf16[7168,128]{1,0:T(8,128)(2,1)} %param.14) | copy-start | bytes 5505028
  7.2 109.2 %all-gather.2.cloned.1.call-start = ((), (), s32[]{:S(2)}) async-start(), calls=%async_computation | async-start | bytes 4128768 | tf_op jit(solution)/shard_map/all_gather | solution.py:331
  13.0 106.4 %copy-start.9 = (f32[7168]{0:T(1024)}, f32[7168]{0:T(1024)S(1)}, u32[]{:S(2)}) copy-start(f32[7168]{0:T(1024)S(1)} %convert_element_type.42) | copy-start | bytes 86020
  66.9 0.5 copy-start.12
  67.0 0.6 copy-start.10
  116.4 3.1 %copy-start.3 = (bf16[256,7168]{1,0:T(8,128)(2,1)S(1)}, bf16[256,7168]{1,0:T(8,128)(2,1)}, u32[]{:S(2)}) copy-start(bf16[256,7168]{1,0:T(8,128)(2,1)} %all-gather.2.cloned.1.call-done) | copy-start | bytes 11010052
  119.5 2.5 %copy-start.14 = (f32[256]{0:T(256)}, f32[256]{0:T(256)S(1)}, u32[]{:S(2)}) copy-start(f32[256]{0:T(256)S(1)} %add_rsqrt_fusion) | copy-start | bytes 3076
  119.5 1.3 copy-start.11
  119.5 1.3 copy-start.13
  122.1 6.4 %copy-start.6 = (f32[256,64]{0,1:T(8,128)S(1)}, f32[256,64]{0,1:T(8,128)}, u32[]{:S(2)}) copy-start(f32[256,64]{0,1:T(8,128)} %get-tuple-element.24) | copy-start | bytes 196612
  122.1 6.4 %copy-start.7 = (f32[256,64]{0,1:T(8,128)S(1)}, f32[256,64]{0,1:T(8,128)}, u32[]{:S(2)}) copy-start(f32[256,64]{0,1:T(8,128)} %get-tuple-element.25) | copy-start | bytes 196612
  136.2 4.6 %copy-start.4 = (bf16[256,1,64]{2,0,1:T(8,128)(2,1)S(1)}, bf16[256,1,64]{2,0,1:T(8,128)(2,1)}, u32[]{:S(2)}) copy-start(bf16[256,1,64]{2,0,1:T(8,128)(2,1)} %get-tuple-element.23) | copy-start | bytes 98308
  140.2 0.6 copy-start.8
  178.7 4.9 %copy-start.1 = (bf16[1,4,4,2,256,128]{5,4,3,2,1,0:T(8,128)(2,1)S(1)}, bf16[1,4,4,2,256,128]{5,4,3,2,1,0:T(8,128)(2,1)}, u32[]{:S(2)}) copy-start(bf16[1,4,4,2,256,128]{5,4,3,2,1,0:T(8,128)(2,1)} %get-tuple-element.19) | copy-start | bytes 6291460
  178.7 4.9 %copy-start.2 = (bf16[2,4,128,128]{3,2,1,0:T(8,128)(2,1)S(1)}, bf16[2,4,128,128]{3,2,1,0:T(8,128)(2,1)}, u32[]{:S(2)}) copy-start(bf16[2,4,128,128]{3,2,1,0:T(8,128)(2,1)} %copy.41) | copy-start | bytes 786436
  183.6 30.4 %copy-start.5 = (bf16[256,1,64]{2,0,1:T(8,128)(2,1)S(1)}, bf16[256,1,64]{2,0,1:T(8,128)(2,1)}, u32[]{:S(2)}) copy-start(bf16[256,1,64]{2,0,1:T(8,128)(2,1)} %get-tuple-element.23) | copy-start | bytes 98308
Sparse Core Ops, SparseCore 0:
  10.6 105.6 all-gather.1

commit v6 on v5

--- a/solution.py
+++ b/solution.py
@@ -211,6 +211,110 @@
     )(stacked)
 
 
+def tp_gather_kernel(ys, x_ref, o_ref, p_send, p_recv, r_send, r_recv, f_send, f_recv, local_sem):
+    me = lax.axis_index("tp")
+    yy = me // 2
+    zh = me % 2
+    right = lax.rem(yy + 1, ys)
+    left = lax.rem(yy + ys - 1, ys)
+    far = lax.rem(yy + 2, ys)
+    width = x_ref.shape[1]
+    mesh_id = pl.DeviceIdType.MESH
+
+    def cols(y, h):
+        return pl.ds(pl.multiple_of((y * 2 + h) * width, 128), width)
+
+    def pair(y):
+        return pl.ds(pl.multiple_of(y * 2 * width, 128), 2 * width)
+
+    def signal(target):
+        pl.semaphore_signal(barrier, inc=1, device_id={"tp": target}, device_id_type=mesh_id)
+
+    barrier = pltpu.get_barrier_semaphore()
+    signal(yy * 2 + 1 - zh)
+    signal(right * 2 + zh)
+    signal(left * 2 + zh)
+    pl.semaphore_wait(barrier, 3)
+
+    local = pltpu.make_async_copy(x_ref, o_ref.at[:, cols(yy, zh)], local_sem)
+    local.start()
+    to_partner = pltpu.make_async_remote_copy(
+        src_ref=x_ref,
+        dst_ref=o_ref.at[:, cols(yy, zh)],
+        send_sem=p_send,
+        recv_sem=p_recv,
+        device_id={"tp": yy * 2 + 1 - zh},
+        device_id_type=mesh_id,
+    )
+    to_partner.start()
+    pltpu.make_async_remote_copy(
+        src_ref=x_ref,
+        dst_ref=o_ref.at[:, cols(yy, 1 - zh)],
+        send_sem=p_send,
+        recv_sem=p_recv,
+        device_id={"tp": yy * 2 + 1 - zh},
+        device_id_type=mesh_id,
+    ).wait_recv()
+    local.wait()
+    to_partner.wait_send()
+
+    def ring(group, target, side):
+        return pltpu.make_async_remote_copy(
+            src_ref=o_ref.at[:, pair(group)],
+            dst_ref=o_ref.at[:, pair(group)],
+            send_sem=r_send.at[side],
+            recv_sem=r_recv.at[side],
+            device_id={"tp": target * 2 + zh},
+            device_id_type=mesh_id,
+        )
+
+    outgoing = [ring(yy, right, 0), ring(yy, left, 1)]
+    for copy in outgoing:
+        copy.start()
+    ring(left, right, 0).wait_recv()
+    ring(right, left, 1).wait_recv()
+    for copy in outgoing:
+        copy.wait_send()
+
+    def relay(group, h, target, side):
+        return pltpu.make_async_remote_copy(
+            src_ref=o_ref.at[:, cols(group, h)],
+            dst_ref=o_ref.at[:, cols(group, h)],
+            send_sem=f_send.at[side],
+            recv_sem=f_recv.at[side],
+            device_id={"tp": target * 2 + zh},
+            device_id_type=mesh_id,
+        )
+
+    relays = [relay(left, 0, right, 0), relay(right, 1, left, 1)]
+    for copy in relays:
+        copy.start()
+    relay(far, 0, right, 0).wait_recv()
+    relay(far, 1, left, 1).wait_recv()
+    for copy in relays:
+        copy.wait_send()
+
+
+def tp_gather(block, n, cid):
+    rows, width = block.shape
+    return pl.pallas_call(
+        functools.partial(tp_gather_kernel, n // 2),
+        out_shape=jax.ShapeDtypeStruct((rows, width * n), block.dtype),
+        in_specs=[pl.BlockSpec(memory_space=pl.ANY)],
+        out_specs=pl.BlockSpec(memory_space=pl.ANY),
+        scratch_shapes=[
+            pltpu.SemaphoreType.DMA,
+            pltpu.SemaphoreType.DMA,
+            pltpu.SemaphoreType.DMA((2,)),
+            pltpu.SemaphoreType.DMA((2,)),
+            pltpu.SemaphoreType.DMA((2,)),
+            pltpu.SemaphoreType.DMA((2,)),
+            pltpu.SemaphoreType.DMA,
+        ],
+        compiler_params=pltpu.CompilerParams(collective_id=cid, has_side_effects=True),
+    )(block)
+
+
 def attention_kernel(
     scale, group_pages,
     wants, page_order, s_idx, s_cnt,
@@ -316,6 +420,7 @@
 
 def body(
     seq_n,
+    tp_n,
     hidden,
     norm_gain,
     w_query,
@@ -328,7 +433,10 @@
     suffix_lengths,
     row_order,
 ):
-    gathered = lax.all_gather(hidden, "tp", axis=1, tiled=True)
+    gathered_prefix = lax.all_gather(
+        jnp.concatenate([prefix_keys, prefix_values], axis=1), "seq", axis=0, tiled=True
+    )
+    gathered = tp_gather(hidden, tp_n, 2)
     local_rows = gathered.shape[0]
     hidden_f = gathered.astype(jnp.float32)
     mean_sq = jnp.mean(hidden_f * hidden_f, axis=1, keepdims=True)
@@ -391,10 +499,9 @@
     s_idx, s_cnt = visible_list(run_visible)
 
     seq_n_blocks = seq_n
-    gathered_prefix = seq_gather(jnp.stack([prefix_keys, prefix_values]), seq_n_blocks, 0)
     prefix_parts = (
-        gathered_prefix[0].reshape(pages, block, HEAD),
-        gathered_prefix[1].reshape(pages, block, HEAD),
+        gathered_prefix[:, :HEAD].reshape(pages, block, HEAD),
+        gathered_prefix[:, HEAD:].reshape(pages, block, HEAD),
     )
     gathered_suffix = seq_gather(jnp.stack([new_keys, new_values]), seq_n_blocks, 1)
     suffix_parts = (
@@ -416,7 +523,7 @@
 
 def solution(mesh):
     return jax.shard_map(
-        functools.partial(body, mesh.shape["seq"]),
+        functools.partial(body, mesh.shape["seq"], mesh.shape["tp"]),
         mesh=mesh,
         in_specs=(
             P("seq", "tp"),

time: 222 us -> 202 us (0.910)
  the two profiles are of different devices: /device:TPU:68 before, /device:TPU:33 now
where the time goes in v6:
time: 202 us; the launch traced here: 201 us
  Pallas kernels  137 us (68%)
  other arithmetic  21.6 us (11%)
  local copies, waits for them, and re-layouts  17.2 us (9%)
  between operations  14.4 us (7%)
  matrix products  11.1 us (5%)
    pallas_call x1, Pallas kernels, tp_gather(): pl.pallas_call(functools.partial(tp_gather_kernel, n // 2), out_shape=jax...  68.7 us
    pallas_call x1, Pallas kernels, seq_gather(): pl.pallas_call(functools.partial(seq_gather_kernel, zs, xs), out_shape=ja...  43.9 us
    pallas_call x1, Pallas kernels, block_attention(): pl.pallas_call(functools.partial(attention_kernel, scale, 4), out_shape=j...  24.4 us
    reshape x1, matrix products, body(): jnp.dot(normed, w_query, preferred_element_type=jnp.float32)  6.33 us
    slice x1, local copies, waits for them, and re-layouts, body(): gathered_suffix[1].reshape(runs, block, HEAD)  4.69 us
  transfers between devices with their start and end apart: 1, of which 0 were waited for; matrix products, arithmetic and copies ran while one was open for 21% of the time, Pallas kernels for 56%

profile of v6, /device:TPU:33, one launch (start us, length us, event | category | flops | bytes accessed | tf_op | source)
XLA Modules:
  0.0 201.3 jit_solution(17840223458235494137)
XLA Ops:
  7.2 1.7 pad_maximum_fusion
  8.9 2.7 %sort.34 = (s32[64]{0:T(128)}, s32[64]{0:T(128)S(1)}) sort(s32[64]{0:T(128)} %param.18, s32[64]{0:T(128)S(1)} %iota.27), dimensions={0}, to_apply=%region_4.5 | sort | flops 384 | bytes 1024 | tf_op jit(solution)/shard_map/jit(argsort)/sort | solution.py:491
  13.3 1.3 convert_element_type.42
  14.6 1.0 convert_reduce_fusion
  15.6 1.0 select_reduce_fusion
  16.6 0.8 sub.16
  17.6 0.9 bitcast_reduce_fusion.2
  18.5 0.9 bitcast_reduce_fusion.1
  19.7 1.0 sort.35
  21.9 68.7 %shard_map.130 = bf16[256,7168]{1,0:T(8,128)(2,1)} custom-call(bf16[256,896]{1,0:T(8,128)(2,1)} %x_ref.1), custom_call_target="tpu_custom_call" | custom-call | tf_op jit(solution)/shard_map/pallas_call | solution.py:300
  90.7 3.0 %fusion = f32[256]{0:T(256)S(1)} fusion(bf16[256,7168]{1,0:T(8,128)(2,1)} %shard_map.130), kind=kLoop, calls=%fused_computation.2 | loop fusion | flops 5504768 | bytes 3671040 | tf_op jit(solution)/shard_map/reduce_sum | solution.py:442
  94.1 6.3 %fusion.15 = f32[256,512]{0,1:T(8,128)S(1)} fusion(bf16[7168,512]{1,0:T(8,128)(2,1)} %param.13, bf16[256,7168]{1,0:T(8,128)(2,1)S(1)} %copy-done.2, f32[7168]{0:T(1024)S(1)} %copy-done.6, f32[256]{0:T(256)S(1)} %add_rsqrt_fusion), kind=kOutput, calls=%fused_computation.46 | convolution fusion | flops 1886388224 | bytes 11564032 | tf_op jit(solution)/shard_map/reshape | solution.py:457
  100.4 0.8 subtract_convert_fusion
  101.2 1.6 concatenate.37
  102.8 1.6 concatenate.38
  104.4 2.0 maximum_bitcast_fusion
  106.4 1.8 copy.41
  108.2 3.5 %convolution_bitcast_fusion = f32[256,1,128]{2,0,1:T(8,128)S(1)} fusion(bf16[7168,128]{1,0:T(8,128)(2,1)S(1)} %copy-done, bf16[256,7168]{1,0:T(8,128)(2,1)} %shard_map.130, f32[7168]{0:T(1024)} %convert_element_type.42, f32[256]{0:T(256)} %copy-done.12), kind=kOutput, calls=%fused_computation.5 | convolution fusion | flops 477102080 | bytes 5665792 | tf_op jit(solution)/shard_map/dot_general | solution.py:464
  112.4 1.3 convolution_convert_fusion
  115.1 43.9 %shard_map.131 = bf16[2,4,4,2,256,128]{5,4,3,2,1,0:T(8,128)(2,1)} custom-call(bf16[2,256,128]{2,1,0:T(8,128)(2,1)} %pad_maximum_fusion.1.x_ref), custom_call_target="tpu_custom_call" | custom-call | tf_op jit(solution)/shard_map/pallas_call | solution.py:194
  158.9 1.6 pad_maximum_fusion.2
  160.5 4.7 %fusion.17 = (bf16[1,4,4,2,256,128]{5,4,3,2,1,0:T(8,128)(2,1)}, bf16[1,4,4,2,256,128]{5,4,3,2,1,0:T(8,128)(2,1)}) fusion(bf16[2,4,4,2,256,128]{5,4,3,2,1,0:T(8,128)(2,1)} %shard_map.131), kind=kLoop, calls=%fused_computation.47 | loop fusion | bytes 8388608 | tf_op jit(solution)/shard_map/slice | solution.py:509
  165.2 3.9 %fusion.18 = (bf16[8192,128]{1,0:T(8,128)(2,1)}, bf16[8192,128]{1,0:T(8,128)(2,1)S(1)}) fusion(bf16[8192,256]{1,0:T(8,128)(2,1)} %all-gather.2.cloned.1.call-done), kind=kLoop, calls=%fused_computation.48 | loop fusion | bytes 8388608 | tf_op jit(solution)/shard_map/slice | solution.py:504
  169.1 24.4 %shard_map.132 = bf16[2,512,128]{2,1,0:T(8,128)(2,1)S(1)} custom-call(s32[2,4]{1,0:T(2,128)S(1)} %convert_element_type.39.wants, s32[4,16]{1,0:T(4,128)S(1)} %reshape.259.page_order, s32[2,64]{1,0:T(2,128)S(1)} %copy.43.s_idx, s32[2]{0:T(128)S(1)} %get-tuple-element.13.s_cnt, bf16[2,512,128]{2,1,0:T(8,128)(2,1)S(1)} %bitcast.49, ...), custom_call_target="tpu_custom_call" | custom-call | tf_op jit(solution)/shard_map/pallas_call | solution.py:406
  (62 shorter events, 6.7 us)
Async XLA Ops:
  7.2 101.0 %copy-start = (bf16[7168,128]{1,0:T(8,128)(2,1)S(1)}, bf16[7168,128]{1,0:T(8,128)(2,1)}, u32[]{:S(2)}) copy-start(bf16[7168,128]{1,0:T(8,128)(2,1)} %param.14) | copy-start | bytes 5505028
  7.2 158.0 %all-gather.2.cloned.1.call-start = ((), (), s32[]{:S(2)}) async-start(), calls=%async_computation | async-start | bytes 4325376 | tf_op jit(solution)/shard_map/all_gather | solution.py:436
  90.6 3.5 %copy-start.2 = (bf16[256,7168]{1,0:T(8,128)(2,1)S(1)}, bf16[256,7168]{1,0:T(8,128)(2,1)}, u32[]{:S(2)}) copy-start(bf16[256,7168]{1,0:T(8,128)(2,1)} %shard_map.130) | copy-start | bytes 11010052
  90.6 3.5 %copy-start.6 = (f32[7168]{0:T(1024)S(1)}, f32[7168]{0:T(1024)}, u32[]{:S(2)}) copy-start(f32[7168]{0:T(1024)} %convert_element_type.42) | copy-start | bytes 86020
  90.6 3.1 %copy-start.10 = (f32[64]{0:T(128)}, f32[64]{0:T(128)S(1)}, u32[]{:S(2)}) copy-start(f32[64]{0:T(128)S(1)} %negate_power_fusion) | copy-start | bytes 772
  90.7 3.0 %copy-start.8 = (f32[256]{0:T(256)}, f32[256]{0:T(256)S(1)}, u32[]{:S(2)}) copy-start(f32[256]{0:T(256)S(1)} %add_convert_fusion.1) | copy-start | bytes 3076
  93.8 6.7 %copy-start.12 = (f32[256]{0:T(256)}, f32[256]{0:T(256)S(1)}, u32[]{:S(2)}) copy-start(f32[256]{0:T(256)S(1)} %add_rsqrt_fusion) | copy-start | bytes 3076
  108.2 3.5 %copy-start.9 = (f32[256]{0:T(256)S(1)}, f32[256]{0:T(256)}, u32[]{:S(2)}) copy-start(f32[256]{0:T(256)} %copy-done.8) | copy-start | bytes 3076
  108.2 3.5 %copy-start.11 = (f32[64]{0:T(128)S(1)}, f32[64]{0:T(128)}, u32[]{:S(2)}) copy-start(f32[64]{0:T(128)} %copy-done.10) | copy-start | bytes 772
  108.2 4.1 %copy-start.3 = (bf16[256,7168]{1,0:T(8,128)(2,1)S(1)}, bf16[256,7168]{1,0:T(8,128)(2,1)}, u32[]{:S(2)}) copy-start(bf16[256,7168]{1,0:T(8,128)(2,1)} %shard_map.130) | copy-start | bytes 11010052
  108.2 4.1 %copy-start.7 = (f32[7168]{0:T(1024)S(1)}, f32[7168]{0:T(1024)}, u32[]{:S(2)}) copy-start(f32[7168]{0:T(1024)} %convert_element_type.42) | copy-start | bytes 86020
  108.2 4.1 %copy-start.13 = (f32[256]{0:T(256)S(1)}, f32[256]{0:T(256)}, u32[]{:S(2)}) copy-start(f32[256]{0:T(256)} %copy-done.12) | copy-start | bytes 3076
  108.2 4.1 %copy-start.14 = (bf16[7168,128]{1,0:T(8,128)(2,1)S(1)}, bf16[7168,128]{1,0:T(8,128)(2,1)}, u32[]{:S(2)}) copy-start(bf16[7168,128]{1,0:T(8,128)(2,1)} %param.15) | copy-start | bytes 5505028
  112.4 1.3 copy-start.4
  113.7 0.6 copy-start.5
  165.2 3.9 %copy-start.1 = (bf16[2,4,128,128]{3,2,1,0:T(8,128)(2,1)S(1)}, bf16[2,4,128,128]{3,2,1,0:T(8,128)(2,1)}, u32[]{:S(2)}) copy-start(bf16[2,4,128,128]{3,2,1,0:T(8,128)(2,1)} %copy.41) | copy-start | bytes 786436
Sparse Core Ops, SparseCore 0:
  9.9 82.6 all-gather.1

commit v7 on v6

--- a/solution.py
+++ b/solution.py
@@ -319,8 +319,8 @@
     scale, group_pages,
     wants, page_order, s_idx, s_cnt,
     q_ref, q_want, q_req, q_pos,
-    pk_ref, pv_ref,
-    sk_ref, sv_ref, s_tag, s_bound,
+    p_ref,
+    s_ref, s_tag, s_bound,
     o_ref, m_sc, l_sc, acc_sc, pm_sc, pl_sc, pacc_sc,
 ):
     prefixes, per_prefix = page_order.shape
@@ -345,7 +345,9 @@
         m_sc[...] = jnp.full(m_sc.shape, -1e30, jnp.float32)
         l_sc[...] = jnp.zeros(l_sc.shape, jnp.float32)
         acc_sc[...] = jnp.zeros(acc_sc.shape, jnp.float32)
-        query = q_ref[i]
+        heads = q_ref.shape[2] // q_ref.shape[1]
+        size = q_ref.shape[1]
+        query = jnp.concatenate([q_ref[i, :, h * size:(h + 1) * size] for h in range(heads)], axis=0)
         want = q_want[i]
         req = q_req[i]
         pos = q_pos[i]
@@ -364,7 +366,12 @@
 
                 def page_step(g, carry):
                     pages = [page_order[p, g * group_pages + j] for j in range(group_pages)]
-                    update(pm_sc, pl_sc, pacc_sc, [score(pk_ref[b]) for b in pages], [pv_ref[b] for b in pages])
+                    blocks = [p_ref[b] for b in pages]
+                    update(
+                        pm_sc, pl_sc, pacc_sc,
+                        [score(blk[:, :size]) for blk in blocks],
+                        [blk[:, size:] for blk in blocks],
+                    )
                     return carry
 
                 lax.fori_loop(0, per_prefix // group_pages, page_step, 0)
@@ -375,7 +382,7 @@
 
         def step(n, carry):
             b = s_idx[i, n]
-            scores = score(sk_ref[b])
+            scores = score(s_ref[0, b])
             seen = (s_tag[b] == req) & (s_bound[b] <= pos)
             run_max = m_sc[...]
             new_max = jnp.maximum(
@@ -385,17 +392,21 @@
             fade = jnp.exp(run_max - new_max)
             l_sc[...] = l_sc[...] * fade + jnp.sum(weights, axis=1, keepdims=True)
             acc_sc[...] = acc_sc[...] * fade + jnp.dot(
-                weights.astype(jnp.bfloat16), sv_ref[b], preferred_element_type=jnp.float32
+                weights.astype(jnp.bfloat16), s_ref[1, b], preferred_element_type=jnp.float32
             )
             m_sc[...] = new_max
             return carry
 
         lax.fori_loop(0, s_cnt[i], step, 0)
-        o_ref[i] = (acc_sc[...] / l_sc[...]).astype(o_ref.dtype)
+        result = (acc_sc[...] / l_sc[...]).astype(o_ref.dtype)
+        for h in range(heads):
+            o_ref[i, :, h * size:(h + 1) * size] = result[h * size:(h + 1) * size]
 
 
 def block_attention(scale, lists, queries, query_meta, prefix_parts, suffix_parts):
-    q_blocks, q_rows, width = queries.shape
+    q_blocks, block_rows, q_width = queries.shape
+    width = queries.shape[1]
+    q_rows = q_width // width * block_rows
     smem = pl.BlockSpec(memory_space=pltpu.SMEM)
     vmem = pl.BlockSpec(memory_space=pltpu.VMEM)
     state = [
@@ -405,8 +416,8 @@
     ]
     return pl.pallas_call(
         functools.partial(attention_kernel, scale, 4),
-        out_shape=jax.ShapeDtypeStruct((q_blocks, q_rows, width), jnp.bfloat16),
-        in_specs=[smem] * 4 + [vmem] * 10,
+        out_shape=jax.ShapeDtypeStruct((q_blocks, block_rows, q_width), jnp.bfloat16),
+        in_specs=[smem] * 4 + [vmem] * 8,
         out_specs=vmem,
         scratch_shapes=state + state,
         compiler_params=pltpu.CompilerParams(vmem_limit_bytes=48 * 1024 * 1024),
@@ -414,7 +425,11 @@
 
 
 def visible_list(visible):
-    order = jnp.argsort(jnp.logical_not(visible), axis=1, stable=True).astype(jnp.int32)
+    count = visible.shape[1]
+    ids = jnp.arange(count, dtype=jnp.int32)
+    rank = jnp.sum((visible[:, :, None] & (ids[:, None] < ids[None, :])[None]).astype(jnp.int32), axis=1)
+    pick = visible[:, None, :] & (rank[:, None, :] == ids[None, :, None])
+    order = jnp.sum(jnp.where(pick, ids[None, None, :], 0), axis=2).astype(jnp.int32)
     return order, jnp.sum(visible.astype(jnp.int32), axis=1)
 
 
@@ -473,11 +488,7 @@
     q_blocks = local_rows // block
     pages = page_prefix.shape[0]
     runs = row_order.shape[0] // block
-    stacked_q = (
-        queries.reshape(q_blocks, block, group_size, HEAD)
-        .transpose(0, 2, 1, 3)
-        .reshape(q_blocks, group_size * block, HEAD)
-    )
+    stacked_q = queries.reshape(q_blocks, block, group_size * HEAD)
 
     def per_query(values):
         spread = jnp.broadcast_to(values.reshape(q_blocks, 1, block), (q_blocks, group_size, block))
@@ -488,7 +499,14 @@
     block_wants = jnp.any(
         want_blocks[:, :, None] == jnp.arange(PREFIXES, dtype=jnp.int32)[None, None, :], axis=1
     )
-    page_order = jnp.argsort(page_prefix, stable=True).astype(jnp.int32).reshape(PREFIXES, -1)
+    page_ids = jnp.arange(pages, dtype=jnp.int32)
+    same = (page_prefix[:, None] == page_prefix[None, :]) & (page_ids[:, None] < page_ids[None, :])
+    page_rank = jnp.sum(same.astype(jnp.int32), axis=0)
+    per_prefix = pages // PREFIXES
+    pick = (page_prefix[None, None, :] == jnp.arange(PREFIXES, dtype=jnp.int32)[:, None, None]) & (
+        page_rank[None, None, :] == jnp.arange(per_prefix, dtype=jnp.int32)[None, :, None]
+    )
+    page_order = jnp.sum(jnp.where(pick, page_ids[None, None, :], 0), axis=2).astype(jnp.int32)
     local_place = lax.dynamic_slice_in_dim(row_order, offset, local_rows).reshape(q_blocks, block)
     first_seen = jnp.min(local_place - position.reshape(q_blocks, block), axis=1)
     last_seen = jnp.max(local_place, axis=1)
@@ -499,25 +517,17 @@
     s_idx, s_cnt = visible_list(run_visible)
 
     seq_n_blocks = seq_n
-    prefix_parts = (
-        gathered_prefix[:, :HEAD].reshape(pages, block, HEAD),
-        gathered_prefix[:, HEAD:].reshape(pages, block, HEAD),
-    )
+    prefix_parts = (gathered_prefix.reshape(pages, block, 2 * HEAD),)
     gathered_suffix = seq_gather(jnp.stack([new_keys, new_values]), seq_n_blocks, 1)
     suffix_parts = (
-        gathered_suffix[0].reshape(runs, block, HEAD),
-        gathered_suffix[1].reshape(runs, block, HEAD),
+        gathered_suffix.reshape(2, runs, block, HEAD),
         (request_all + PREFIXES).reshape(runs, 1, block).astype(jnp.int32),
         position_all.reshape(runs, 1, block).astype(jnp.int32),
     )
     out = block_attention(
         score_scale, (block_wants.astype(jnp.int32), page_order, s_idx, s_cnt), stacked_q, query_meta, prefix_parts, suffix_parts
     )
-    attended = (
-        out.reshape(q_blocks, group_size, block, HEAD)
-        .transpose(0, 2, 1, 3)
-        .reshape(local_rows, group_size * HEAD)
-    )
+    attended = out.reshape(local_rows, group_size * HEAD)
     return (attended, new_keys, new_values)
 
 

time: 202 us -> 189 us (0.936)
  the two profiles are of different devices: /device:TPU:33 before, /device:TPU:165 now
where the time goes in v7:
time: 189 us; the launch traced here: 185 us
  Pallas kernels  130 us (69%)
  other arithmetic  19.2 us (10%)
  between operations  14.3 us (8%)
  matrix products  12.7 us (7%)
  local copies, waits for them, and re-layouts  9.36 us (5%)
    pallas_call x1, Pallas kernels, tp_gather(): pl.pallas_call(functools.partial(tp_gather_kernel, n // 2), out_shape=jax...  57.3 us
    pallas_call x1, Pallas kernels, seq_gather(): pl.pallas_call(functools.partial(seq_gather_kernel, zs, xs), out_shape=ja...  49.2 us
    pallas_call x1, Pallas kernels, block_attention(): pl.pallas_call(functools.partial(attention_kernel, scale, 4), out_shape=j...  23 us
    dot_general x1, matrix products, body(): jnp.dot(normed, w_query, preferred_element_type=jnp.float32)  7.16 us
  transfers between devices with their start and end apart: 1, of which 0 were waited for; matrix products, arithmetic and copies ran while one was open for 19% of the time, Pallas kernels for 58%

profile of v7, /device:TPU:165, one launch (start us, length us, event | category | flops | bytes accessed | tf_op | source)
XLA Modules:
  0.0 185.1 jit_solution(15147678723689128112)
XLA Ops:
  7.2 1.7 pad_maximum_fusion.1
  8.9 0.7 copy.21
  10.5 0.7 convert_element_type.53
  11.2 1.0 convert_reduce_fusion
  12.2 1.0 select_reduce_fusion
  13.2 0.8 sub.16
  14.3 0.9 bitcast_reduce_fusion.2
  16.2 57.3 %shard_map.130 = bf16[256,7168]{1,0:T(8,128)(2,1)} custom-call(bf16[256,896]{1,0:T(8,128)(2,1)} %x_ref.1), custom_call_target="tpu_custom_call" | custom-call | tf_op jit(solution)/shard_map/pallas_call | solution.py:300
  73.6 2.9 %fusion = f32[256]{0:T(256)S(1)} fusion(bf16[256,7168]{1,0:T(8,128)(2,1)} %shard_map.130), kind=kLoop, calls=%fused_computation.2 | loop fusion | flops 5504768 | bytes 3671040 | tf_op jit(solution)/shard_map/reduce_sum | solution.py:457
  76.5 7.2 %fusion.16 = f32[256,512]{1,0:T(8,128)} fusion(bf16[7168,512]{1,0:T(8,128)(2,1)} %param.13, bf16[256,7168]{1,0:T(8,128)(2,1)} %shard_map.130, f32[7168]{0:T(1024)S(1)} %convert_element_type.53, f32[256]{0:T(256)S(1)} %add_rsqrt_fusion), kind=kOutput, calls=%fused_computation.54 | convolution fusion | flops 1886388224 | bytes 11564032 | tf_op jit(solution)/shard_map/dot_general | solution.py:472
  83.6 2.1 %reshape.402 = f32[256,4,128]{2,1,0:T(4,128)} reshape(f32[256,512]{1,0:T(8,128)} %fusion.16) | data formatting | bytes 1048576 | tf_op jit(solution)/shard_map/reshape | solution.py:472
  86.3 1.7 subtract_convert_fusion
  88.0 1.1 pad_maximum_fusion
  89.1 1.8 convert_element_type.56.q_ref
  90.8 3.5 %convolution_bitcast_fusion = f32[256,1,128]{2,0,1:T(8,128)S(1)} fusion(bf16[7168,128]{1,0:T(8,128)(2,1)S(1)} %copy-done, bf16[256,7168]{1,0:T(8,128)(2,1)} %shard_map.130, f32[7168]{0:T(1024)S(1)} %convert_element_type.53, f32[256]{0:T(256)S(1)} %add_rsqrt_fusion), kind=kOutput, calls=%fused_computation.5 | convolution fusion | flops 477102080 | bytes 5665792 | tf_op jit(solution)/shard_map/dot_general | solution.py:479
  94.9 2.1 %convolution_convert_fusion = bf16[256,128]{1,0:T(8,128)(2,1)S(1)} fusion(bf16[7168,128]{1,0:T(8,128)(2,1)S(1)} %copy-done.9, bf16[256,7168]{1,0:T(8,128)(2,1)S(1)} %copy-done.3, f32[7168]{0:T(1024)S(1)} %convert_element_type.53, f32[256]{0:T(256)} %copy-done.8), kind=kOutput, calls=%fused_computation.6 | convolution fusion | flops 477134848 | bytes 5600256 | tf_op jit(solution)/shard_map/dot_general | solution.py:485
  97.6 0.7 pad_maximum_fusion.2.x_ref
  98.4 49.2 %shard_map.131 = bf16[2,4,4,2,256,128]{5,4,3,2,1,0:T(8,128)(2,1)} custom-call(bf16[2,256,128]{2,1,0:T(8,128)(2,1)} %pad_maximum_fusion.2.x_ref), custom_call_target="tpu_custom_call" | custom-call | tf_op jit(solution)/shard_map/pallas_call | solution.py:194
  147.6 0.8 convert_reduce_fusion.2
  149.4 1.6 pad_maximum_fusion.3
  151.4 0.8 broadcast_add_fusion
  152.1 2.2 %copy-done.1 = bf16[8192,256]{1,0:T(8,128)(2,1)S(1)} copy-done((bf16[8192,256]{1,0:T(8,128)(2,1)S(1)}, bf16[8192,256]{1,0:T(8,128)(2,1)}, u32[]{:S(2)}) %copy-start.1) | copy-done | bytes 4194328
  154.3 0.9 copy-done.2
  155.3 23.0 %shard_map.132 = bf16[2,128,512]{2,1,0:T(8,128)(2,1)} custom-call(s32[2,4]{1,0:T(2,128)S(1)} %convert_element_type.48.wants, s32[4,16]{1,0:T(4,128)S(1)} %select_reduce_fusion.3.page_order, s32[2,64]{1,0:T(2,128)S(1)} %select_reduce_fusion.2.s_idx, s32[2]{0:T(128)S(1)} %get-tuple-element.9.s_cnt, bf16[2,128,512]{2,1,0:T(8,128)(2,1)S(1)} %copy-done.2, ...), custom_call_target="tpu_custom_call" | custom-call | tf_op jit(solution)/shard_map/pallas_call | solution.py:417
  (46 shorter events, 5.3 us)
Async XLA Ops:
  7.2 83.7 %copy-start = (bf16[7168,128]{1,0:T(8,128)(2,1)S(1)}, bf16[7168,128]{1,0:T(8,128)(2,1)}, u32[]{:S(2)}) copy-start(bf16[7168,128]{1,0:T(8,128)(2,1)} %param.14) | copy-start | bytes 5505028
  7.2 145.0 %all-gather.2.cloned.1.call-start = ((), (), s32[]{:S(2)}) async-start(), calls=%async_computation | async-start | bytes 4325376 | tf_op jit(solution)/shard_map/all_gather | solution.py:451
  12.2 1.9 %copy-start.6 = (s32[8192]{0:T(1024)}, s32[8192]{0:T(1024)S(1)}, u32[]{:S(2)}) copy-start(s32[8192]{0:T(1024)S(1)} %convert_reduce_fusion) | copy-start | bytes 98308
  76.5 14.4 %copy-start.8 = (f32[256]{0:T(256)}, f32[256]{0:T(256)S(1)}, u32[]{:S(2)}) copy-start(f32[256]{0:T(256)S(1)} %add_rsqrt_fusion) | copy-start | bytes 3076
  90.8 4.1 %copy-start.3 = (bf16[256,7168]{1,0:T(8,128)(2,1)S(1)}, bf16[256,7168]{1,0:T(8,128)(2,1)}, u32[]{:S(2)}) copy-start(bf16[256,7168]{1,0:T(8,128)(2,1)} %shard_map.130) | copy-start | bytes 11010052
  90.8 4.1 %copy-start.9 = (bf16[7168,128]{1,0:T(8,128)(2,1)S(1)}, bf16[7168,128]{1,0:T(8,128)(2,1)}, u32[]{:S(2)}) copy-start(bf16[7168,128]{1,0:T(8,128)(2,1)} %param.15) | copy-start | bytes 5505028
  94.9 2.1 %copy-start.4 = (bf16[256,1,64]{2,0,1:T(8,128)(2,1)}, bf16[256,1,64]{2,0,1:T(8,128)(2,1)S(1)}, u32[]{:S(2)}) copy-start(bf16[256,1,64]{2,0,1:T(8,128)(2,1)S(1)} %get-tuple-element.15) | copy-start | bytes 98308
  97.0 0.6 copy-start.7
  97.0 52.3 %copy-start.5 = (s32[8192]{0:T(1024)S(1)}, s32[8192]{0:T(1024)}, u32[]{:S(2)}) copy-start(s32[8192]{0:T(1024)} %param.21) | copy-start | bytes 98308
  152.1 2.2 %copy-start.1 = (bf16[8192,256]{1,0:T(8,128)(2,1)S(1)}, bf16[8192,256]{1,0:T(8,128)(2,1)}, u32[]{:S(2)}) copy-start(bf16[8192,256]{1,0:T(8,128)(2,1)} %all-gather.2.cloned.1.call-done) | copy-start | bytes 12582916
  154.3 0.9 copy-start.2
Sparse Core Ops, SparseCore 0:
  9.9 76.2 all-gather.1

commit v8 on v7

--- a/solution.py
+++ b/solution.py
@@ -315,6 +315,58 @@
     )(block)
 
 
+def project_kernel(x_ref, g_ref, wq_ref, wk_ref, wv_ref, cos_ref, sin_ref, q_ref, k_ref, v_ref):
+    x = x_ref[...].astype(jnp.float32)
+    mean_sq = jnp.mean(x * x, axis=1, keepdims=True)
+    normed = (x * lax.rsqrt(mean_sq + 1e-05) * g_ref[...].astype(jnp.float32)).astype(jnp.bfloat16)
+    cosine = cos_ref[...]
+    sine = sin_ref[...]
+
+    def rotated(values):
+        half = values.shape[1] // 2
+        return values * cosine + pltpu.roll(values, half, 1) * sine
+
+    queries = jnp.dot(normed, wq_ref[...], preferred_element_type=jnp.float32)
+    for h in range(queries.shape[1] // HEAD):
+        q_ref[0, :, h * HEAD:(h + 1) * HEAD] = rotated(queries[:, h * HEAD:(h + 1) * HEAD]).astype(q_ref.dtype)
+    keys = jnp.dot(normed, wk_ref[...], preferred_element_type=jnp.float32)
+    for h in range(keys.shape[1] // HEAD):
+        k_ref[:, h * HEAD:(h + 1) * HEAD] = rotated(keys[:, h * HEAD:(h + 1) * HEAD]).astype(k_ref.dtype)
+    v_ref[...] = jnp.dot(normed, wv_ref[...], preferred_element_type=jnp.float32).astype(v_ref.dtype)
+
+
+def project(gathered, norm_gain, w_query, w_key, w_value, cosine, sine, block):
+    rows, width = gathered.shape
+    steps = rows // block
+    q_width = w_query.shape[1]
+    kv_width = w_key.shape[1]
+    whole = lambda i: (0, 0)
+    return pl.pallas_call(
+        project_kernel,
+        grid=(steps,),
+        out_shape=(
+            jax.ShapeDtypeStruct((steps, block, q_width), jnp.bfloat16),
+            jax.ShapeDtypeStruct((rows, kv_width), jnp.bfloat16),
+            jax.ShapeDtypeStruct((rows, kv_width), jnp.bfloat16),
+        ),
+        in_specs=[
+            pl.BlockSpec((block, width), lambda i: (i, 0)),
+            pl.BlockSpec((1, width), whole),
+            pl.BlockSpec((width, q_width), whole),
+            pl.BlockSpec((width, kv_width), whole),
+            pl.BlockSpec((width, kv_width), whole),
+            pl.BlockSpec((block, HEAD), lambda i: (i, 0)),
+            pl.BlockSpec((block, HEAD), lambda i: (i, 0)),
+        ],
+        out_specs=(
+            pl.BlockSpec((1, block, q_width), lambda i: (i, 0, 0)),
+            pl.BlockSpec((block, kv_width), lambda i: (i, 0)),
+            pl.BlockSpec((block, kv_width), lambda i: (i, 0)),
+        ),
+        compiler_params=pltpu.CompilerParams(vmem_limit_bytes=60 * 1024 * 1024),
+    )(gathered, norm_gain.reshape(1, width), w_query, w_key, w_value, cosine, sine)
+
+
 def attention_kernel(
     scale, group_pages,
     wants, page_order, s_idx, s_cnt,
@@ -453,11 +505,6 @@
     )
     gathered = tp_gather(hidden, tp_n, 2)
     local_rows = gathered.shape[0]
-    hidden_f = gathered.astype(jnp.float32)
-    mean_sq = jnp.mean(hidden_f * hidden_f, axis=1, keepdims=True)
-    normed = (
-        hidden_f * lax.rsqrt(mean_sq + 1e-05) * norm_gain.astype(jnp.float32)[None, :]
-    ).astype(jnp.bfloat16)
     request_all, position_all, wanted_all = locate(row_order, suffix_lengths, request_prefix)
     offset = lax.axis_index("seq") * local_rows
     request = lax.dynamic_slice_in_dim(request_all, offset, local_rows)
@@ -468,27 +515,21 @@
     q_heads = w_query.shape[1] // HEAD
     kv_heads = w_key.shape[1] // HEAD
     group_size = q_heads // kv_heads
-    queries = rotate(
-        jnp.dot(normed, w_query, preferred_element_type=jnp.float32).reshape(
-            local_rows, q_heads, HEAD
-        ),
-        rope_at,
-    ).astype(jnp.bfloat16)
-    queries = queries.reshape(local_rows, kv_heads, group_size, HEAD)
-    new_keys = rotate(
-        jnp.dot(normed, w_key, preferred_element_type=jnp.float32).reshape(
-            local_rows, kv_heads, HEAD
-        ),
-        rope_at,
-    ).astype(jnp.bfloat16)
-    new_keys = new_keys.reshape(local_rows, kv_heads * HEAD)
-    new_values = jnp.dot(normed, w_value, preferred_element_type=jnp.float32).astype(jnp.bfloat16)
+    half_dim = HEAD // 2
+    frequency = ROPE_BASE ** (-(jnp.arange(half_dim, dtype=jnp.float32) * 2.0 / HEAD))
+    angles = rope_at.astype(jnp.float32)[:, None] * frequency[None, :]
+    cosine = jnp.cos(angles)
+    sine_part = jnp.sin(angles)
+    cos_full = jnp.concatenate([cosine, cosine], axis=1)
+    sin_signed = jnp.concatenate([-sine_part, sine_part], axis=1)
+    stacked_q, new_keys, new_values = project(
+        gathered, norm_gain, w_query, w_key, w_value, cos_full, sin_signed, PAGE
+    )
     score_scale = 1.0 / math.sqrt(HEAD)
     block = PAGE
     q_blocks = local_rows // block
     pages = page_prefix.shape[0]
     runs = row_order.shape[0] // block
-    stacked_q = queries.reshape(q_blocks, block, group_size * HEAD)
 
     def per_query(values):
         spread = jnp.broadcast_to(values.reshape(q_blocks, 1, block), (q_blocks, group_size, block))

time: 189 us -> 174 us (0.921)
  matrix products: 12.7 us -> 0 us
  Pallas kernels: 130 us -> 141 us
  other arithmetic: 19.2 us -> 10.1 us
  local copies, waits for them, and re-layouts: 9.36 us -> 5.3 us
    dot_general x3 -> x0, matrix products: 12.7 us -> none  [the longest x1 7.16 us: body(): jnp.dot(normed, w_query, preferred_element_type=jnp.float32)]
    pallas_call x0 -> x1, Pallas kernels: none -> 10.5 us  [project(): pl.pallas_call(project_kernel, grid=(steps,), out_shape=(jax.ShapeDtypeSt...]
    reduce_sum x1 -> x0, other arithmetic: 2.89 us -> none  [body(): mean_sq = jnp.mean(hidden_f * hidden_f, axis=1, keepdims=True)]
    another operation x4 -> x2, other arithmetic: 2.42 us -> 0.17 us
  transfers between devices with their start and end apart: 1 -> 1, of which waited for: 0 -> 0; matrix products, arithmetic and copies ran while one was open for 19% -> 7% of each run, Pallas kernels for 58% -> 69%
where the time goes in v8:
time: 174 us; the launch traced here: 171 us
  Pallas kernels  141 us (81%)
  between operations  14.2 us (8%)
  other arithmetic  10.1 us (6%)
  local copies, waits for them, and re-layouts  5.3 us (3%)
    pallas_call x1, Pallas kernels, tp_gather(): pl.pallas_call(functools.partial(tp_gather_kernel, n // 2), out_shape=jax...  57.3 us
    pallas_call x1, Pallas kernels, seq_gather(): pl.pallas_call(functools.partial(seq_gather_kernel, zs, xs), out_shape=ja...  50.3 us
    pallas_call x1, Pallas kernels, block_attention(): pl.pallas_call(functools.partial(attention_kernel, scale, 4), out_shape=j...  23 us
    pallas_call x1, Pallas kernels, project(): pl.pallas_call(project_kernel, grid=(steps,), out_shape=(jax.ShapeDtypeSt...  10.5 us
  transfers between devices with their start and end apart: 1, of which 0 were waited for; matrix products, arithmetic and copies ran while one was open for 7% of the time, Pallas kernels for 69%

profile of v8, /device:TPU:165, one launch (start us, length us, event | category | flops | bytes accessed | tf_op | source)
XLA Modules:
  0.0 170.8 jit_solution(14009066153079463909)
XLA Ops:
  7.2 1.5 pad_maximum_fusion.2
  8.8 0.7 copy.19
  9.6 0.1 reduce
  9.7 0.7 sub.9
  10.4 1.3 reshape.253.g_ref
  11.7 1.0 convert_reduce_fusion
  12.7 1.0 select_reduce_fusion
  13.7 0.8 sub.10
  14.6 0.1 fusion.2
  14.7 0.9 bitcast_reduce_fusion.2
  15.6 0.3 reshape.263.q_pos
  16.0 0.3 reshape.262.q_req
  16.4 0.3 reshape.261.q_want
  16.7 57.3 %shard_map.130.x_ref = bf16[256,7168]{1,0:T(8,128)(2,1)} custom-call(bf16[256,896]{1,0:T(8,128)(2,1)} %x_ref.1), custom_call_target="tpu_custom_call" | custom-call | tf_op jit(solution)/shard_map/pallas_call | solution.py:300
  74.1 0.5 fusion.1
  74.7 0.8 pad_maximum_fusion
  75.5 10.5 %shard_map.131 = (bf16[2,128,512]{2,1,0:T(8,128)(2,1)}, bf16[256,128]{1,0:T(8,128)(2,1)}, bf16[256,128]{1,0:T(8,128)(2,1)}) custom-call(bf16[256,7168]{1,0:T(8,128)(2,1)} %shard_map.130.x_ref, bf16[1,7168]{1,0:T(2,128)(2,1)} %reshape.253.g_ref, bf16[7168,512]{1,0:T(8,128)(2,1)} %wq_ref.1, bf16[7168,128]{1,0:T(8,128)(2,1)} %wk_ref.1, ...), custom_call_target="tpu_custom_call" | custom-call | tf_op jit(solution)/shard_map/pallas_call | solution.py:344
  86.0 1.6 pad_maximum_fusion.3.x_ref
  87.6 50.3 %shard_map.132 = bf16[2,4,4,2,256,128]{5,4,3,2,1,0:T(8,128)(2,1)} custom-call(bf16[2,256,128]{2,1,0:T(8,128)(2,1)} %pad_maximum_fusion.3.x_ref), custom_call_target="tpu_custom_call" | custom-call | tf_op jit(solution)/shard_map/pallas_call | solution.py:194
  138.1 0.1 select_reduce_fusion.3.page_order
  138.4 0.2 convert_reduce_fusion.3
  138.6 0.1 select_reduce_fusion.2.s_idx
  138.8 2.2 %copy-done = bf16[8192,256]{1,0:T(8,128)(2,1)S(1)} copy-done((bf16[8192,256]{1,0:T(8,128)(2,1)S(1)}, bf16[8192,256]{1,0:T(8,128)(2,1)}, u32[]{:S(2)}) %copy-start) | copy-done | bytes 4194328
  141.0 23.0 %shard_map.133 = bf16[2,128,512]{2,1,0:T(8,128)(2,1)} custom-call(s32[2,4]{1,0:T(2,128)S(1)} %convert_element_type.19.wants, s32[4,16]{1,0:T(4,128)S(1)} %select_reduce_fusion.3.page_order, s32[2,64]{1,0:T(2,128)S(1)} %select_reduce_fusion.2.s_idx, s32[2]{0:T(128)S(1)} %get-tuple-element.15.s_cnt, bf16[2,128,512]{2,1,0:T(8,128)(2,1)S(1)} %copy-done.1, ...), custom_call_target="tpu_custom_call" | custom-call | tf_op jit(solution)/shard_map/pallas_call | solution.py:469
  (25 shorter events, 0.7 us)
Async XLA Ops:
  7.2 131.6 %all-gather.2.cloned.1.call-start = ((), (), s32[]{:S(2)}) async-start(), calls=%async_computation | async-start | bytes 4325376 | tf_op jit(solution)/shard_map/all_gather | solution.py:503
  86.0 51.9 %copy-start.3 = (s32[64]{0:T(128)S(1)}, s32[64]{0:T(128)}, u32[]{:S(2)}) copy-start(s32[64]{0:T(128)} %param.18) | copy-start | bytes 772
  86.0 52.2 %copy-start.2 = (s32[8192]{0:T(1024)S(1)}, s32[8192]{0:T(1024)}, u32[]{:S(2)}) copy-start(s32[8192]{0:T(1024)} %param.21) | copy-start | bytes 98308
  86.0 52.8 %copy-start.1 = (bf16[2,128,512]{2,1,0:T(8,128)(2,1)S(1)}, bf16[2,128,512]{2,1,0:T(8,128)(2,1)}, u32[]{:S(2)}) copy-start(bf16[2,128,512]{2,1,0:T(8,128)(2,1)} %get-tuple-element.6.q_ref) | copy-start | bytes 786436
  138.8 2.2 %copy-start = (bf16[8192,256]{1,0:T(8,128)(2,1)S(1)}, bf16[8192,256]{1,0:T(8,128)(2,1)}, u32[]{:S(2)}) copy-start(bf16[8192,256]{1,0:T(8,128)(2,1)} %all-gather.2.cloned.1.call-done) | copy-start | bytes 12582916
Sparse Core Ops, SparseCore 0:
  9.9 76.7 all-gather.1

commit v9 on v8

--- a/solution.py
+++ b/solution.py
@@ -211,7 +211,7 @@
     )(stacked)
 
 
-def tp_gather_kernel(ys, x_ref, o_ref, p_send, p_recv, r_send, r_recv, f_send, f_recv, local_sem):
+def tp_gather_kernel(ys, x_ref, z_ref, o_ref, r_send, r_recv, f_send, f_recv, local_sem):
     me = lax.axis_index("tp")
     yy = me // 2
     zh = me % 2
@@ -231,32 +231,16 @@
         pl.semaphore_signal(barrier, inc=1, device_id={"tp": target}, device_id_type=mesh_id)
 
     barrier = pltpu.get_barrier_semaphore()
-    signal(yy * 2 + 1 - zh)
     signal(right * 2 + zh)
     signal(left * 2 + zh)
-    pl.semaphore_wait(barrier, 3)
-
-    local = pltpu.make_async_copy(x_ref, o_ref.at[:, cols(yy, zh)], local_sem)
-    local.start()
-    to_partner = pltpu.make_async_remote_copy(
-        src_ref=x_ref,
-        dst_ref=o_ref.at[:, cols(yy, zh)],
-        send_sem=p_send,
-        recv_sem=p_recv,
-        device_id={"tp": yy * 2 + 1 - zh},
-        device_id_type=mesh_id,
-    )
-    to_partner.start()
-    pltpu.make_async_remote_copy(
-        src_ref=x_ref,
-        dst_ref=o_ref.at[:, cols(yy, 1 - zh)],
-        send_sem=p_send,
-        recv_sem=p_recv,
-        device_id={"tp": yy * 2 + 1 - zh},
-        device_id_type=mesh_id,
-    ).wait_recv()
-    local.wait()
-    to_partner.wait_send()
+    pl.semaphore_wait(barrier, 2)
+
+    own = pltpu.make_async_copy(x_ref, o_ref.at[:, cols(yy, zh)], local_sem.at[0])
+    other = pltpu.make_async_copy(z_ref, o_ref.at[:, cols(yy, 1 - zh)], local_sem.at[1])
+    own.start()
+    other.start()
+    own.wait()
+    other.wait()
 
     def ring(group, target, side):
         return pltpu.make_async_remote_copy(
@@ -295,27 +279,25 @@
         copy.wait_send()
 
 
-def tp_gather(block, n, cid):
+def tp_gather(block, partner_block, n, cid):
     rows, width = block.shape
     return pl.pallas_call(
         functools.partial(tp_gather_kernel, n // 2),
         out_shape=jax.ShapeDtypeStruct((rows, width * n), block.dtype),
-        in_specs=[pl.BlockSpec(memory_space=pl.ANY)],
+        in_specs=[pl.BlockSpec(memory_space=pl.ANY)] * 2,
         out_specs=pl.BlockSpec(memory_space=pl.ANY),
         scratch_shapes=[
-            pltpu.SemaphoreType.DMA,
-            pltpu.SemaphoreType.DMA,
             pltpu.SemaphoreType.DMA((2,)),
             pltpu.SemaphoreType.DMA((2,)),
             pltpu.SemaphoreType.DMA((2,)),
             pltpu.SemaphoreType.DMA((2,)),
-            pltpu.SemaphoreType.DMA,
+            pltpu.SemaphoreType.DMA((2,)),
         ],
         compiler_params=pltpu.CompilerParams(collective_id=cid, has_side_effects=True),
-    )(block)
-
-
-def project_kernel(x_ref, g_ref, wq_ref, wk_ref, wv_ref, cos_ref, sin_ref, q_ref, k_ref, v_ref):
+    )(block, partner_block)
+
+
+def project_kernel(x_ref, g_ref, wq_ref, wk_ref, wv_ref, cos_ref, sin_ref, q_ref, k_ref, v_ref, kv_ref):
     x = x_ref[...].astype(jnp.float32)
     mean_sq = jnp.mean(x * x, axis=1, keepdims=True)
     normed = (x * lax.rsqrt(mean_sq + 1e-05) * g_ref[...].astype(jnp.float32)).astype(jnp.bfloat16)
@@ -331,8 +313,12 @@
         q_ref[0, :, h * HEAD:(h + 1) * HEAD] = rotated(queries[:, h * HEAD:(h + 1) * HEAD]).astype(q_ref.dtype)
     keys = jnp.dot(normed, wk_ref[...], preferred_element_type=jnp.float32)
     for h in range(keys.shape[1] // HEAD):
-        k_ref[:, h * HEAD:(h + 1) * HEAD] = rotated(keys[:, h * HEAD:(h + 1) * HEAD]).astype(k_ref.dtype)
-    v_ref[...] = jnp.dot(normed, wv_ref[...], preferred_element_type=jnp.float32).astype(v_ref.dtype)
+        part = rotated(keys[:, h * HEAD:(h + 1) * HEAD]).astype(k_ref.dtype)
+        k_ref[:, h * HEAD:(h + 1) * HEAD] = part
+        kv_ref[0, :, h * HEAD:(h + 1) * HEAD] = part
+    values = jnp.dot(normed, wv_ref[...], preferred_element_type=jnp.float32).astype(v_ref.dtype)
+    v_ref[...] = values
+    kv_ref[1] = values
 
 
 def project(gathered, norm_gain, w_query, w_key, w_value, cosine, sine, block):
@@ -348,6 +334,7 @@
             jax.ShapeDtypeStruct((steps, block, q_width), jnp.bfloat16),
             jax.ShapeDtypeStruct((rows, kv_width), jnp.bfloat16),
             jax.ShapeDtypeStruct((rows, kv_width), jnp.bfloat16),
+            jax.ShapeDtypeStruct((2, rows, kv_width), jnp.bfloat16),
         ),
         in_specs=[
             pl.BlockSpec((block, width), lambda i: (i, 0)),
@@ -362,6 +349,7 @@
             pl.BlockSpec((1, block, q_width), lambda i: (i, 0, 0)),
             pl.BlockSpec((block, kv_width), lambda i: (i, 0)),
             pl.BlockSpec((block, kv_width), lambda i: (i, 0)),
+            pl.BlockSpec((2, block, kv_width), lambda i: (0, i, 0)),
         ),
         compiler_params=pltpu.CompilerParams(vmem_limit_bytes=60 * 1024 * 1024),
     )(gathered, norm_gain.reshape(1, width), w_query, w_key, w_value, cosine, sine)
@@ -503,7 +491,8 @@
     gathered_prefix = lax.all_gather(
         jnp.concatenate([prefix_keys, prefix_values], axis=1), "seq", axis=0, tiled=True
     )
-    gathered = tp_gather(hidden, tp_n, 2)
+    partner_block = lax.ppermute(hidden, "tp", [(t, t ^ 1) for t in range(tp_n)])
+    gathered = tp_gather(hidden, partner_block, tp_n, 2)
     local_rows = gathered.shape[0]
     request_all, position_all, wanted_all = locate(row_order, suffix_lengths, request_prefix)
     offset = lax.axis_index("seq") * local_rows
@@ -522,7 +511,7 @@
     sine_part = jnp.sin(angles)
     cos_full = jnp.concatenate([cosine, cosine], axis=1)
     sin_signed = jnp.concatenate([-sine_part, sine_part], axis=1)
-    stacked_q, new_keys, new_values = project(
+    stacked_q, new_keys, new_values, stacked_kv = project(
         gathered, norm_gain, w_query, w_key, w_value, cos_full, sin_signed, PAGE
     )
     score_scale = 1.0 / math.sqrt(HEAD)
@@ -559,7 +548,7 @@
 
     seq_n_blocks = seq_n
     prefix_parts = (gathered_prefix.reshape(pages, block, 2 * HEAD),)
-    gathered_suffix = seq_gather(jnp.stack([new_keys, new_values]), seq_n_blocks, 1)
+    gathered_suffix = seq_gather(stacked_kv, seq_n_blocks, 1)
     suffix_parts = (
         gathered_suffix.reshape(2, runs, block, HEAD),
         (request_all + PREFIXES).reshape(runs, 1, block).astype(jnp.int32),

time: 174 us -> 193 us (1.11)
  the two profiles are of different devices: /device:TPU:165 before, /device:TPU:38 now
where the time goes in v9:
time: 193 us
  Pallas kernels  143 us (74%)
  between operations  14.2 us (7%)
  waiting for transfers between devices  12.4 us (6%)
  other arithmetic  10.7 us (6%)
  starting transfers between devices  6.41 us (3%)
  local copies, waits for them, and re-layouts  6.07 us (3%)
    pallas_call x1, Pallas kernels, tp_gather(): pl.pallas_call(functools.partial(tp_gather_kernel, n // 2), out_shape=jax...  62.2 us
    pallas_call x1, Pallas kernels, seq_gather(): pl.pallas_call(functools.partial(seq_gather_kernel, zs, xs), out_shape=ja...  42 us
    pallas_call x1, Pallas kernels, block_attention(): pl.pallas_call(functools.partial(attention_kernel, scale, 4), out_shape=j...  28.3 us
    ppermute x1, waiting for transfers between devices, body(): lax.ppermute(hidden, 'tp', [(t, t ^ 1) for t in range(tp_n)])  12.4 us
    pallas_call x1, Pallas kernels, project(): pl.pallas_call(project_kernel, grid=(steps,), out_shape=(jax.ShapeDtypeSt...  10.5 us
    ppermute x1, starting transfers between devices, body(): lax.ppermute(hidden, 'tp', [(t, t ^ 1) for t in range(tp_n)])  6.38 us
  transfers between devices with their start and end apart: 2, of which 1 were waited for; matrix products, arithmetic and copies ran while one was open for 6% of the time, Pallas kernels for 59%

profile of v9, /device:TPU:38, one launch (start us, length us, event | category | flops | bytes accessed | tf_op | source)
XLA Modules:
  0.0 192.8 jit_solution(5105089599228010294)
XLA Ops:
  7.2 1.5 pad_maximum_fusion.2
  8.8 6.4 %collective-permute-start = (bf16[256,896]{1,0:T(8,128)(2,1)}, bf16[256,896]{1,0:T(8,128)(2,1)S(1)}, u32[]{:S(2)}, u32[]{:S(2)}) collective-permute-start(bf16[256,896]{1,0:T(8,128)(2,1)} %x_ref.1), channel_id=1, source_target_pairs={{0,1},{1,0},{2,3},{3,2},{4,5},{5,4},{6,7},{7,6},{8,9},{9,8},{10,11... | collective-permute-start | bytes 1376264 | tf_op jit(solution)/shard_map/ppermute | solution.py:494
  15.2 0.7 copy.19
  16.1 0.7 sub.9
  16.7 1.3 reshape.253.g_ref
  18.1 1.0 convert_reduce_fusion
  19.1 1.0 select_reduce_fusion
  20.1 0.8 sub.10
  21.1 0.9 bitcast_reduce_fusion.2
  22.0 0.3 reshape.263.q_pos
  22.5 0.8 convert_reduce_fusion.2
  23.3 0.7 iota_compare_fusion.5
  24.1 0.9 bitcast_reduce_fusion.1
  25.3 0.5 fusion.1
  25.8 0.3 reshape.262.q_req
  26.2 0.3 reshape.261.q_want
  26.7 0.9 pad_maximum_fusion
  27.5 12.4 %collective-permute-done.z_ref = bf16[256,896]{1,0:T(8,128)(2,1)S(1)} collective-permute-done((bf16[256,896]{1,0:T(8,128)(2,1)}, bf16[256,896]{1,0:T(8,128)(2,1)S(1)}, u32[]{:S(2)}, u32[]{:S(2)}) %collective-permute-start) | collective-permute-done | bytes 458784 | tf_op jit(solution)/shard_map/ppermute | solution.py:494
  39.9 0.8 copy-done.2
  40.7 62.2 %shard_map.130.x_ref = bf16[256,7168]{1,0:T(8,128)(2,1)} custom-call(bf16[256,896]{1,0:T(8,128)(2,1)} %x_ref.1, bf16[256,896]{1,0:T(8,128)(2,1)} %copy-done.2), custom_call_target="tpu_custom_call" | custom-call | tf_op jit(solution)/shard_map/pallas_call | solution.py:284
  102.9 10.5 %shard_map.131 = (bf16[2,128,512]{2,1,0:T(8,128)(2,1)}, bf16[256,128]{1,0:T(8,128)(2,1)}, bf16[256,128]{1,0:T(8,128)(2,1)}, bf16[2,256,128]{2,1,0:T(8,128)(2,1)}) custom-call(bf16[256,7168]{1,0:T(8,128)(2,1)} %shard_map.130.x_ref, bf16[1,7168]{1,0:T(2,128)(2,1)} %reshape.253.g_ref, bf16[7168,512]{1,0:T(8,128)(2,1)} %wq_ref.1, bf16[7168,128]{1,0:T(8,128)(2,1)} %wk_ref.1, ...), custom_call_target="tpu_custom_call" | custom-call | tf_op jit(solution)/shard_map/pallas_call | solution.py:330
  113.4 42.0 %shard_map.132 = bf16[2,4,4,2,256,128]{5,4,3,2,1,0:T(8,128)(2,1)} custom-call(bf16[2,256,128]{2,1,0:T(8,128)(2,1)} %get-tuple-element.8.x_ref), custom_call_target="tpu_custom_call" | custom-call | tf_op jit(solution)/shard_map/pallas_call | solution.py:194
  155.4 2.2 %copy-done = bf16[8192,256]{1,0:T(8,128)(2,1)S(1)} copy-done((bf16[8192,256]{1,0:T(8,128)(2,1)S(1)}, bf16[8192,256]{1,0:T(8,128)(2,1)}, u32[]{:S(2)}) %copy-start) | copy-done | bytes 4194328
  157.6 28.3 %shard_map.133 = bf16[2,128,512]{2,1,0:T(8,128)(2,1)} custom-call(s32[2,4]{1,0:T(2,128)S(1)} %convert_element_type.19.wants, s32[4,16]{1,0:T(4,128)S(1)} %select_reduce_fusion.3.page_order, s32[2,64]{1,0:T(2,128)S(1)} %select_reduce_fusion.2.s_idx, s32[2]{0:T(128)S(1)} %get-tuple-element.17.s_cnt, bf16[2,128,512]{2,1,0:T(8,128)(2,1)S(1)} %copy-done.1, ...), custom_call_target="tpu_custom_call" | custom-call | tf_op jit(solution)/shard_map/pallas_call | solution.py:457
  (24 shorter events, 1.2 us)
Async XLA Ops:
  7.2 148.3 %all-gather.2.cloned.1.call-start = ((), (), s32[]{:S(2)}) async-start(), calls=%async_computation | async-start | bytes 4325376 | tf_op jit(solution)/shard_map/all_gather | solution.py:491
  8.8 31.2 %collective-permute-start = (bf16[256,896]{1,0:T(8,128)(2,1)}, bf16[256,896]{1,0:T(8,128)(2,1)S(1)}, u32[]{:S(2)}, u32[]{:S(2)}) collective-permute-start(bf16[256,896]{1,0:T(8,128)(2,1)} %x_ref.1), channel_id=1, source_target_pairs={{0,1},{1,0},{2,3},{3,2},{4,5},{5,4},{6,7},{7,6},{8,9},{9,8},{10,11... | collective-permute-start | bytes 1376264 | tf_op jit(solution)/shard_map/ppermute | solution.py:494
  39.9 0.8 copy-start.2
  113.4 42.0 %copy-start.1 = (bf16[2,128,512]{2,1,0:T(8,128)(2,1)S(1)}, bf16[2,128,512]{2,1,0:T(8,128)(2,1)}, u32[]{:S(2)}) copy-start(bf16[2,128,512]{2,1,0:T(8,128)(2,1)} %get-tuple-element.7.q_ref) | copy-start | bytes 786436
  155.4 2.2 %copy-start = (bf16[8192,256]{1,0:T(8,128)(2,1)S(1)}, bf16[8192,256]{1,0:T(8,128)(2,1)}, u32[]{:S(2)}) copy-start(bf16[8192,256]{1,0:T(8,128)(2,1)} %all-gather.2.cloned.1.call-done) | copy-start | bytes 12582916
Sparse Core Ops, SparseCore 0:
  9.9 71.9 all-gather.1

commit v10 on v8

--- a/solution.py
+++ b/solution.py
@@ -258,39 +258,50 @@
     local.wait()
     to_partner.wait_send()
 
-    def ring(group, target, side):
+    pieces = r_send.shape[1]
+    span = x_ref.shape[0] // pieces
+
+    def ring(group, target, side, c):
+        rows = pl.ds(c * span, span)
         return pltpu.make_async_remote_copy(
-            src_ref=o_ref.at[:, pair(group)],
-            dst_ref=o_ref.at[:, pair(group)],
-            send_sem=r_send.at[side],
-            recv_sem=r_recv.at[side],
+            src_ref=o_ref.at[rows, pair(group)],
+            dst_ref=o_ref.at[rows, pair(group)],
+            send_sem=r_send.at[side, c],
+            recv_sem=r_recv.at[side, c],
             device_id={"tp": target * 2 + zh},
             device_id_type=mesh_id,
         )
 
-    outgoing = [ring(yy, right, 0), ring(yy, left, 1)]
+    outgoing = []
+    for c in range(pieces):
+        outgoing += [ring(yy, right, 0, c), ring(yy, left, 1, c)]
     for copy in outgoing:
         copy.start()
-    ring(left, right, 0).wait_recv()
-    ring(right, left, 1).wait_recv()
+    for c in range(pieces):
+        ring(left, right, 0, c).wait_recv()
+        ring(right, left, 1, c).wait_recv()
     for copy in outgoing:
         copy.wait_send()
 
-    def relay(group, h, target, side):
+    def relay(group, h, target, side, c):
+        rows = pl.ds(c * span, span)
         return pltpu.make_async_remote_copy(
-            src_ref=o_ref.at[:, cols(group, h)],
-            dst_ref=o_ref.at[:, cols(group, h)],
-            send_sem=f_send.at[side],
-            recv_sem=f_recv.at[side],
+            src_ref=o_ref.at[rows, cols(group, h)],
+            dst_ref=o_ref.at[rows, cols(group, h)],
+            send_sem=f_send.at[side, c],
+            recv_sem=f_recv.at[side, c],
             device_id={"tp": target * 2 + zh},
             device_id_type=mesh_id,
         )
 
-    relays = [relay(left, 0, right, 0), relay(right, 1, left, 1)]
+    relays = []
+    for c in range(pieces):
+        relays += [relay(left, 0, right, 0, c), relay(right, 1, left, 1, c)]
     for copy in relays:
         copy.start()
-    relay(far, 0, right, 0).wait_recv()
-    relay(far, 1, left, 1).wait_recv()
+    for c in range(pieces):
+        relay(far, 0, right, 0, c).wait_recv()
+        relay(far, 1, left, 1, c).wait_recv()
     for copy in relays:
         copy.wait_send()
 
@@ -305,17 +316,17 @@
         scratch_shapes=[
             pltpu.SemaphoreType.DMA,
             pltpu.SemaphoreType.DMA,
-            pltpu.SemaphoreType.DMA((2,)),
-            pltpu.SemaphoreType.DMA((2,)),
-            pltpu.SemaphoreType.DMA((2,)),
-            pltpu.SemaphoreType.DMA((2,)),
+            pltpu.SemaphoreType.DMA((2, 4)),
+            pltpu.SemaphoreType.DMA((2, 4)),
+            pltpu.SemaphoreType.DMA((2, 4)),
+            pltpu.SemaphoreType.DMA((2, 4)),
             pltpu.SemaphoreType.DMA,
         ],
         compiler_params=pltpu.CompilerParams(collective_id=cid, has_side_effects=True),
     )(block)
 
 
-def project_kernel(x_ref, g_ref, wq_ref, wk_ref, wv_ref, cos_ref, sin_ref, q_ref, k_ref, v_ref):
+def project_kernel(x_ref, g_ref, wq_ref, wk_ref, wv_ref, cos_ref, sin_ref, q_ref, k_ref, v_ref, kv_ref):
     x = x_ref[...].astype(jnp.float32)
     mean_sq = jnp.mean(x * x, axis=1, keepdims=True)
     normed = (x * lax.rsqrt(mean_sq + 1e-05) * g_ref[...].astype(jnp.float32)).astype(jnp.bfloat16)
@@ -331,8 +342,12 @@
         q_ref[0, :, h * HEAD:(h + 1) * HEAD] = rotated(queries[:, h * HEAD:(h + 1) * HEAD]).astype(q_ref.dtype)
     keys = jnp.dot(normed, wk_ref[...], preferred_element_type=jnp.float32)
     for h in range(keys.shape[1] // HEAD):
-        k_ref[:, h * HEAD:(h + 1) * HEAD] = rotated(keys[:, h * HEAD:(h + 1) * HEAD]).astype(k_ref.dtype)
-    v_ref[...] = jnp.dot(normed, wv_ref[...], preferred_element_type=jnp.float32).astype(v_ref.dtype)
+        part = rotated(keys[:, h * HEAD:(h + 1) * HEAD]).astype(k_ref.dtype)
+        k_ref[:, h * HEAD:(h + 1) * HEAD] = part
+        kv_ref[0, :, h * HEAD:(h + 1) * HEAD] = part
+    values = jnp.dot(normed, wv_ref[...], preferred_element_type=jnp.float32).astype(v_ref.dtype)
+    v_ref[...] = values
+    kv_ref[1] = values
 
 
 def project(gathered, norm_gain, w_query, w_key, w_value, cosine, sine, block):
@@ -348,6 +363,7 @@
             jax.ShapeDtypeStruct((steps, block, q_width), jnp.bfloat16),
             jax.ShapeDtypeStruct((rows, kv_width), jnp.bfloat16),
             jax.ShapeDtypeStruct((rows, kv_width), jnp.bfloat16),
+            jax.ShapeDtypeStruct((2, rows, kv_width), jnp.bfloat16),
         ),
         in_specs=[
             pl.BlockSpec((block, width), lambda i: (i, 0)),
@@ -362,6 +378,7 @@
             pl.BlockSpec((1, block, q_width), lambda i: (i, 0, 0)),
             pl.BlockSpec((block, kv_width), lambda i: (i, 0)),
             pl.BlockSpec((block, kv_width), lambda i: (i, 0)),
+            pl.BlockSpec((2, block, kv_width), lambda i: (0, i, 0)),
         ),
         compiler_params=pltpu.CompilerParams(vmem_limit_bytes=60 * 1024 * 1024),
     )(gathered, norm_gain.reshape(1, width), w_query, w_key, w_value, cosine, sine)
@@ -522,7 +539,7 @@
     sine_part = jnp.sin(angles)
     cos_full = jnp.concatenate([cosine, cosine], axis=1)
     sin_signed = jnp.concatenate([-sine_part, sine_part], axis=1)
-    stacked_q, new_keys, new_values = project(
+    stacked_q, new_keys, new_values, stacked_kv = project(
         gathered, norm_gain, w_query, w_key, w_value, cos_full, sin_signed, PAGE
     )
     score_scale = 1.0 / math.sqrt(HEAD)
@@ -559,7 +576,7 @@
 
     seq_n_blocks = seq_n
     prefix_parts = (gathered_prefix.reshape(pages, block, 2 * HEAD),)
-    gathered_suffix = seq_gather(jnp.stack([new_keys, new_values]), seq_n_blocks, 1)
+    gathered_suffix = seq_gather(stacked_kv, seq_n_blocks, 1)
     suffix_parts = (
         gathered_suffix.reshape(2, runs, block, HEAD),
         (request_all + PREFIXES).reshape(runs, 1, block).astype(jnp.int32),

time: 174 us -> 174 us (level)
  the two profiles are of different devices: /device:TPU:165 before, /device:TPU:160 now
where the time goes in v10:
time: 174 us; the launch traced here: 173 us
  Pallas kernels  145 us (83%)
  between operations  14.2 us (8%)
  other arithmetic  8.56 us (5%)
  local copies, waits for them, and re-layouts  5.31 us (3%)
    pallas_call x1, Pallas kernels, tp_gather(): pl.pallas_call(functools.partial(tp_gather_kernel, n // 2), out_shape=jax...  68.6 us
    pallas_call x1, Pallas kernels, seq_gather(): pl.pallas_call(functools.partial(seq_gather_kernel, zs, xs), out_shape=ja...  40.5 us
    pallas_call x1, Pallas kernels, block_attention(): pl.pallas_call(functools.partial(attention_kernel, scale, 4), out_shape=j...  25.6 us
    pallas_call x1, Pallas kernels, project(): pl.pallas_call(project_kernel, grid=(steps,), out_shape=(jax.ShapeDtypeSt...  10.5 us
  transfers between devices with their start and end apart: 1, of which 0 were waited for; matrix products, arithmetic and copies ran while one was open for 6% of the time, Pallas kernels for 69%

profile of v10, /device:TPU:160, one launch (start us, length us, event | category | flops | bytes accessed | tf_op | source)
XLA Modules:
  0.0 173.3 jit_solution(7905752648525870846)
XLA Ops:
  7.2 1.5 pad_maximum_fusion.2
  8.8 0.7 copy.19
  9.6 0.1 reduce
  9.7 0.7 sub.9
  10.4 1.3 reshape.253.g_ref
  11.7 1.0 convert_reduce_fusion
  12.7 1.0 select_reduce_fusion
  13.7 0.8 sub.10
  14.6 0.1 fusion.2
  14.7 0.9 bitcast_reduce_fusion.2
  15.6 0.3 reshape.263.q_pos
  16.0 0.3 reshape.262.q_req
  16.4 0.3 reshape.261.q_want
  16.7 68.6 %shard_map.130.x_ref = bf16[256,7168]{1,0:T(8,128)(2,1)} custom-call(bf16[256,896]{1,0:T(8,128)(2,1)} %x_ref.1), custom_call_target="tpu_custom_call" | custom-call | tf_op jit(solution)/shard_map/pallas_call | solution.py:311
  85.4 0.5 fusion.1
  86.0 0.8 pad_maximum_fusion
  86.8 10.5 %shard_map.131 = (bf16[2,128,512]{2,1,0:T(8,128)(2,1)}, bf16[256,128]{1,0:T(8,128)(2,1)}, bf16[256,128]{1,0:T(8,128)(2,1)}, bf16[2,256,128]{2,1,0:T(8,128)(2,1)}) custom-call(bf16[256,7168]{1,0:T(8,128)(2,1)} %shard_map.130.x_ref, bf16[1,7168]{1,0:T(2,128)(2,1)} %reshape.253.g_ref, bf16[7168,512]{1,0:T(8,128)(2,1)} %wq_ref.1, bf16[7168,128]{1,0:T(8,128)(2,1)} %wk_ref.1, ...), custom_call_target="tpu_custom_call" | custom-call | tf_op jit(solution)/shard_map/pallas_call | solution.py:359
  97.3 40.5 %shard_map.132 = bf16[2,4,4,2,256,128]{5,4,3,2,1,0:T(8,128)(2,1)} custom-call(bf16[2,256,128]{2,1,0:T(8,128)(2,1)} %get-tuple-element.8.x_ref), custom_call_target="tpu_custom_call" | custom-call | tf_op jit(solution)/shard_map/pallas_call | solution.py:194
  138.0 0.1 select_reduce_fusion.3.page_order
  138.1 0.1 bitcast_reduce_fusion.1
  138.2 0.2 convert_reduce_fusion.3
  138.5 0.1 select_reduce_fusion.2.s_idx
  138.7 2.2 %copy-done = bf16[8192,256]{1,0:T(8,128)(2,1)S(1)} copy-done((bf16[8192,256]{1,0:T(8,128)(2,1)S(1)}, bf16[8192,256]{1,0:T(8,128)(2,1)}, u32[]{:S(2)}) %copy-start) | copy-done | bytes 4194328
  140.9 25.6 %shard_map.133 = bf16[2,128,512]{2,1,0:T(8,128)(2,1)} custom-call(s32[2,4]{1,0:T(2,128)S(1)} %convert_element_type.19.wants, s32[4,16]{1,0:T(4,128)S(1)} %select_reduce_fusion.3.page_order, s32[2,64]{1,0:T(2,128)S(1)} %select_reduce_fusion.2.s_idx, s32[2]{0:T(128)S(1)} %get-tuple-element.17.s_cnt, bf16[2,128,512]{2,1,0:T(8,128)(2,1)S(1)} %copy-done.1, ...), custom_call_target="tpu_custom_call" | custom-call | tf_op jit(solution)/shard_map/pallas_call | solution.py:486
  (24 shorter events, 0.6 us)
Async XLA Ops:
  7.2 131.5 %all-gather.2.cloned.1.call-start = ((), (), s32[]{:S(2)}) async-start(), calls=%async_computation | async-start | bytes 4325376 | tf_op jit(solution)/shard_map/all_gather | solution.py:520
  97.3 40.6 %copy-start.3 = (s32[64]{0:T(128)S(1)}, s32[64]{0:T(128)}, u32[]{:S(2)}) copy-start(s32[64]{0:T(128)} %param.18) | copy-start | bytes 772
  97.3 40.9 %copy-start.2 = (s32[8192]{0:T(1024)S(1)}, s32[8192]{0:T(1024)}, u32[]{:S(2)}) copy-start(s32[8192]{0:T(1024)} %param.21) | copy-start | bytes 98308
  97.3 41.4 %copy-start.1 = (bf16[2,128,512]{2,1,0:T(8,128)(2,1)S(1)}, bf16[2,128,512]{2,1,0:T(8,128)(2,1)}, u32[]{:S(2)}) copy-start(bf16[2,128,512]{2,1,0:T(8,128)(2,1)} %get-tuple-element.7.q_ref) | copy-start | bytes 786436
  138.7 2.2 %copy-start = (bf16[8192,256]{1,0:T(8,128)(2,1)S(1)}, bf16[8192,256]{1,0:T(8,128)(2,1)}, u32[]{:S(2)}) copy-start(bf16[8192,256]{1,0:T(8,128)(2,1)} %all-gather.2.cloned.1.call-done) | copy-start | bytes 12582916
Sparse Core Ops, SparseCore 0:
  9.9 77.2 all-gather.1

commit v11 on v10

--- a/solution.py
+++ b/solution.py
@@ -108,6 +108,21 @@
     lax.fori_loop(1, zs, z_finish, 0)
     local.wait()
 
+    def hand(a, group, slot):
+        return pltpu.make_async_remote_copy(
+            src_ref=o_ref.at[a, :, group, slot],
+            dst_ref=o_ref.at[a, :, group, slot],
+            send_sem=c_send.at[a, group],
+            recv_sem=c_recv.at[a, group],
+            device_id={"seq": seq_of(za, xb, 1 - core)},
+            device_id_type=mesh_id,
+        )
+
+    across = []
+    for a in range(parts):
+        across.append(hand(a, xb, core))
+        across[-1].start()
+
     def ring_copy(a, side, group, target_x, sem_side):
         return pltpu.make_async_remote_copy(
             src_ref=o_ref.at[a, :, group, core],
@@ -127,6 +142,10 @@
     for a in range(parts):
         ring_copy(a, 0, left, right, 0).wait_recv()
         ring_copy(a, 1, right, left, 1).wait_recv()
+    for a in range(parts):
+        for group in (left, right):
+            across.append(hand(a, group, core))
+            across[-1].start()
     for copy in outgoing:
         copy.wait_send()
 
@@ -167,23 +186,15 @@
     ).wait_recv()
     relay_k.wait_send()
     relay_v.wait_send()
-
-    across = [
-        pltpu.make_async_remote_copy(
-            src_ref=o_ref.at[a, :, :, core],
-            dst_ref=o_ref.at[a, :, :, core],
-            send_sem=c_send.at[a],
-            recv_sem=c_recv.at[a],
-            device_id={"seq": seq_of(za, xb, 1 - core)},
-            device_id_type=mesh_id,
-        )
-        for a in range(parts)
-    ]
-    for copy in across:
-        copy.start()
+    for a in range(parts):
+        across.append(hand(a, far, core))
+        across[-1].start()
+
     for copy in across:
         copy.wait_send()
-        copy.wait_recv()
+    for a in range(parts):
+        for g in range(xs):
+            hand(a, g, 1 - core).wait_recv()
 
 
 def seq_gather(stacked, n, cid):
@@ -203,8 +214,8 @@
             pltpu.SemaphoreType.DMA((parts, 2)),
             pltpu.SemaphoreType.DMA((parts,)),
             pltpu.SemaphoreType.DMA((parts,)),
-            pltpu.SemaphoreType.DMA((parts,)),
-            pltpu.SemaphoreType.DMA((parts,)),
+            pltpu.SemaphoreType.DMA((parts, xs)),
+            pltpu.SemaphoreType.DMA((parts, xs)),
             pltpu.SemaphoreType.DMA,
         ],
         compiler_params=pltpu.CompilerParams(collective_id=cid, has_side_effects=True),

time: 174 us -> 173 us (level)
  the two profiles are of different devices: /device:TPU:160 before, /device:TPU:161 now
where the time goes in v11:
time: 173 us; the launch traced here: 172 us
  Pallas kernels  144 us (83%)
  between operations  14.2 us (8%)
  other arithmetic  8.56 us (5%)
  local copies, waits for them, and re-layouts  5.31 us (3%)
    pallas_call x1, Pallas kernels, tp_gather(): pl.pallas_call(functools.partial(tp_gather_kernel, n // 2), out_shape=jax...  66.5 us
    pallas_call x1, Pallas kernels, seq_gather(): pl.pallas_call(functools.partial(seq_gather_kernel, zs, xs), out_shape=ja...  41 us
    pallas_call x1, Pallas kernels, block_attention(): pl.pallas_call(functools.partial(attention_kernel, scale, 4), out_shape=j...  26.1 us
    pallas_call x1, Pallas kernels, project(): pl.pallas_call(project_kernel, grid=(steps,), out_shape=(jax.ShapeDtypeSt...  10.4 us
  transfers between devices with their start and end apart: 1, of which 0 were waited for; matrix products, arithmetic and copies ran while one was open for 6% of the time, Pallas kernels for 68%

profile of v11, /device:TPU:161, one launch (start us, length us, event | category | flops | bytes accessed | tf_op | source)
XLA Modules:
  0.0 172.3 jit_solution(5049219020603824865)
XLA Ops:
  7.2 1.5 pad_maximum_fusion.2
  8.8 0.7 copy.19
  9.6 0.1 reduce
  9.7 0.7 sub.9
  10.4 1.3 reshape.253.g_ref
  11.7 1.0 convert_reduce_fusion
  12.7 1.0 select_reduce_fusion
  13.7 0.8 sub.10
  14.6 0.1 fusion.2
  14.7 0.9 bitcast_reduce_fusion.2
  15.6 0.3 reshape.263.q_pos
  16.0 0.3 reshape.262.q_req
  16.4 0.3 reshape.261.q_want
  16.7 66.5 %shard_map.130.x_ref = bf16[256,7168]{1,0:T(8,128)(2,1)} custom-call(bf16[256,896]{1,0:T(8,128)(2,1)} %x_ref.1), custom_call_target="tpu_custom_call" | custom-call | tf_op jit(solution)/shard_map/pallas_call | solution.py:322
  83.3 0.5 fusion.1
  83.9 0.8 pad_maximum_fusion
  84.7 10.4 %shard_map.131 = (bf16[2,128,512]{2,1,0:T(8,128)(2,1)}, bf16[256,128]{1,0:T(8,128)(2,1)}, bf16[256,128]{1,0:T(8,128)(2,1)}, bf16[2,256,128]{2,1,0:T(8,128)(2,1)}) custom-call(bf16[256,7168]{1,0:T(8,128)(2,1)} %shard_map.130.x_ref, bf16[1,7168]{1,0:T(2,128)(2,1)} %reshape.253.g_ref, bf16[7168,512]{1,0:T(8,128)(2,1)} %wq_ref.1, bf16[7168,128]{1,0:T(8,128)(2,1)} %wk_ref.1, ...), custom_call_target="tpu_custom_call" | custom-call | tf_op jit(solution)/shard_map/pallas_call | solution.py:370
  95.2 41.0 %shard_map.132 = bf16[2,4,4,2,256,128]{5,4,3,2,1,0:T(8,128)(2,1)} custom-call(bf16[2,256,128]{2,1,0:T(8,128)(2,1)} %get-tuple-element.8.x_ref), custom_call_target="tpu_custom_call" | custom-call | tf_op jit(solution)/shard_map/pallas_call | solution.py:205
  136.4 0.1 select_reduce_fusion.3.page_order
  136.5 0.1 bitcast_reduce_fusion.1
  136.6 0.2 convert_reduce_fusion.3
  136.9 0.1 select_reduce_fusion.2.s_idx
  137.1 2.2 %copy-done = bf16[8192,256]{1,0:T(8,128)(2,1)S(1)} copy-done((bf16[8192,256]{1,0:T(8,128)(2,1)S(1)}, bf16[8192,256]{1,0:T(8,128)(2,1)}, u32[]{:S(2)}) %copy-start) | copy-done | bytes 4194328
  139.3 26.1 %shard_map.133 = bf16[2,128,512]{2,1,0:T(8,128)(2,1)} custom-call(s32[2,4]{1,0:T(2,128)S(1)} %convert_element_type.19.wants, s32[4,16]{1,0:T(4,128)S(1)} %select_reduce_fusion.3.page_order, s32[2,64]{1,0:T(2,128)S(1)} %select_reduce_fusion.2.s_idx, s32[2]{0:T(128)S(1)} %get-tuple-element.17.s_cnt, bf16[2,128,512]{2,1,0:T(8,128)(2,1)S(1)} %copy-done.1, ...), custom_call_target="tpu_custom_call" | custom-call | tf_op jit(solution)/shard_map/pallas_call | solution.py:497
  (24 shorter events, 0.6 us)
Async XLA Ops:
  7.2 129.9 %all-gather.2.cloned.1.call-start = ((), (), s32[]{:S(2)}) async-start(), calls=%async_computation | async-start | bytes 4325376 | tf_op jit(solution)/shard_map/all_gather | solution.py:531
  95.2 41.1 %copy-start.3 = (s32[64]{0:T(128)S(1)}, s32[64]{0:T(128)}, u32[]{:S(2)}) copy-start(s32[64]{0:T(128)} %param.18) | copy-start | bytes 772
  95.2 41.4 %copy-start.2 = (s32[8192]{0:T(1024)S(1)}, s32[8192]{0:T(1024)}, u32[]{:S(2)}) copy-start(s32[8192]{0:T(1024)} %param.21) | copy-start | bytes 98308
  95.2 41.9 %copy-start.1 = (bf16[2,128,512]{2,1,0:T(8,128)(2,1)S(1)}, bf16[2,128,512]{2,1,0:T(8,128)(2,1)}, u32[]{:S(2)}) copy-start(bf16[2,128,512]{2,1,0:T(8,128)(2,1)} %get-tuple-element.7.q_ref) | copy-start | bytes 786436
  137.1 2.2 %copy-start = (bf16[8192,256]{1,0:T(8,128)(2,1)S(1)}, bf16[8192,256]{1,0:T(8,128)(2,1)}, u32[]{:S(2)}) copy-start(bf16[8192,256]{1,0:T(8,128)(2,1)} %all-gather.2.cloned.1.call-done) | copy-start | bytes 12582916
Sparse Core Ops, SparseCore 0:
  9.9 77.6 all-gather.1

commit v12 on v11

--- a/solution.py
+++ b/solution.py
@@ -258,6 +258,20 @@
         device_id_type=mesh_id,
     )
     to_partner.start()
+
+    def ring(src, h, group, target, side):
+        return pltpu.make_async_remote_copy(
+            src_ref=src,
+            dst_ref=o_ref.at[:, cols(group, h)],
+            send_sem=r_send.at[side, h],
+            recv_sem=r_recv.at[side, h],
+            device_id={"tp": target * 2 + zh},
+            device_id_type=mesh_id,
+        )
+
+    outgoing = [ring(x_ref, zh, yy, right, 0), ring(x_ref, zh, yy, left, 1)]
+    for copy in outgoing:
+        copy.start()
     pltpu.make_async_remote_copy(
         src_ref=x_ref,
         dst_ref=o_ref.at[:, cols(yy, 1 - zh)],
@@ -266,33 +280,19 @@
         device_id={"tp": yy * 2 + 1 - zh},
         device_id_type=mesh_id,
     ).wait_recv()
+    partner_src = o_ref.at[:, cols(yy, 1 - zh)]
+    later = [ring(partner_src, 1 - zh, yy, right, 0), ring(partner_src, 1 - zh, yy, left, 1)]
+    for copy in later:
+        copy.start()
     local.wait()
     to_partner.wait_send()
-
-    pieces = r_send.shape[1]
+    for h in range(2):
+        ring(x_ref, h, left, right, 0).wait_recv()
+        ring(x_ref, h, right, left, 1).wait_recv()
+    for copy in outgoing + later:
+        copy.wait_send()
+    pieces = f_send.shape[1]
     span = x_ref.shape[0] // pieces
-
-    def ring(group, target, side, c):
-        rows = pl.ds(c * span, span)
-        return pltpu.make_async_remote_copy(
-            src_ref=o_ref.at[rows, pair(group)],
-            dst_ref=o_ref.at[rows, pair(group)],
-            send_sem=r_send.at[side, c],
-            recv_sem=r_recv.at[side, c],
-            device_id={"tp": target * 2 + zh},
-            device_id_type=mesh_id,
-        )
-
-    outgoing = []
-    for c in range(pieces):
-        outgoing += [ring(yy, right, 0, c), ring(yy, left, 1, c)]
-    for copy in outgoing:
-        copy.start()
-    for c in range(pieces):
-        ring(left, right, 0, c).wait_recv()
-        ring(right, left, 1, c).wait_recv()
-    for copy in outgoing:
-        copy.wait_send()
 
     def relay(group, h, target, side, c):
         rows = pl.ds(c * span, span)
@@ -327,8 +327,8 @@
         scratch_shapes=[
             pltpu.SemaphoreType.DMA,
             pltpu.SemaphoreType.DMA,
-            pltpu.SemaphoreType.DMA((2, 4)),
-            pltpu.SemaphoreType.DMA((2, 4)),
+            pltpu.SemaphoreType.DMA((2, 2)),
+            pltpu.SemaphoreType.DMA((2, 2)),
             pltpu.SemaphoreType.DMA((2, 4)),
             pltpu.SemaphoreType.DMA((2, 4)),
             pltpu.SemaphoreType.DMA,

time: 173 us -> 163 us (0.942)
  the two profiles are of different devices: /device:TPU:161 before, /device:TPU:196 now
where the time goes in v12:
time: 163 us
  Pallas kernels  135 us (83%)
  between operations  14.2 us (9%)
  other arithmetic  8.56 us (5%)
  local copies, waits for them, and re-layouts  5.31 us (3%)
    pallas_call x1, Pallas kernels, tp_gather(): pl.pallas_call(functools.partial(tp_gather_kernel, n // 2), out_shape=jax...  49.8 us
    pallas_call x1, Pallas kernels, seq_gather(): pl.pallas_call(functools.partial(seq_gather_kernel, zs, xs), out_shape=ja...  44.2 us
    pallas_call x1, Pallas kernels, block_attention(): pl.pallas_call(functools.partial(attention_kernel, scale, 4), out_shape=j...  30.3 us
    pallas_call x1, Pallas kernels, project(): pl.pallas_call(project_kernel, grid=(steps,), out_shape=(jax.ShapeDtypeSt...  10.6 us
  transfers between devices with their start and end apart: 1, of which 0 were waited for; matrix products, arithmetic and copies ran while one was open for 6% of the time, Pallas kernels for 64%

profile of v12, /device:TPU:196, one launch (start us, length us, event | category | flops | bytes accessed | tf_op | source)
XLA Modules:
  0.0 162.9 jit_solution(6400795273449585090)
XLA Ops:
  7.2 1.5 pad_maximum_fusion.2
  8.8 0.7 copy.19
  9.6 0.1 reduce
  9.7 0.7 sub.9
  10.4 1.3 reshape.253.g_ref
  11.7 1.0 convert_reduce_fusion
  12.7 1.0 select_reduce_fusion
  13.7 0.8 sub.10
  14.6 0.1 fusion.2
  14.7 0.9 bitcast_reduce_fusion.2
  15.6 0.3 reshape.263.q_pos
  16.0 0.3 reshape.262.q_req
  16.4 0.3 reshape.261.q_want
  16.7 49.8 %shard_map.130.x_ref = bf16[256,7168]{1,0:T(8,128)(2,1)} custom-call(bf16[256,896]{1,0:T(8,128)(2,1)} %x_ref.1), custom_call_target="tpu_custom_call" | custom-call | tf_op jit(solution)/shard_map/pallas_call | solution.py:322
  66.6 0.5 fusion.1
  67.2 0.8 pad_maximum_fusion
  68.0 10.6 %shard_map.131 = (bf16[2,128,512]{2,1,0:T(8,128)(2,1)}, bf16[256,128]{1,0:T(8,128)(2,1)}, bf16[256,128]{1,0:T(8,128)(2,1)}, bf16[2,256,128]{2,1,0:T(8,128)(2,1)}) custom-call(bf16[256,7168]{1,0:T(8,128)(2,1)} %shard_map.130.x_ref, bf16[1,7168]{1,0:T(2,128)(2,1)} %reshape.253.g_ref, bf16[7168,512]{1,0:T(8,128)(2,1)} %wq_ref.1, bf16[7168,128]{1,0:T(8,128)(2,1)} %wk_ref.1, ...), custom_call_target="tpu_custom_call" | custom-call | tf_op jit(solution)/shard_map/pallas_call | solution.py:370
  78.6 44.2 %shard_map.132 = bf16[2,4,4,2,256,128]{5,4,3,2,1,0:T(8,128)(2,1)} custom-call(bf16[2,256,128]{2,1,0:T(8,128)(2,1)} %get-tuple-element.8.x_ref), custom_call_target="tpu_custom_call" | custom-call | tf_op jit(solution)/shard_map/pallas_call | solution.py:205
  122.9 0.1 select_reduce_fusion.3.page_order
  123.1 0.1 bitcast_reduce_fusion.1
  123.2 0.2 convert_reduce_fusion.3
  123.5 0.1 select_reduce_fusion.2.s_idx
  123.7 2.2 %copy-done = bf16[8192,256]{1,0:T(8,128)(2,1)S(1)} copy-done((bf16[8192,256]{1,0:T(8,128)(2,1)S(1)}, bf16[8192,256]{1,0:T(8,128)(2,1)}, u32[]{:S(2)}) %copy-start) | copy-done | bytes 4194328
  125.8 30.3 %shard_map.133 = bf16[2,128,512]{2,1,0:T(8,128)(2,1)} custom-call(s32[2,4]{1,0:T(2,128)S(1)} %convert_element_type.19.wants, s32[4,16]{1,0:T(4,128)S(1)} %select_reduce_fusion.3.page_order, s32[2,64]{1,0:T(2,128)S(1)} %select_reduce_fusion.2.s_idx, s32[2]{0:T(128)S(1)} %get-tuple-element.17.s_cnt, bf16[2,128,512]{2,1,0:T(8,128)(2,1)S(1)} %copy-done.1, ...), custom_call_target="tpu_custom_call" | custom-call | tf_op jit(solution)/shard_map/pallas_call | solution.py:497
  (24 shorter events, 0.6 us)
Async XLA Ops:
  7.2 116.5 %all-gather.2.cloned.1.call-start = ((), (), s32[]{:S(2)}) async-start(), calls=%async_computation | async-start | bytes 4325376 | tf_op jit(solution)/shard_map/all_gather | solution.py:531
  78.6 44.2 %copy-start.3 = (s32[64]{0:T(128)S(1)}, s32[64]{0:T(128)}, u32[]{:S(2)}) copy-start(s32[64]{0:T(128)} %param.18) | copy-start | bytes 772
  78.6 44.5 %copy-start.2 = (s32[8192]{0:T(1024)S(1)}, s32[8192]{0:T(1024)}, u32[]{:S(2)}) copy-start(s32[8192]{0:T(1024)} %param.21) | copy-start | bytes 98308
  78.6 45.0 %copy-start.1 = (bf16[2,128,512]{2,1,0:T(8,128)(2,1)S(1)}, bf16[2,128,512]{2,1,0:T(8,128)(2,1)}, u32[]{:S(2)}) copy-start(bf16[2,128,512]{2,1,0:T(8,128)(2,1)} %get-tuple-element.7.q_ref) | copy-start | bytes 786436
  123.6 2.2 %copy-start = (bf16[8192,256]{1,0:T(8,128)(2,1)S(1)}, bf16[8192,256]{1,0:T(8,128)(2,1)}, u32[]{:S(2)}) copy-start(bf16[8192,256]{1,0:T(8,128)(2,1)} %all-gather.2.cloned.1.call-done) | copy-start | bytes 12582916
Sparse Core Ops, SparseCore 0:
  9.9 76.6 all-gather.1

commit v13 on v12

--- a/solution.py
+++ b/solution.py
@@ -89,6 +89,16 @@
             device_id_type=mesh_id,
         )
 
+    def ring_slot(a, slot, side, group, target_x, sem_side, src=None):
+        return pltpu.make_async_remote_copy(
+            src_ref=o_ref.at[a, slot, group, core] if src is None else src,
+            dst_ref=o_ref.at[a, slot, group, core],
+            send_sem=r_send.at[a, side, slot],
+            recv_sem=r_recv.at[a, sem_side, slot],
+            device_id={"seq": seq_of(za, target_x, core)},
+            device_id_type=mesh_id,
+        )
+
     def z_start(k, carry):
         peer_z = lax.rem(za + k, zs)
         for a in range(parts):
@@ -96,13 +106,18 @@
         return carry
 
     lax.fori_loop(1, zs, z_start, 0)
+    for a in range(parts):
+        ring_slot(a, za, 0, xb, right, 0, x_ref.at[a]).start()
+        ring_slot(a, za, 1, xb, left, 1, x_ref.at[a]).start()
 
     def z_finish(k, carry):
         peer_z = lax.rem(za + k, zs)
         for a in range(parts):
             copy = z_copy(a, peer_z, peer_z)
+            copy.wait_recv()
+            ring_slot(a, peer_z, 0, xb, right, 0).start()
+            ring_slot(a, peer_z, 1, xb, left, 1).start()
             copy.wait_send()
-            copy.wait_recv()
         return carry
 
     lax.fori_loop(1, zs, z_finish, 0)
@@ -123,31 +138,18 @@
         across.append(hand(a, xb, core))
         across[-1].start()
 
-    def ring_copy(a, side, group, target_x, sem_side):
-        return pltpu.make_async_remote_copy(
-            src_ref=o_ref.at[a, :, group, core],
-            dst_ref=o_ref.at[a, :, group, core],
-            send_sem=r_send.at[a, side],
-            recv_sem=r_recv.at[a, sem_side],
-            device_id={"seq": seq_of(za, target_x, core)},
-            device_id_type=mesh_id,
-        )
-
-    outgoing = []
     for a in range(parts):
-        outgoing.append(ring_copy(a, 0, xb, right, 0))
-        outgoing.append(ring_copy(a, 1, xb, left, 1))
-    for copy in outgoing:
-        copy.start()
-    for a in range(parts):
-        ring_copy(a, 0, left, right, 0).wait_recv()
-        ring_copy(a, 1, right, left, 1).wait_recv()
+        for slot in range(zs):
+            ring_slot(a, slot, 0, left, right, 0).wait_recv()
+            ring_slot(a, slot, 1, right, left, 1).wait_recv()
     for a in range(parts):
         for group in (left, right):
             across.append(hand(a, group, core))
             across[-1].start()
-    for copy in outgoing:
-        copy.wait_send()
+    for a in range(parts):
+        for slot in range(zs):
+            ring_slot(a, slot, 0, xb, right, 0).wait_send()
+            ring_slot(a, slot, 1, xb, left, 1).wait_send()
 
     far = lax.rem(xb + 2, xs)
     relay_k = pltpu.make_async_remote_copy(
@@ -210,8 +212,8 @@
         scratch_shapes=[
             pltpu.SemaphoreType.DMA((parts, zs)),
             pltpu.SemaphoreType.DMA((parts, zs)),
-            pltpu.SemaphoreType.DMA((parts, 2)),
-            pltpu.SemaphoreType.DMA((parts, 2)),
+            pltpu.SemaphoreType.DMA((parts, 2, zs)),
+            pltpu.SemaphoreType.DMA((parts, 2, zs)),
             pltpu.SemaphoreType.DMA((parts,)),
             pltpu.SemaphoreType.DMA((parts,)),
             pltpu.SemaphoreType.DMA((parts, xs)),

time: 163 us -> 156 us (0.957)
  the two profiles are of different devices: /device:TPU:196 before, /device:TPU:128 now
where the time goes in v13:
time: 156 us
  Pallas kernels  128 us (82%)
  between operations  14.2 us (9%)
  other arithmetic  8.56 us (5%)
  local copies, waits for them, and re-layouts  5.31 us (3%)
    pallas_call x1, Pallas kernels, tp_gather(): pl.pallas_call(functools.partial(tp_gather_kernel, n // 2), out_shape=jax...  61 us
    pallas_call x1, Pallas kernels, seq_gather(): pl.pallas_call(functools.partial(seq_gather_kernel, zs, xs), out_shape=ja...  29 us
    pallas_call x1, Pallas kernels, block_attention(): pl.pallas_call(functools.partial(attention_kernel, scale, 4), out_shape=j...  27.1 us
    pallas_call x1, Pallas kernels, project(): pl.pallas_call(project_kernel, grid=(steps,), out_shape=(jax.ShapeDtypeSt...  10.6 us
  transfers between devices with their start and end apart: 1, of which 0 were waited for; matrix products, arithmetic and copies ran while one was open for 6% of the time, Pallas kernels for 65%

profile of v13, /device:TPU:128, one launch (start us, length us, event | category | flops | bytes accessed | tf_op | source)
XLA Modules:
  0.0 155.8 jit_solution(9072473665954895317)
XLA Ops:
  7.2 1.5 pad_maximum_fusion.2
  8.8 0.7 copy.19
  9.6 0.1 reduce
  9.7 0.7 sub.9
  10.4 1.3 reshape.253.g_ref
  11.7 1.0 convert_reduce_fusion
  12.7 1.0 select_reduce_fusion
  13.7 0.8 sub.10
  14.6 0.1 fusion.2
  14.7 0.9 bitcast_reduce_fusion.2
  15.6 0.3 reshape.263.q_pos
  16.0 0.3 reshape.262.q_req
  16.4 0.3 reshape.261.q_want
  16.7 61.0 %shard_map.130.x_ref = bf16[256,7168]{1,0:T(8,128)(2,1)} custom-call(bf16[256,896]{1,0:T(8,128)(2,1)} %x_ref.1), custom_call_target="tpu_custom_call" | custom-call | tf_op jit(solution)/shard_map/pallas_call | solution.py:324
  77.8 0.5 fusion.1
  78.3 0.8 pad_maximum_fusion
  79.2 10.6 %shard_map.131 = (bf16[2,128,512]{2,1,0:T(8,128)(2,1)}, bf16[256,128]{1,0:T(8,128)(2,1)}, bf16[256,128]{1,0:T(8,128)(2,1)}, bf16[2,256,128]{2,1,0:T(8,128)(2,1)}) custom-call(bf16[256,7168]{1,0:T(8,128)(2,1)} %shard_map.130.x_ref, bf16[1,7168]{1,0:T(2,128)(2,1)} %reshape.253.g_ref, bf16[7168,512]{1,0:T(8,128)(2,1)} %wq_ref.1, bf16[7168,128]{1,0:T(8,128)(2,1)} %wk_ref.1, ...), custom_call_target="tpu_custom_call" | custom-call | tf_op jit(solution)/shard_map/pallas_call | solution.py:372
  89.8 29.0 %shard_map.132 = bf16[2,4,4,2,256,128]{5,4,3,2,1,0:T(8,128)(2,1)} custom-call(bf16[2,256,128]{2,1,0:T(8,128)(2,1)} %get-tuple-element.8.x_ref), custom_call_target="tpu_custom_call" | custom-call | tf_op jit(solution)/shard_map/pallas_call | solution.py:207
  118.9 0.1 select_reduce_fusion.3.page_order
  119.1 0.1 bitcast_reduce_fusion.1
  119.2 0.2 convert_reduce_fusion.3
  119.5 0.1 select_reduce_fusion.2.s_idx
  119.7 2.2 %copy-done = bf16[8192,256]{1,0:T(8,128)(2,1)S(1)} copy-done((bf16[8192,256]{1,0:T(8,128)(2,1)S(1)}, bf16[8192,256]{1,0:T(8,128)(2,1)}, u32[]{:S(2)}) %copy-start) | copy-done | bytes 4194328
  121.8 27.1 %shard_map.133 = bf16[2,128,512]{2,1,0:T(8,128)(2,1)} custom-call(s32[2,4]{1,0:T(2,128)S(1)} %convert_element_type.19.wants, s32[4,16]{1,0:T(4,128)S(1)} %select_reduce_fusion.3.page_order, s32[2,64]{1,0:T(2,128)S(1)} %select_reduce_fusion.2.s_idx, s32[2]{0:T(128)S(1)} %get-tuple-element.17.s_cnt, bf16[2,128,512]{2,1,0:T(8,128)(2,1)S(1)} %copy-done.1, ...), custom_call_target="tpu_custom_call" | custom-call | tf_op jit(solution)/shard_map/pallas_call | solution.py:499
  (24 shorter events, 0.6 us)
Async XLA Ops:
  7.2 112.5 %all-gather.2.cloned.1.call-start = ((), (), s32[]{:S(2)}) async-start(), calls=%async_computation | async-start | bytes 4325376 | tf_op jit(solution)/shard_map/all_gather | solution.py:533
  89.8 29.0 %copy-start.3 = (s32[64]{0:T(128)S(1)}, s32[64]{0:T(128)}, u32[]{:S(2)}) copy-start(s32[64]{0:T(128)} %param.18) | copy-start | bytes 772
  89.8 29.3 %copy-start.2 = (s32[8192]{0:T(1024)S(1)}, s32[8192]{0:T(1024)}, u32[]{:S(2)}) copy-start(s32[8192]{0:T(1024)} %param.21) | copy-start | bytes 98308
  89.8 29.9 %copy-start.1 = (bf16[2,128,512]{2,1,0:T(8,128)(2,1)S(1)}, bf16[2,128,512]{2,1,0:T(8,128)(2,1)}, u32[]{:S(2)}) copy-start(bf16[2,128,512]{2,1,0:T(8,128)(2,1)} %get-tuple-element.7.q_ref) | copy-start | bytes 786436
  119.7 2.2 %copy-start = (bf16[8192,256]{1,0:T(8,128)(2,1)S(1)}, bf16[8192,256]{1,0:T(8,128)(2,1)}, u32[]{:S(2)}) copy-start(bf16[8192,256]{1,0:T(8,128)(2,1)} %all-gather.2.cloned.1.call-done) | copy-start | bytes 12582916
Sparse Core Ops, SparseCore 0:
  9.9 77.5 all-gather.1

commit v14 on v13

--- a/solution.py
+++ b/solution.py
@@ -138,10 +138,26 @@
         across.append(hand(a, xb, core))
         across[-1].start()
 
-    for a in range(parts):
-        for slot in range(zs):
-            ring_slot(a, slot, 0, left, right, 0).wait_recv()
-            ring_slot(a, slot, 1, right, left, 1).wait_recv()
+    far = lax.rem(xb + 2, xs)
+
+    def relay(a, slot, group, target_x, src_group):
+        return pltpu.make_async_remote_copy(
+            src_ref=o_ref.at[a, slot, src_group, core],
+            dst_ref=o_ref.at[a, slot, group, core],
+            send_sem=f_send.at[a, slot],
+            recv_sem=f_recv.at[a, slot],
+            device_id={"seq": seq_of(za, target_x, core)},
+            device_id_type=mesh_id,
+        )
+
+    for slot in range(zs):
+        ring_slot(0, slot, 0, left, right, 0).wait_recv()
+        relay(0, slot, left, right, left).start()
+        ring_slot(1, slot, 1, right, left, 1).wait_recv()
+        relay(1, slot, right, left, right).start()
+    for slot in range(zs):
+        ring_slot(1, slot, 0, left, right, 0).wait_recv()
+        ring_slot(0, slot, 1, right, left, 1).wait_recv()
     for a in range(parts):
         for group in (left, right):
             across.append(hand(a, group, core))
@@ -150,44 +166,12 @@
         for slot in range(zs):
             ring_slot(a, slot, 0, xb, right, 0).wait_send()
             ring_slot(a, slot, 1, xb, left, 1).wait_send()
-
-    far = lax.rem(xb + 2, xs)
-    relay_k = pltpu.make_async_remote_copy(
-        src_ref=o_ref.at[0, :, left, core],
-        dst_ref=o_ref.at[0, :, left, core],
-        send_sem=f_send.at[0],
-        recv_sem=f_recv.at[0],
-        device_id={"seq": seq_of(za, right, core)},
-        device_id_type=mesh_id,
-    )
-    relay_v = pltpu.make_async_remote_copy(
-        src_ref=o_ref.at[1, :, right, core],
-        dst_ref=o_ref.at[1, :, right, core],
-        send_sem=f_send.at[1],
-        recv_sem=f_recv.at[1],
-        device_id={"seq": seq_of(za, left, core)},
-        device_id_type=mesh_id,
-    )
-    relay_k.start()
-    relay_v.start()
-    pltpu.make_async_remote_copy(
-        src_ref=o_ref.at[0, :, far, core],
-        dst_ref=o_ref.at[0, :, far, core],
-        send_sem=f_send.at[0],
-        recv_sem=f_recv.at[0],
-        device_id={"seq": seq_of(za, right, core)},
-        device_id_type=mesh_id,
-    ).wait_recv()
-    pltpu.make_async_remote_copy(
-        src_ref=o_ref.at[1, :, far, core],
-        dst_ref=o_ref.at[1, :, far, core],
-        send_sem=f_send.at[1],
-        recv_sem=f_recv.at[1],
-        device_id={"seq": seq_of(za, left, core)},
-        device_id_type=mesh_id,
-    ).wait_recv()
-    relay_k.wait_send()
-    relay_v.wait_send()
+    for slot in range(zs):
+        relay(0, slot, far, right, left).wait_recv()
+        relay(1, slot, far, left, right).wait_recv()
+    for slot in range(zs):
+        relay(0, slot, left, right, left).wait_send()
+        relay(1, slot, right, left, right).wait_send()
     for a in range(parts):
         across.append(hand(a, far, core))
         across[-1].start()
@@ -214,8 +198,8 @@
             pltpu.SemaphoreType.DMA((parts, zs)),
             pltpu.SemaphoreType.DMA((parts, 2, zs)),
             pltpu.SemaphoreType.DMA((parts, 2, zs)),
-            pltpu.SemaphoreType.DMA((parts,)),
-            pltpu.SemaphoreType.DMA((parts,)),
+            pltpu.SemaphoreType.DMA((parts, zs)),
+            pltpu.SemaphoreType.DMA((parts, zs)),
             pltpu.SemaphoreType.DMA((parts, xs)),
             pltpu.SemaphoreType.DMA((parts, xs)),
             pltpu.SemaphoreType.DMA,
@@ -288,11 +272,6 @@
         copy.start()
     local.wait()
     to_partner.wait_send()
-    for h in range(2):
-        ring(x_ref, h, left, right, 0).wait_recv()
-        ring(x_ref, h, right, left, 1).wait_recv()
-    for copy in outgoing + later:
-        copy.wait_send()
     pieces = f_send.shape[1]
     span = x_ref.shape[0] // pieces
 
@@ -308,10 +287,18 @@
         )
 
     relays = []
+    ring(x_ref, 0, left, right, 0).wait_recv()
     for c in range(pieces):
-        relays += [relay(left, 0, right, 0, c), relay(right, 1, left, 1, c)]
-    for copy in relays:
-        copy.start()
+        relays.append(relay(left, 0, right, 0, c))
+        relays[-1].start()
+    ring(x_ref, 1, right, left, 1).wait_recv()
+    for c in range(pieces):
+        relays.append(relay(right, 1, left, 1, c))
+        relays[-1].start()
+    ring(x_ref, 1, left, right, 0).wait_recv()
+    ring(x_ref, 0, right, left, 1).wait_recv()
+    for copy in outgoing + later:
+        copy.wait_send()
     for c in range(pieces):
         relay(far, 0, right, 0, c).wait_recv()
         relay(far, 1, left, 1, c).wait_recv()

time: 156 us -> 162 us (1.038)
  the two profiles are of different devices: /device:TPU:128 before, /device:TPU:165 now
where the time goes in v14:
time: 162 us; the launch traced here: 161 us
  Pallas kernels  133 us (82%)
  between operations  14.2 us (9%)
  other arithmetic  8.56 us (5%)
  local copies, waits for them, and re-layouts  5.31 us (3%)
    pallas_call x1, Pallas kernels, tp_gather(): pl.pallas_call(functools.partial(tp_gather_kernel, n // 2), out_shape=jax...  47.6 us
    pallas_call x1, Pallas kernels, seq_gather(): pl.pallas_call(functools.partial(seq_gather_kernel, zs, xs), out_shape=ja...  46.2 us
    pallas_call x1, Pallas kernels, block_attention(): pl.pallas_call(functools.partial(attention_kernel, scale, 4), out_shape=j...  28.7 us
    pallas_call x1, Pallas kernels, project(): pl.pallas_call(project_kernel, grid=(steps,), out_shape=(jax.ShapeDtypeSt...  10.5 us
  transfers between devices with their start and end apart: 1, of which 0 were waited for; matrix products, arithmetic and copies ran while one was open for 6% of the time, Pallas kernels for 65%

profile of v14, /device:TPU:165, one launch (start us, length us, event | category | flops | bytes accessed | tf_op | source)
XLA Modules:
  0.0 161.2 jit_solution(8276910145336824815)
XLA Ops:
  7.2 1.5 pad_maximum_fusion.2
  8.8 0.7 copy.19
  9.6 0.1 reduce
  9.7 0.7 sub.9
  10.4 1.3 reshape.253.g_ref
  11.7 1.0 convert_reduce_fusion
  12.7 1.0 select_reduce_fusion
  13.7 0.8 sub.10
  14.6 0.1 fusion.2
  14.7 0.9 bitcast_reduce_fusion.2
  15.6 0.3 reshape.263.q_pos
  16.0 0.3 reshape.262.q_req
  16.4 0.3 reshape.261.q_want
  16.7 47.6 %shard_map.130.x_ref = bf16[256,7168]{1,0:T(8,128)(2,1)} custom-call(bf16[256,896]{1,0:T(8,128)(2,1)} %x_ref.1), custom_call_target="tpu_custom_call" | custom-call | tf_op jit(solution)/shard_map/pallas_call | solution.py:311
  64.5 0.5 fusion.1
  65.0 0.8 pad_maximum_fusion
  65.8 10.5 %shard_map.131 = (bf16[2,128,512]{2,1,0:T(8,128)(2,1)}, bf16[256,128]{1,0:T(8,128)(2,1)}, bf16[256,128]{1,0:T(8,128)(2,1)}, bf16[2,256,128]{2,1,0:T(8,128)(2,1)}) custom-call(bf16[256,7168]{1,0:T(8,128)(2,1)} %shard_map.130.x_ref, bf16[1,7168]{1,0:T(2,128)(2,1)} %reshape.253.g_ref, bf16[7168,512]{1,0:T(8,128)(2,1)} %wq_ref.1, bf16[7168,128]{1,0:T(8,128)(2,1)} %wk_ref.1, ...), custom_call_target="tpu_custom_call" | custom-call | tf_op jit(solution)/shard_map/pallas_call | solution.py:359
  76.4 46.2 %shard_map.132 = bf16[2,4,4,2,256,128]{5,4,3,2,1,0:T(8,128)(2,1)} custom-call(bf16[2,256,128]{2,1,0:T(8,128)(2,1)} %get-tuple-element.8.x_ref), custom_call_target="tpu_custom_call" | custom-call | tf_op jit(solution)/shard_map/pallas_call | solution.py:191
  122.8 0.1 select_reduce_fusion.3.page_order
  122.9 0.1 bitcast_reduce_fusion.1
  123.1 0.2 convert_reduce_fusion.3
  123.3 0.1 select_reduce_fusion.2.s_idx
  123.5 2.2 %copy-done = bf16[8192,256]{1,0:T(8,128)(2,1)S(1)} copy-done((bf16[8192,256]{1,0:T(8,128)(2,1)S(1)}, bf16[8192,256]{1,0:T(8,128)(2,1)}, u32[]{:S(2)}) %copy-start) | copy-done | bytes 4194328
  125.7 28.7 %shard_map.133 = bf16[2,128,512]{2,1,0:T(8,128)(2,1)} custom-call(s32[2,4]{1,0:T(2,128)S(1)} %convert_element_type.19.wants, s32[4,16]{1,0:T(4,128)S(1)} %select_reduce_fusion.3.page_order, s32[2,64]{1,0:T(2,128)S(1)} %select_reduce_fusion.2.s_idx, s32[2]{0:T(128)S(1)} %get-tuple-element.17.s_cnt, bf16[2,128,512]{2,1,0:T(8,128)(2,1)S(1)} %copy-done.1, ...), custom_call_target="tpu_custom_call" | custom-call | tf_op jit(solution)/shard_map/pallas_call | solution.py:486
  (24 shorter events, 0.6 us)
Async XLA Ops:
  7.2 116.3 %all-gather.2.cloned.1.call-start = ((), (), s32[]{:S(2)}) async-start(), calls=%async_computation | async-start | bytes 4325376 | tf_op jit(solution)/shard_map/all_gather | solution.py:520
  76.4 46.3 %copy-start.3 = (s32[64]{0:T(128)S(1)}, s32[64]{0:T(128)}, u32[]{:S(2)}) copy-start(s32[64]{0:T(128)} %param.18) | copy-start | bytes 772
  76.4 46.5 %copy-start.2 = (s32[8192]{0:T(1024)S(1)}, s32[8192]{0:T(1024)}, u32[]{:S(2)}) copy-start(s32[8192]{0:T(1024)} %param.21) | copy-start | bytes 98308
  76.4 47.1 %copy-start.1 = (bf16[2,128,512]{2,1,0:T(8,128)(2,1)S(1)}, bf16[2,128,512]{2,1,0:T(8,128)(2,1)}, u32[]{:S(2)}) copy-start(bf16[2,128,512]{2,1,0:T(8,128)(2,1)} %get-tuple-element.7.q_ref) | copy-start | bytes 786436
  123.5 2.2 %copy-start = (bf16[8192,256]{1,0:T(8,128)(2,1)S(1)}, bf16[8192,256]{1,0:T(8,128)(2,1)}, u32[]{:S(2)}) copy-start(bf16[8192,256]{1,0:T(8,128)(2,1)} %all-gather.2.cloned.1.call-done) | copy-start | bytes 12582916
Sparse Core Ops, SparseCore 0:
  9.9 76.6 all-gather.1

commit v15 on v14

--- a/solution.py
+++ b/solution.py
@@ -517,9 +517,15 @@
     suffix_lengths,
     row_order,
 ):
-    gathered_prefix = lax.all_gather(
-        jnp.concatenate([prefix_keys, prefix_values], axis=1), "seq", axis=0, tiled=True
-    )
+    own_pages = jnp.concatenate([prefix_keys, prefix_values], axis=1)
+    chips = seq_n // 2
+    same_core = [own_pages] + [
+        lax.ppermute(own_pages, "seq", [(i, (i + 2 * k) % seq_n) for i in range(seq_n)])
+        for k in range(1, chips)
+    ]
+    mine = jnp.stack(same_core)
+    theirs = lax.ppermute(mine, "seq", [(i, i ^ 1) for i in range(seq_n)])
+    gathered_prefix = jnp.concatenate([mine, theirs], axis=0)
     gathered = tp_gather(hidden, tp_n, 2)
     local_rows = gathered.shape[0]
     request_all, position_all, wanted_all = locate(row_order, suffix_lengths, request_prefix)
@@ -565,6 +571,12 @@
         page_rank[None, None, :] == jnp.arange(per_prefix, dtype=jnp.int32)[None, :, None]
     )
     page_order = jnp.sum(jnp.where(pick, page_ids[None, None, :], 0), axis=2).astype(jnp.int32)
+    me_seq = lax.axis_index("seq")
+    page_device = page_order // 2
+    same = (page_device % 2) == (me_seq % 2)
+    holder = jnp.where(same, me_seq, me_seq ^ 1)
+    slot = jnp.where(same, 0, seq_n // 2) + ((holder - page_device) % seq_n) // 2
+    page_order = (slot * 2 + page_order % 2).astype(jnp.int32)
     local_place = lax.dynamic_slice_in_dim(row_order, offset, local_rows).reshape(q_blocks, block)
     first_seen = jnp.min(local_place - position.reshape(q_blocks, block), axis=1)
     last_seen = jnp.max(local_place, axis=1)

time: 162 us -> 198 us (1.22)
  the two profiles are of different devices: /device:TPU:165 before, /device:TPU:55 now
where the time goes in v15:
time: 198 us; the launch traced here: 197 us
  Pallas kernels  124 us (63%)
  waiting for transfers between devices  24 us (12%)
  starting transfers between devices  22.7 us (11%)
  local copies, waits for them, and re-layouts  19 us (10%)
  other arithmetic  6.35 us (3%)
    pallas_call x1, Pallas kernels, tp_gather(): pl.pallas_call(functools.partial(tp_gather_kernel, n // 2), out_shape=jax...  47.8 us
    pallas_call x1, Pallas kernels, seq_gather(): pl.pallas_call(functools.partial(seq_gather_kernel, zs, xs), out_shape=ja...  37 us
    pallas_call x1, Pallas kernels, block_attention(): pl.pallas_call(functools.partial(attention_kernel, scale, 4), out_shape=j...  29.1 us
    ppermute x15, waiting for transfers between devices, body(): lax.ppermute(own_pages, 'seq', [(i, (i + 2 * k) % seq_n) for i in range(s...  22.3 us
    ppermute x15, starting transfers between devices, body(): lax.ppermute(own_pages, 'seq', [(i, (i + 2 * k) % seq_n) for i in range(s...  21.8 us
    unnamed x24, local copies, waits for them, and re-layouts  11.9 us
    pallas_call x1, Pallas kernels, project(): pl.pallas_call(project_kernel, grid=(steps,), out_shape=(jax.ShapeDtypeSt...  10.5 us
  transfers between devices with their start and end apart: 16, of which 6 were waited for; matrix products, arithmetic and copies ran while one was open for 10% of the time, Pallas kernels for 48%

profile of v15, /device:TPU:55, one launch (start us, length us, event | category | flops | bytes accessed | tf_op | source)
XLA Modules:
  0.0 197.2 jit_solution(6666607909197198161)
XLA Ops:
  0.6 0.9 constant_dynamic-update-slice_fusion.1
  1.5 0.9 constant_dynamic-update-slice_fusion
  2.4 1.6 collective-permute-start
  4.0 2.1 %collective-permute-start.1 = (bf16[256,256]{1,0:T(8,128)(2,1)S(1)}, bf16[256,256]{1,0:T(8,128)(2,1)S(1)}, u32[]{:S(2)}, u32[]{:S(2)}) collective-permute-start(bf16[256,256]{1,0:T(8,128)(2,1)S(1)} %constant_dynamic-update-slice_fusion), channel_id=1, source_target_pairs={{0,32},{8,40},{16,48},{24,56},{32,64},{40,72},{48,80},{56,88},{64,... | collective-permute-start | bytes 393224 | tf_op jit(solution)/shard_map/ppermute | solution.py:523
  6.1 1.0 collective-permute-start.2
  7.8 2.7 %collective-permute-start.4 = (bf16[256,256]{1,0:T(8,128)(2,1)S(1)}, bf16[256,256]{1,0:T(8,128)(2,1)S(1)}, u32[]{:S(2)}, u32[]{:S(2)}) collective-permute-start(bf16[256,256]{1,0:T(8,128)(2,1)S(1)} %constant_dynamic-update-slice_fusion), channel_id=1, source_target_pairs={{0,80},{8,88},{16,96},{24,104},{32,112},{40,120},{48,128},{56,136}... | collective-permute-start | bytes 393224 | tf_op jit(solution)/shard_map/ppermute | solution.py:523
  12.0 1.0 convert_reduce_fusion
  13.0 1.0 select_reduce_fusion
  14.8 47.8 %shard_map.130.x_ref = bf16[256,7168]{1,0:T(8,128)(2,1)} custom-call(bf16[256,896]{1,0:T(8,128)(2,1)} %x_ref.1), custom_call_target="tpu_custom_call" | custom-call | tf_op jit(solution)/shard_map/pallas_call | solution.py:311
  63.8 0.8 pad_maximum_fusion
  64.7 10.5 %shard_map.131 = (bf16[2,128,512]{2,1,0:T(8,128)(2,1)}, bf16[256,128]{1,0:T(8,128)(2,1)}, bf16[256,128]{1,0:T(8,128)(2,1)}, bf16[2,256,128]{2,1,0:T(8,128)(2,1)}) custom-call(bf16[256,7168]{1,0:T(8,128)(2,1)} %shard_map.130.x_ref, bf16[1,7168]{1,0:T(2,128)(2,1)} %reshape.253.g_ref, bf16[7168,512]{1,0:T(8,128)(2,1)} %wq_ref.1, bf16[7168,128]{1,0:T(8,128)(2,1)} %wk_ref.1, ...), custom_call_target="tpu_custom_call" | custom-call | tf_op jit(solution)/shard_map/pallas_call | solution.py:359
  75.1 37.0 %shard_map.132 = bf16[2,4,4,2,256,128]{5,4,3,2,1,0:T(8,128)(2,1)} custom-call(bf16[2,256,128]{2,1,0:T(8,128)(2,1)} %get-tuple-element.8.x_ref), custom_call_target="tpu_custom_call" | custom-call | tf_op jit(solution)/shard_map/pallas_call | solution.py:191
  113.6 4.6 %collective-permute-start.6 = (bf16[256,256]{1,0:T(8,128)(2,1)S(1)}, bf16[256,256]{1,0:T(8,128)(2,1)S(1)}, u32[]{:S(2)}, u32[]{:S(2)}) collective-permute-start(bf16[256,256]{1,0:T(8,128)(2,1)S(1)} %constant_dynamic-update-slice_fusion), channel_id=1, source_target_pairs={{0,112},{8,120},{16,128},{24,136},{32,144},{40,152},{48,160},{56,1... | collective-permute-start | bytes 393224 | tf_op jit(solution)/shard_map/ppermute | solution.py:523
  119.6 2.0 %collective-permute-start.8 = (bf16[256,256]{1,0:T(8,128)(2,1)S(1)}, bf16[256,256]{1,0:T(8,128)(2,1)S(1)}, u32[]{:S(2)}, u32[]{:S(2)}) collective-permute-start(bf16[256,256]{1,0:T(8,128)(2,1)S(1)} %constant_dynamic-update-slice_fusion), channel_id=1, source_target_pairs={{0,144},{8,152},{16,160},{24,168},{32,176},{40,184},{48,192},{56,2... | collective-permute-start | bytes 393224 | tf_op jit(solution)/shard_map/ppermute | solution.py:523
  122.4 2.2 %collective-permute-start.9 = (bf16[256,256]{1,0:T(8,128)(2,1)S(1)}, bf16[256,256]{1,0:T(8,128)(2,1)S(1)}, u32[]{:S(2)}, u32[]{:S(2)}) collective-permute-start(bf16[256,256]{1,0:T(8,128)(2,1)S(1)} %constant_dynamic-update-slice_fusion), channel_id=1, source_target_pairs={{0,160},{8,168},{16,176},{24,184},{32,192},{40,200},{48,208},{56,2... | collective-permute-start | bytes 393224 | tf_op jit(solution)/shard_map/ppermute | solution.py:523
  125.3 10.1 %collective-permute-done.5 = bf16[256,256]{1,0:T(8,128)(2,1)S(1)} collective-permute-done((bf16[256,256]{1,0:T(8,128)(2,1)S(1)}, bf16[256,256]{1,0:T(8,128)(2,1)S(1)}, u32[]{:S(2)}, u32[]{:S(2)}) %collective-permute-start.5) | collective-permute-done | bytes 131104 | tf_op jit(solution)/shard_map/ppermute | solution.py:523
  136.1 2.2 %collective-permute-done.6 = bf16[256,256]{1,0:T(8,128)(2,1)S(1)} collective-permute-done((bf16[256,256]{1,0:T(8,128)(2,1)S(1)}, bf16[256,256]{1,0:T(8,128)(2,1)S(1)}, u32[]{:S(2)}, u32[]{:S(2)}) %collective-permute-start.6) | collective-permute-done | bytes 131104 | tf_op jit(solution)/shard_map/ppermute | solution.py:523
  139.1 2.1 %collective-permute-done.7 = bf16[256,256]{1,0:T(8,128)(2,1)S(1)} collective-permute-done((bf16[256,256]{1,0:T(8,128)(2,1)S(1)}, bf16[256,256]{1,0:T(8,128)(2,1)S(1)}, u32[]{:S(2)}, u32[]{:S(2)}) %collective-permute-start.7) | collective-permute-done | bytes 131104 | tf_op jit(solution)/shard_map/ppermute | solution.py:523
  141.9 4.9 %collective-permute-start.13 = (bf16[256,256]{1,0:T(8,128)(2,1)S(1)}, bf16[256,256]{1,0:T(8,128)(2,1)S(1)}, u32[]{:S(2)}, u32[]{:S(2)}) collective-permute-start(bf16[256,256]{1,0:T(8,128)(2,1)S(1)} %constant_dynamic-update-slice_fusion), channel_id=1, source_target_pairs={{0,224},{8,232},{16,240},{24,248},{32,0},{40,8},{48,16},{56,24},{6... | collective-permute-start | bytes 393224 | tf_op jit(solution)/shard_map/ppermute | solution.py:523
  150.6 7.9 %collective-permute-done.13 = bf16[256,256]{1,0:T(8,128)(2,1)S(1)} collective-permute-done((bf16[256,256]{1,0:T(8,128)(2,1)S(1)}, bf16[256,256]{1,0:T(8,128)(2,1)S(1)}, u32[]{:S(2)}, u32[]{:S(2)}) %collective-permute-start.13) | collective-permute-done | bytes 131104 | tf_op jit(solution)/shard_map/ppermute | solution.py:523
  159.9 0.9 collective-permute-start.15
  163.3 1.7 collective-permute-done.15
  165.0 3.1 %constant_dynamic-update-slice_fusion.2 = bf16[32,256,256]{2,1,0:T(8,128)(2,1)} fusion(bf16[32,256,256]{2,1,0:T(8,128)(2,1)} %get-tuple-element.21, bf16[16,256,256]{2,1,0:T(8,128)(2,1)} %collective-permute-done.15), kind=kLoop, calls=%fused_computation.42 | loop fusion | bytes 4194304 | tf_op jit(solution)/shard_map/concatenate | solution.py:528
  168.1 29.1 %shard_map.133 = bf16[2,128,512]{2,1,0:T(8,128)(2,1)} custom-call(s32[2,4]{1,0:T(2,128)S(1)} %convert_element_type.19.wants, s32[4,16]{1,0:T(4,128)S(1)} %fusion.9.page_order, s32[2,64]{1,0:T(2,128)S(1)} %select_reduce_fusion.2.s_idx, s32[2]{0:T(128)S(1)} %get-tuple-element.17.s_cnt, bf16[2,128,512]{2,1,0:T(8,128)(2,1)S(1)} %copy-done, ...), custom_call_target="tpu_custom_call" | custom-call | tf_op jit(solution)/shard_map/pallas_call | solution.py:486
  (72 shorter events, 18.5 us)
Async XLA Ops:
  0.6 61.9 %copy-start.2 = (bf16[7168]{0:T(1024)(128)(2,1)S(1)}, bf16[7168]{0:T(1024)(128)(2,1)}, u32[]{:S(2)}) copy-start(bf16[7168]{0:T(1024)(128)(2,1)} %param.12) | copy-start | bytes 43012
  2.4 110.5 %collective-permute-start = (bf16[256,256]{1,0:T(8,128)(2,1)S(1)}, bf16[256,256]{1,0:T(8,128)(2,1)S(1)}, u32[]{:S(2)}, u32[]{:S(2)}) collective-permute-start(bf16[256,256]{1,0:T(8,128)(2,1)S(1)} %constant_dynamic-update-slice_fusion), channel_id=1, source_target_pairs={{0,16},{8,24},{16,32},{24,40},{32,48},{40,56},{48,64},{56,72},{64,... | collective-permute-start | bytes 393224 | tf_op jit(solution)/shard_map/ppermute | solution.py:523
  4.0 109.6 %collective-permute-start.1 = (bf16[256,256]{1,0:T(8,128)(2,1)S(1)}, bf16[256,256]{1,0:T(8,128)(2,1)S(1)}, u32[]{:S(2)}, u32[]{:S(2)}) collective-permute-start(bf16[256,256]{1,0:T(8,128)(2,1)S(1)} %constant_dynamic-update-slice_fusion), channel_id=1, source_target_pairs={{0,32},{8,40},{16,48},{24,56},{32,64},{40,72},{48,80},{56,88},{64,... | collective-permute-start | bytes 393224 | tf_op jit(solution)/shard_map/ppermute | solution.py:523
  6.1 112.7 %collective-permute-start.2 = (bf16[256,256]{1,0:T(8,128)(2,1)S(1)}, bf16[256,256]{1,0:T(8,128)(2,1)S(1)}, u32[]{:S(2)}, u32[]{:S(2)}) collective-permute-start(bf16[256,256]{1,0:T(8,128)(2,1)S(1)} %constant_dynamic-update-slice_fusion), channel_id=1, source_target_pairs={{0,48},{8,56},{16,64},{24,72},{32,80},{40,88},{48,96},{56,104},{64... | collective-permute-start | bytes 393224 | tf_op jit(solution)/shard_map/ppermute | solution.py:523
  7.1 112.5 %collective-permute-start.3 = (bf16[256,256]{1,0:T(8,128)(2,1)S(1)}, bf16[256,256]{1,0:T(8,128)(2,1)S(1)}, u32[]{:S(2)}, u32[]{:S(2)}) collective-permute-start(bf16[256,256]{1,0:T(8,128)(2,1)S(1)} %constant_dynamic-update-slice_fusion), channel_id=1, source_target_pairs={{0,64},{8,72},{16,80},{24,88},{32,96},{40,104},{48,112},{56,120},{... | collective-permute-start | bytes 393224 | tf_op jit(solution)/shard_map/ppermute | solution.py:523
  7.8 114.6 %collective-permute-start.4 = (bf16[256,256]{1,0:T(8,128)(2,1)S(1)}, bf16[256,256]{1,0:T(8,128)(2,1)S(1)}, u32[]{:S(2)}, u32[]{:S(2)}) collective-permute-start(bf16[256,256]{1,0:T(8,128)(2,1)S(1)} %constant_dynamic-update-slice_fusion), channel_id=1, source_target_pairs={{0,80},{8,88},{16,96},{24,104},{32,112},{40,120},{48,128},{56,136}... | collective-permute-start | bytes 393224 | tf_op jit(solution)/shard_map/ppermute | solution.py:523
  112.1 49.3 %copy-start.1 = (s32[8192]{0:T(1024)S(1)}, s32[8192]{0:T(1024)}, u32[]{:S(2)}) copy-start(s32[8192]{0:T(1024)} %param.21) | copy-start | bytes 98308
  112.1 50.3 %copy-start.3 = (s32[64]{0:T(128)S(1)}, s32[64]{0:T(128)}, u32[]{:S(2)}) copy-start(s32[64]{0:T(128)} %param.18) | copy-start | bytes 772
  112.8 22.5 %collective-permute-start.5 = (bf16[256,256]{1,0:T(8,128)(2,1)S(1)}, bf16[256,256]{1,0:T(8,128)(2,1)S(1)}, u32[]{:S(2)}, u32[]{:S(2)}) collective-permute-start(bf16[256,256]{1,0:T(8,128)(2,1)S(1)} %constant_dynamic-update-slice_fusion), channel_id=1, source_target_pairs={{0,96},{8,104},{16,112},{24,120},{32,128},{40,136},{48,144},{56,15... | collective-permute-start | bytes 393224 | tf_op jit(solution)/shard_map/ppermute | solution.py:523
  113.6 24.7 %collective-permute-start.6 = (bf16[256,256]{1,0:T(8,128)(2,1)S(1)}, bf16[256,256]{1,0:T(8,128)(2,1)S(1)}, u32[]{:S(2)}, u32[]{:S(2)}) collective-permute-start(bf16[256,256]{1,0:T(8,128)(2,1)S(1)} %constant_dynamic-update-slice_fusion), channel_id=1, source_target_pairs={{0,112},{8,120},{16,128},{24,136},{32,144},{40,152},{48,160},{56,1... | collective-permute-start | bytes 393224 | tf_op jit(solution)/shard_map/ppermute | solution.py:523
  118.9 22.2 %collective-permute-start.7 = (bf16[256,256]{1,0:T(8,128)(2,1)S(1)}, bf16[256,256]{1,0:T(8,128)(2,1)S(1)}, u32[]{:S(2)}, u32[]{:S(2)}) collective-permute-start(bf16[256,256]{1,0:T(8,128)(2,1)S(1)} %constant_dynamic-update-slice_fusion), channel_id=1, source_target_pairs={{0,128},{8,136},{16,144},{24,152},{32,160},{40,168},{48,176},{56,1... | collective-permute-start | bytes 393224 | tf_op jit(solution)/shard_map/ppermute | solution.py:523
  119.6 22.3 %collective-permute-start.8 = (bf16[256,256]{1,0:T(8,128)(2,1)S(1)}, bf16[256,256]{1,0:T(8,128)(2,1)S(1)}, u32[]{:S(2)}, u32[]{:S(2)}) collective-permute-start(bf16[256,256]{1,0:T(8,128)(2,1)S(1)} %constant_dynamic-update-slice_fusion), channel_id=1, source_target_pairs={{0,144},{8,152},{16,160},{24,168},{32,176},{40,184},{48,192},{56,2... | collective-permute-start | bytes 393224 | tf_op jit(solution)/shard_map/ppermute | solution.py:523
  122.4 25.1 %collective-permute-start.9 = (bf16[256,256]{1,0:T(8,128)(2,1)S(1)}, bf16[256,256]{1,0:T(8,128)(2,1)S(1)}, u32[]{:S(2)}, u32[]{:S(2)}) collective-permute-start(bf16[256,256]{1,0:T(8,128)(2,1)S(1)} %constant_dynamic-update-slice_fusion), channel_id=1, source_target_pairs={{0,160},{8,168},{16,176},{24,184},{32,192},{40,200},{48,208},{56,2... | collective-permute-start | bytes 393224 | tf_op jit(solution)/shard_map/ppermute | solution.py:523
  135.4 12.9 %collective-permute-start.10 = (bf16[256,256]{1,0:T(8,128)(2,1)S(1)}, bf16[256,256]{1,0:T(8,128)(2,1)S(1)}, u32[]{:S(2)}, u32[]{:S(2)}) collective-permute-start(bf16[256,256]{1,0:T(8,128)(2,1)S(1)} %constant_dynamic-update-slice_fusion), channel_id=1, source_target_pairs={{0,176},{8,184},{16,192},{24,200},{32,208},{40,216},{48,224},{56,2... | collective-permute-start | bytes 393224 | tf_op jit(solution)/shard_map/ppermute | solution.py:523
  138.3 10.7 %collective-permute-start.11 = (bf16[256,256]{1,0:T(8,128)(2,1)S(1)}, bf16[256,256]{1,0:T(8,128)(2,1)S(1)}, u32[]{:S(2)}, u32[]{:S(2)}) collective-permute-start(bf16[256,256]{1,0:T(8,128)(2,1)S(1)} %constant_dynamic-update-slice_fusion), channel_id=1, source_target_pairs={{0,192},{8,200},{16,208},{24,216},{32,224},{40,232},{48,240},{56,2... | collective-permute-start | bytes 393224 | tf_op jit(solution)/shard_map/ppermute | solution.py:523
  141.1 8.7 %collective-permute-start.12 = (bf16[256,256]{1,0:T(8,128)(2,1)S(1)}, bf16[256,256]{1,0:T(8,128)(2,1)S(1)}, u32[]{:S(2)}, u32[]{:S(2)}) collective-permute-start(bf16[256,256]{1,0:T(8,128)(2,1)S(1)} %constant_dynamic-update-slice_fusion), channel_id=1, source_target_pairs={{0,208},{8,216},{16,224},{24,232},{32,240},{40,248},{48,0},{56,8},... | collective-permute-start | bytes 393224 | tf_op jit(solution)/shard_map/ppermute | solution.py:523
  141.9 16.6 %collective-permute-start.13 = (bf16[256,256]{1,0:T(8,128)(2,1)S(1)}, bf16[256,256]{1,0:T(8,128)(2,1)S(1)}, u32[]{:S(2)}, u32[]{:S(2)}) collective-permute-start(bf16[256,256]{1,0:T(8,128)(2,1)S(1)} %constant_dynamic-update-slice_fusion), channel_id=1, source_target_pairs={{0,224},{8,232},{16,240},{24,248},{32,0},{40,8},{48,16},{56,24},{6... | collective-permute-start | bytes 393224 | tf_op jit(solution)/shard_map/ppermute | solution.py:523
  147.5 20.6 %copy-start = (bf16[2,128,512]{2,1,0:T(8,128)(2,1)S(1)}, bf16[2,128,512]{2,1,0:T(8,128)(2,1)}, u32[]{:S(2)}) copy-start(bf16[2,128,512]{2,1,0:T(8,128)(2,1)} %get-tuple-element.7.q_ref) | copy-start | bytes 786436
  147.5 11.7 %collective-permute-start.14 = (bf16[256,256]{1,0:T(8,128)(2,1)S(1)}, bf16[256,256]{1,0:T(8,128)(2,1)S(1)}, u32[]{:S(2)}, u32[]{:S(2)}) collective-permute-start(bf16[256,256]{1,0:T(8,128)(2,1)S(1)} %constant_dynamic-update-slice_fusion), channel_id=1, source_target_pairs={{0,240},{8,248},{16,0},{24,8},{32,16},{40,24},{48,32},{56,40},{64,... | collective-permute-start | bytes 393224 | tf_op jit(solution)/shard_map/ppermute | solution.py:523
  159.9 5.0 %collective-permute-start.15 = (bf16[16,256,256]{2,1,0:T(8,128)(2,1)}, bf16[16,256,256]{2,1,0:T(8,128)(2,1)}, u32[]{:S(2)}, u32[]{:S(2)}) collective-permute-start(bf16[16,256,256]{2,1,0:T(8,128)(2,1)} %get-tuple-element.20), channel_id=1, source_target_pairs={{0,8},{8,0},{16,24},{24,16},{32,40},{40,32},{48,56},{56,48},{64,72... | collective-permute-start | bytes 6291464 | tf_op jit(solution)/shard_map/ppermute | solution.py:527

commit v16 on v14

--- a/solution.py
+++ b/solution.py
@@ -329,7 +329,8 @@
 def project_kernel(x_ref, g_ref, wq_ref, wk_ref, wv_ref, cos_ref, sin_ref, q_ref, k_ref, v_ref, kv_ref):
     x = x_ref[...].astype(jnp.float32)
     mean_sq = jnp.mean(x * x, axis=1, keepdims=True)
-    normed = (x * lax.rsqrt(mean_sq + 1e-05) * g_ref[...].astype(jnp.float32)).astype(jnp.bfloat16)
+    gain = g_ref[...].astype(jnp.float32).reshape(1, x.shape[1])
+    normed = (x * lax.rsqrt(mean_sq + 1e-05) * gain).astype(jnp.bfloat16)
     cosine = cos_ref[...]
     sine = sin_ref[...]
 
@@ -367,7 +368,7 @@
         ),
         in_specs=[
             pl.BlockSpec((block, width), lambda i: (i, 0)),
-            pl.BlockSpec((1, width), whole),
+            pl.BlockSpec(memory_space=pltpu.VMEM),
             pl.BlockSpec((width, q_width), whole),
             pl.BlockSpec((width, kv_width), whole),
             pl.BlockSpec((width, kv_width), whole),
@@ -381,7 +382,7 @@
             pl.BlockSpec((2, block, kv_width), lambda i: (0, i, 0)),
         ),
         compiler_params=pltpu.CompilerParams(vmem_limit_bytes=60 * 1024 * 1024),
-    )(gathered, norm_gain.reshape(1, width), w_query, w_key, w_value, cosine, sine)
+    )(gathered, norm_gain, w_query, w_key, w_value, cosine, sine)
 
 
 def attention_kernel(

time: 162 us -> 151 us (0.932)
  the two profiles are of different devices: /device:TPU:165 before, /device:TPU:39 now
where the time goes in v16:
time: 151 us
  Pallas kernels  124 us (82%)
  between operations  14.2 us (9%)
  other arithmetic  8.56 us (6%)
  local copies, waits for them, and re-layouts  3.97 us (3%)
    pallas_call x1, Pallas kernels, tp_gather(): pl.pallas_call(functools.partial(tp_gather_kernel, n // 2), out_shape=jax...  52.3 us
    pallas_call x1, Pallas kernels, seq_gather(): pl.pallas_call(functools.partial(seq_gather_kernel, zs, xs), out_shape=ja...  37.8 us
    pallas_call x1, Pallas kernels, block_attention(): pl.pallas_call(functools.partial(attention_kernel, scale, 4), out_shape=j...  23.4 us
    pallas_call x1, Pallas kernels, project(): pl.pallas_call(project_kernel, grid=(steps,), out_shape=(jax.ShapeDtypeSt...  10.6 us
  transfers between devices with their start and end apart: 1, of which 0 were waited for; matrix products, arithmetic and copies ran while one was open for 6% of the time, Pallas kernels for 67%

profile of v16, /device:TPU:39, one launch (start us, length us, event | category | flops | bytes accessed | tf_op | source)
XLA Modules:
  0.0 151.0 jit_solution(14924699937320573127)
XLA Ops:
  7.2 1.5 %pad_maximum_fusion.2 = bf16[256,256]{1,0:T(8,128)(2,1)} fusion(bf16[256,128]{1,0:T(8,128)(2,1)} %param.17, bf16[256,128]{1,0:T(8,128)(2,1)} %param.16), kind=kLoop, calls=%fused_computation.8 | loop fusion | flops 262144 | bytes 262144 | tf_op jit(solution)/shard_map/concatenate | solution.py:522
  8.8 0.7 copy.19
  9.6 0.1 reduce
  9.7 0.7 sub.9
  10.4 1.0 convert_reduce_fusion
  11.3 1.0 select_reduce_fusion
  12.4 0.8 sub.10
  13.2 0.1 fusion.2
  13.4 0.9 bitcast_reduce_fusion.2
  14.3 0.3 reshape.259.q_pos
  14.7 0.3 reshape.258.q_req
  15.0 0.3 reshape.257.q_want
  15.4 52.3 %shard_map.130.x_ref = bf16[256,7168]{1,0:T(8,128)(2,1)} custom-call(bf16[256,896]{1,0:T(8,128)(2,1)} %x_ref.1), custom_call_target="tpu_custom_call" | custom-call | tf_op jit(solution)/shard_map/pallas_call | solution.py:311
  67.8 0.5 fusion.1
  68.4 0.8 pad_maximum_fusion
  69.2 10.6 %shard_map.131 = (bf16[2,128,512]{2,1,0:T(8,128)(2,1)}, bf16[256,128]{1,0:T(8,128)(2,1)}, bf16[256,128]{1,0:T(8,128)(2,1)}, bf16[2,256,128]{2,1,0:T(8,128)(2,1)}) custom-call(bf16[256,7168]{1,0:T(8,128)(2,1)} %shard_map.130.x_ref, bf16[7168]{0:T(1024)(128)(2,1)} %g_ref.1, bf16[7168,512]{1,0:T(8,128)(2,1)} %wq_ref.1, bf16[7168,128]{1,0:T(8,128)(2,1)} %wk_ref.1, ...), custom_call_target="tpu_custom_call" | custom-call | tf_op jit(solution)/shard_map/pallas_call | solution.py:360
  79.8 37.8 %shard_map.132 = bf16[2,4,4,2,256,128]{5,4,3,2,1,0:T(8,128)(2,1)} custom-call(bf16[2,256,128]{2,1,0:T(8,128)(2,1)} %get-tuple-element.8.x_ref), custom_call_target="tpu_custom_call" | custom-call | tf_op jit(solution)/shard_map/pallas_call | solution.py:191
  117.8 0.1 select_reduce_fusion.3.page_order
  118.0 0.1 bitcast_reduce_fusion.1
  118.1 0.2 convert_reduce_fusion.3
  118.3 0.1 convert_reduce_fusion.1
  118.4 0.1 select_reduce_fusion.2.s_idx
  118.5 2.2 %copy-done = bf16[8192,256]{1,0:T(8,128)(2,1)S(1)} copy-done((bf16[8192,256]{1,0:T(8,128)(2,1)S(1)}, bf16[8192,256]{1,0:T(8,128)(2,1)}, u32[]{:S(2)}) %copy-start) | copy-done | bytes 4194328
  120.7 23.4 %shard_map.133 = bf16[2,128,512]{2,1,0:T(8,128)(2,1)} custom-call(s32[2,4]{1,0:T(2,128)S(1)} %convert_element_type.19.wants, s32[4,16]{1,0:T(4,128)S(1)} %select_reduce_fusion.3.page_order, s32[2,64]{1,0:T(2,128)S(1)} %select_reduce_fusion.2.s_idx, s32[2]{0:T(128)S(1)} %get-tuple-element.17.s_cnt, bf16[2,128,512]{2,1,0:T(8,128)(2,1)S(1)} %copy-done.1, ...), custom_call_target="tpu_custom_call" | custom-call | tf_op jit(solution)/shard_map/pallas_call | solution.py:487
  (23 shorter events, 0.5 us)
Async XLA Ops:
  7.2 111.4 %all-gather.2.cloned.1.call-start = ((), (), s32[]{:S(2)}) async-start(), calls=%async_computation | async-start | bytes 4325376 | tf_op jit(solution)/shard_map/all_gather | solution.py:521
  79.8 37.9 %copy-start.3 = (s32[64]{0:T(128)S(1)}, s32[64]{0:T(128)}, u32[]{:S(2)}) copy-start(s32[64]{0:T(128)} %param.18) | copy-start | bytes 772
  79.8 38.1 %copy-start.2 = (s32[8192]{0:T(1024)S(1)}, s32[8192]{0:T(1024)}, u32[]{:S(2)}) copy-start(s32[8192]{0:T(1024)} %param.21) | copy-start | bytes 98308
  79.8 38.7 %copy-start.1 = (bf16[2,128,512]{2,1,0:T(8,128)(2,1)S(1)}, bf16[2,128,512]{2,1,0:T(8,128)(2,1)}, u32[]{:S(2)}) copy-start(bf16[2,128,512]{2,1,0:T(8,128)(2,1)} %get-tuple-element.7.q_ref) | copy-start | bytes 786436
  118.5 2.2 %copy-start = (bf16[8192,256]{1,0:T(8,128)(2,1)S(1)}, bf16[8192,256]{1,0:T(8,128)(2,1)}, u32[]{:S(2)}) copy-start(bf16[8192,256]{1,0:T(8,128)(2,1)} %all-gather.2.cloned.1.call-done) | copy-start | bytes 12582916
Sparse Core Ops, SparseCore 0:
  9.9 80.9 all-gather.1

commit v17 on v16

--- a/solution.py
+++ b/solution.py
@@ -388,7 +388,7 @@
 def attention_kernel(
     scale, group_pages,
     wants, page_order, s_idx, s_cnt,
-    q_ref, q_want, q_req, q_pos,
+    q_ref, q_meta,
     p_ref,
     s_ref, s_tag, s_bound,
     o_ref, m_sc, l_sc, acc_sc, pm_sc, pl_sc, pacc_sc,
@@ -418,9 +418,9 @@
         heads = q_ref.shape[2] // q_ref.shape[1]
         size = q_ref.shape[1]
         query = jnp.concatenate([q_ref[i, :, h * size:(h + 1) * size] for h in range(heads)], axis=0)
-        want = q_want[i]
-        req = q_req[i]
-        pos = q_pos[i]
+        want = q_meta[0, i]
+        req = q_meta[1, i]
+        pos = q_meta[2, i]
 
         def score(keys):
             return lax.dot_general(
@@ -487,7 +487,7 @@
     return pl.pallas_call(
         functools.partial(attention_kernel, scale, 4),
         out_shape=jax.ShapeDtypeStruct((q_blocks, block_rows, q_width), jnp.bfloat16),
-        in_specs=[smem] * 4 + [vmem] * 8,
+        in_specs=[smem] * 4 + [vmem] * 6,
         out_specs=vmem,
         scratch_shapes=state + state,
         compiler_params=pltpu.CompilerParams(vmem_limit_bytes=48 * 1024 * 1024),
@@ -535,11 +535,11 @@
     group_size = q_heads // kv_heads
     half_dim = HEAD // 2
     frequency = ROPE_BASE ** (-(jnp.arange(half_dim, dtype=jnp.float32) * 2.0 / HEAD))
-    angles = rope_at.astype(jnp.float32)[:, None] * frequency[None, :]
-    cosine = jnp.cos(angles)
-    sine_part = jnp.sin(angles)
-    cos_full = jnp.concatenate([cosine, cosine], axis=1)
-    sin_signed = jnp.concatenate([-sine_part, sine_part], axis=1)
+    frequency_full = jnp.concatenate([frequency, frequency])
+    sign_full = jnp.concatenate([-jnp.ones((half_dim,), jnp.float32), jnp.ones((half_dim,), jnp.float32)])
+    angles = rope_at.astype(jnp.float32)[:, None] * frequency_full[None, :]
+    cos_full = jnp.cos(angles)
+    sin_signed = jnp.sin(angles) * sign_full[None, :]
     stacked_q, new_keys, new_values, stacked_kv = project(
         gathered, norm_gain, w_query, w_key, w_value, cos_full, sin_signed, PAGE
     )
@@ -550,10 +550,11 @@
     runs = row_order.shape[0] // block
 
     def per_query(values):
-        spread = jnp.broadcast_to(values.reshape(q_blocks, 1, block), (q_blocks, group_size, block))
-        return spread.reshape(q_blocks, group_size * block, 1).astype(jnp.int32)
-
-    query_meta = (per_query(wanted), per_query(request + PREFIXES), per_query(position))
+        kinds = values.shape[0]
+        spread = jnp.broadcast_to(values.reshape(kinds, q_blocks, 1, block), (kinds, q_blocks, group_size, block))
+        return spread.reshape(kinds, q_blocks, group_size * block, 1).astype(jnp.int32)
+
+    query_meta = (per_query(jnp.stack([wanted, request + PREFIXES, position])),)
     want_blocks = wanted.reshape(q_blocks, block)
     block_wants = jnp.any(
         want_blocks[:, :, None] == jnp.arange(PREFIXES, dtype=jnp.int32)[None, None, :], axis=1

time: 151 us -> 150 us (level)
  the two profiles are of different devices: /device:TPU:39 before, /device:TPU:166 now
where the time goes in v17:
time: 150 us
  Pallas kernels  123 us (82%)
  between operations  14.2 us (9%)
  other arithmetic  7.8 us (5%)
  local copies, waits for them, and re-layouts  4.4 us (3%)
    pallas_call x1, Pallas kernels, tp_gather(): pl.pallas_call(functools.partial(tp_gather_kernel, n // 2), out_shape=jax...  51.7 us
    pallas_call x1, Pallas kernels, seq_gather(): pl.pallas_call(functools.partial(seq_gather_kernel, zs, xs), out_shape=ja...  37.9 us
    pallas_call x1, Pallas kernels, block_attention(): pl.pallas_call(functools.partial(attention_kernel, scale, 4), out_shape=j...  22.9 us
    pallas_call x1, Pallas kernels, project(): pl.pallas_call(project_kernel, grid=(steps,), out_shape=(jax.ShapeDtypeSt...  10.6 us
  transfers between devices with their start and end apart: 1, of which 0 were waited for; matrix products, arithmetic and copies ran while one was open for 6% of the time, Pallas kernels for 67%

profile of v17, /device:TPU:166, one launch (start us, length us, event | category | flops | bytes accessed | tf_op | source)
XLA Modules:
  0.0 149.5 jit_solution(1175332340350854356)
XLA Ops:
  7.2 1.5 %pad_maximum_fusion = bf16[256,256]{1,0:T(8,128)(2,1)} fusion(bf16[256,128]{1,0:T(8,128)(2,1)} %param.17, bf16[256,128]{1,0:T(8,128)(2,1)} %param.16), kind=kLoop, calls=%fused_computation.7 | loop fusion | flops 262144 | bytes 262144 | tf_op jit(solution)/shard_map/concatenate | solution.py:522
  8.8 0.7 copy.17
  9.6 0.1 reduce
  9.7 0.7 sub.9
  10.4 1.0 convert_reduce_fusion
  11.4 1.0 select_reduce_fusion
  12.4 0.8 sub.10
  13.2 0.1 fusion.2
  13.4 0.1 dynamic-slice_bitcast_fusion.2
  13.5 1.5 reshape.245.q_meta
  14.9 51.7 %shard_map.130.x_ref = bf16[256,7168]{1,0:T(8,128)(2,1)} custom-call(bf16[256,896]{1,0:T(8,128)(2,1)} %x_ref.1), custom_call_target="tpu_custom_call" | custom-call | tf_op jit(solution)/shard_map/pallas_call | solution.py:311
  66.7 0.1 pad_maximum_fusion.1
  66.8 1.2 fusion
  68.0 10.6 %shard_map.131 = (bf16[2,128,512]{2,1,0:T(8,128)(2,1)}, bf16[256,128]{1,0:T(8,128)(2,1)}, bf16[256,128]{1,0:T(8,128)(2,1)}, bf16[2,256,128]{2,1,0:T(8,128)(2,1)}) custom-call(bf16[256,7168]{1,0:T(8,128)(2,1)} %shard_map.130.x_ref, bf16[7168]{0:T(1024)(128)(2,1)} %g_ref.1, bf16[7168,512]{1,0:T(8,128)(2,1)} %wq_ref.1, bf16[7168,128]{1,0:T(8,128)(2,1)} %wk_ref.1, ...), custom_call_target="tpu_custom_call" | custom-call | tf_op jit(solution)/shard_map/pallas_call | solution.py:360
  78.6 37.9 %shard_map.132 = bf16[2,4,4,2,256,128]{5,4,3,2,1,0:T(8,128)(2,1)} custom-call(bf16[2,256,128]{2,1,0:T(8,128)(2,1)} %get-tuple-element.8.x_ref), custom_call_target="tpu_custom_call" | custom-call | tf_op jit(solution)/shard_map/pallas_call | solution.py:191
  116.5 0.2 bitcast_reduce_fusion.2
  116.7 0.1 convert_reduce_fusion.2
  116.8 0.1 select_reduce_fusion.3.page_order
  117.0 0.1 bitcast_reduce_fusion.1
  117.1 0.2 convert_reduce_fusion.3
  117.3 0.1 convert_reduce_fusion.1
  117.4 0.1 select_reduce_fusion.2.s_idx
  117.6 2.2 %copy-done = bf16[8192,256]{1,0:T(8,128)(2,1)S(1)} copy-done((bf16[8192,256]{1,0:T(8,128)(2,1)S(1)}, bf16[8192,256]{1,0:T(8,128)(2,1)}, u32[]{:S(2)}) %copy-start) | copy-done | bytes 4194328
  119.8 22.9 %shard_map.133 = bf16[2,128,512]{2,1,0:T(8,128)(2,1)} custom-call(s32[2,4]{1,0:T(2,128)S(1)} %convert_element_type.19.wants, s32[4,16]{1,0:T(4,128)S(1)} %select_reduce_fusion.3.page_order, s32[2,64]{1,0:T(2,128)S(1)} %select_reduce_fusion.2.s_idx, s32[2]{0:T(128)S(1)} %get-tuple-element.17.s_cnt, bf16[2,128,512]{2,1,0:T(8,128)(2,1)S(1)} %copy-done.1, ...), custom_call_target="tpu_custom_call" | custom-call | tf_op jit(solution)/shard_map/pallas_call | solution.py:487
  (22 shorter events, 0.3 us)
Async XLA Ops:
  7.2 59.6 %copy-start.3 = (f32[128]{0:T(128)S(1)}, f32[128]{0:T(128)}, u32[]{:S(2)}) copy-start(f32[128]{0:T(128)} %constant.34.clone.1) | copy-start | bytes 1540
  7.2 110.4 %all-gather.2.cloned.1.call-start = ((), (), s32[]{:S(2)}) async-start(), calls=%async_computation | async-start | bytes 4325376 | tf_op jit(solution)/shard_map/all_gather | solution.py:521
  78.6 37.9 %copy-start.2 = (s32[8192]{0:T(1024)S(1)}, s32[8192]{0:T(1024)}, u32[]{:S(2)}) copy-start(s32[8192]{0:T(1024)} %param.21) | copy-start | bytes 98308
  78.6 38.1 %copy-start.4 = (s32[64]{0:T(128)S(1)}, s32[64]{0:T(128)}, u32[]{:S(2)}) copy-start(s32[64]{0:T(128)} %param.18) | copy-start | bytes 772
  78.6 39.0 %copy-start.1 = (bf16[2,128,512]{2,1,0:T(8,128)(2,1)S(1)}, bf16[2,128,512]{2,1,0:T(8,128)(2,1)}, u32[]{:S(2)}) copy-start(bf16[2,128,512]{2,1,0:T(8,128)(2,1)} %get-tuple-element.7.q_ref) | copy-start | bytes 786436
  117.6 2.2 %copy-start = (bf16[8192,256]{1,0:T(8,128)(2,1)S(1)}, bf16[8192,256]{1,0:T(8,128)(2,1)}, u32[]{:S(2)}) copy-start(bf16[8192,256]{1,0:T(8,128)(2,1)} %all-gather.2.cloned.1.call-done) | copy-start | bytes 12582916
Sparse Core Ops, SparseCore 0:
  9.9 74.8 all-gather.1

commit v18 on v17

--- a/solution.py
+++ b/solution.py
@@ -535,11 +535,11 @@
     group_size = q_heads // kv_heads
     half_dim = HEAD // 2
     frequency = ROPE_BASE ** (-(jnp.arange(half_dim, dtype=jnp.float32) * 2.0 / HEAD))
-    frequency_full = jnp.concatenate([frequency, frequency])
-    sign_full = jnp.concatenate([-jnp.ones((half_dim,), jnp.float32), jnp.ones((half_dim,), jnp.float32)])
-    angles = rope_at.astype(jnp.float32)[:, None] * frequency_full[None, :]
-    cos_full = jnp.cos(angles)
-    sin_signed = jnp.sin(angles) * sign_full[None, :]
+    angles = rope_at.astype(jnp.float32)[:, None] * frequency[None, :]
+    cosine = jnp.cos(angles)
+    sine_part = jnp.sin(angles)
+    cos_full = jnp.concatenate([cosine, cosine], axis=1)
+    sin_signed = jnp.concatenate([-sine_part, sine_part], axis=1)
     stacked_q, new_keys, new_values, stacked_kv = project(
         gathered, norm_gain, w_query, w_key, w_value, cos_full, sin_signed, PAGE
     )

time: 150 us -> 150 us (level)
  the two profiles are of different devices: /device:TPU:166 before, /device:TPU:165 now
where the time goes in v18:
time: 150 us; the launch traced here: 148 us
  Pallas kernels  122 us (81%)
  between operations  14.2 us (9%)
  other arithmetic  7.87 us (5%)
  local copies, waits for them, and re-layouts  4.4 us (3%)
    pallas_call x1, Pallas kernels, tp_gather(): pl.pallas_call(functools.partial(tp_gather_kernel, n // 2), out_shape=jax...  47.6 us
    pallas_call x1, Pallas kernels, seq_gather(): pl.pallas_call(functools.partial(seq_gather_kernel, zs, xs), out_shape=ja...  41.4 us
    pallas_call x1, Pallas kernels, block_attention(): pl.pallas_call(functools.partial(attention_kernel, scale, 4), out_shape=j...  21.9 us
    pallas_call x1, Pallas kernels, project(): pl.pallas_call(project_kernel, grid=(steps,), out_shape=(jax.ShapeDtypeSt...  10.6 us
  transfers between devices with their start and end apart: 1, of which 0 were waited for; matrix products, arithmetic and copies ran while one was open for 6% of the time, Pallas kernels for 67%

profile of v18, /device:TPU:165, one launch (start us, length us, event | category | flops | bytes accessed | tf_op | source)
XLA Modules:
  0.0 148.0 jit_solution(8924383008982065511)
XLA Ops:
  7.2 1.5 %pad_maximum_fusion.2 = bf16[256,256]{1,0:T(8,128)(2,1)} fusion(bf16[256,128]{1,0:T(8,128)(2,1)} %param.17, bf16[256,128]{1,0:T(8,128)(2,1)} %param.16), kind=kLoop, calls=%fused_computation.8 | loop fusion | flops 262144 | bytes 262144 | tf_op jit(solution)/shard_map/concatenate | solution.py:522
  8.8 0.7 copy.17
  9.6 0.1 reduce
  9.7 0.7 sub.9
  10.4 1.0 convert_reduce_fusion
  11.3 1.0 select_reduce_fusion
  12.4 0.8 sub.10
  13.2 0.1 fusion.2
  13.4 0.1 dynamic-slice_bitcast_fusion.2
  13.5 1.5 reshape.250.q_meta
  14.9 47.6 %shard_map.130.x_ref = bf16[256,7168]{1,0:T(8,128)(2,1)} custom-call(bf16[256,896]{1,0:T(8,128)(2,1)} %x_ref.1), custom_call_target="tpu_custom_call" | custom-call | tf_op jit(solution)/shard_map/pallas_call | solution.py:311
  62.6 0.5 fusion.1
  63.1 0.8 pad_maximum_fusion
  64.0 10.6 %shard_map.131 = (bf16[2,128,512]{2,1,0:T(8,128)(2,1)}, bf16[256,128]{1,0:T(8,128)(2,1)}, bf16[256,128]{1,0:T(8,128)(2,1)}, bf16[2,256,128]{2,1,0:T(8,128)(2,1)}) custom-call(bf16[256,7168]{1,0:T(8,128)(2,1)} %shard_map.130.x_ref, bf16[7168]{0:T(1024)(128)(2,1)} %g_ref.1, bf16[7168,512]{1,0:T(8,128)(2,1)} %wq_ref.1, bf16[7168,128]{1,0:T(8,128)(2,1)} %wk_ref.1, ...), custom_call_target="tpu_custom_call" | custom-call | tf_op jit(solution)/shard_map/pallas_call | solution.py:360
  74.6 41.4 %shard_map.132 = bf16[2,4,4,2,256,128]{5,4,3,2,1,0:T(8,128)(2,1)} custom-call(bf16[2,256,128]{2,1,0:T(8,128)(2,1)} %get-tuple-element.8.x_ref), custom_call_target="tpu_custom_call" | custom-call | tf_op jit(solution)/shard_map/pallas_call | solution.py:191
  116.0 0.2 bitcast_reduce_fusion.2
  116.2 0.1 convert_reduce_fusion.2
  116.4 0.1 select_reduce_fusion.3.page_order
  116.5 0.1 bitcast_reduce_fusion.1
  116.6 0.2 convert_reduce_fusion.3
  116.8 0.1 convert_reduce_fusion.1
  116.9 0.1 select_reduce_fusion.2.s_idx
  117.1 2.2 %copy-done = bf16[8192,256]{1,0:T(8,128)(2,1)S(1)} copy-done((bf16[8192,256]{1,0:T(8,128)(2,1)S(1)}, bf16[8192,256]{1,0:T(8,128)(2,1)}, u32[]{:S(2)}) %copy-start) | copy-done | bytes 4194328
  119.3 21.9 %shard_map.133 = bf16[2,128,512]{2,1,0:T(8,128)(2,1)} custom-call(s32[2,4]{1,0:T(2,128)S(1)} %convert_element_type.19.wants, s32[4,16]{1,0:T(4,128)S(1)} %select_reduce_fusion.3.page_order, s32[2,64]{1,0:T(2,128)S(1)} %select_reduce_fusion.2.s_idx, s32[2]{0:T(128)S(1)} %get-tuple-element.17.s_cnt, bf16[2,128,512]{2,1,0:T(8,128)(2,1)S(1)} %copy-done.1, ...), custom_call_target="tpu_custom_call" | custom-call | tf_op jit(solution)/shard_map/pallas_call | solution.py:487
  (20 shorter events, 0.3 us)
Async XLA Ops:
  7.2 109.9 %all-gather.2.cloned.1.call-start = ((), (), s32[]{:S(2)}) async-start(), calls=%async_computation | async-start | bytes 4325376 | tf_op jit(solution)/shard_map/all_gather | solution.py:521
  74.6 41.4 %copy-start.2 = (s32[8192]{0:T(1024)S(1)}, s32[8192]{0:T(1024)}, u32[]{:S(2)}) copy-start(s32[8192]{0:T(1024)} %param.21) | copy-start | bytes 98308
  74.6 41.7 %copy-start.3 = (s32[64]{0:T(128)S(1)}, s32[64]{0:T(128)}, u32[]{:S(2)}) copy-start(s32[64]{0:T(128)} %param.18) | copy-start | bytes 772
  74.6 42.5 %copy-start.1 = (bf16[2,128,512]{2,1,0:T(8,128)(2,1)S(1)}, bf16[2,128,512]{2,1,0:T(8,128)(2,1)}, u32[]{:S(2)}) copy-start(bf16[2,128,512]{2,1,0:T(8,128)(2,1)} %get-tuple-element.7.q_ref) | copy-start | bytes 786436
  117.1 2.2 %copy-start = (bf16[8192,256]{1,0:T(8,128)(2,1)S(1)}, bf16[8192,256]{1,0:T(8,128)(2,1)}, u32[]{:S(2)}) copy-start(bf16[8192,256]{1,0:T(8,128)(2,1)} %all-gather.2.cloned.1.call-done) | copy-start | bytes 12582916
Sparse Core Ops, SparseCore 0:
  9.9 75.2 all-gather.1

commit v19 on v18

--- a/solution.py
+++ b/solution.py
@@ -390,7 +390,7 @@
     wants, page_order, s_idx, s_cnt,
     q_ref, q_meta,
     p_ref,
-    s_ref, s_tag, s_bound,
+    s_ref, s_meta,
     o_ref, m_sc, l_sc, acc_sc, pm_sc, pl_sc, pacc_sc,
 ):
     prefixes, per_prefix = page_order.shape
@@ -453,7 +453,7 @@
         def step(n, carry):
             b = s_idx[i, n]
             scores = score(s_ref[0, b])
-            seen = (s_tag[b] == req) & (s_bound[b] <= pos)
+            seen = (s_meta[0, b] == req) & (s_meta[1, b] <= pos)
             run_max = m_sc[...]
             new_max = jnp.maximum(
                 run_max, jnp.max(jnp.where(seen, scores, -1e30), axis=1, keepdims=True)
@@ -487,7 +487,7 @@
     return pl.pallas_call(
         functools.partial(attention_kernel, scale, 4),
         out_shape=jax.ShapeDtypeStruct((q_blocks, block_rows, q_width), jnp.bfloat16),
-        in_specs=[smem] * 4 + [vmem] * 6,
+        in_specs=[smem] * 4 + [vmem] * 5,
         out_specs=vmem,
         scratch_shapes=state + state,
         compiler_params=pltpu.CompilerParams(vmem_limit_bytes=48 * 1024 * 1024),
@@ -581,8 +581,7 @@
     gathered_suffix = seq_gather(stacked_kv, seq_n_blocks, 1)
     suffix_parts = (
         gathered_suffix.reshape(2, runs, block, HEAD),
-        (request_all + PREFIXES).reshape(runs, 1, block).astype(jnp.int32),
-        position_all.reshape(runs, 1, block).astype(jnp.int32),
+        jnp.stack([request_all + PREFIXES, position_all]).reshape(2, runs, 1, block).astype(jnp.int32),
     )
     out = block_attention(
         score_scale, (block_wants.astype(jnp.int32), page_order, s_idx, s_cnt), stacked_q, query_meta, prefix_parts, suffix_parts

time: 150 us -> 154 us (1.027)
  Pallas kernels: 122 us -> 126 us
    pallas_call x1, Pallas kernels: 21.9 us -> 26.1 us  [block_attention(): pl.pallas_call(functools.partial(attention_kernel, scale, 4), out_shape=j...]
  transfers between devices with their start and end apart: 1 -> 1, of which waited for: 0 -> 0; matrix products, arithmetic and copies ran while one was open for 6% -> 6% of each run, Pallas kernels for 67% -> 65%
where the time goes in v19:
time: 154 us; the launch traced here: 152 us
  Pallas kernels  126 us (82%)
  between operations  14.2 us (9%)
  other arithmetic  7.88 us (5%)
  local copies, waits for them, and re-layouts  4.4 us (3%)
    pallas_call x1, Pallas kernels, tp_gather(): pl.pallas_call(functools.partial(tp_gather_kernel, n // 2), out_shape=jax...  47.6 us
    pallas_call x1, Pallas kernels, seq_gather(): pl.pallas_call(functools.partial(seq_gather_kernel, zs, xs), out_shape=ja...  41.4 us
    pallas_call x1, Pallas kernels, block_attention(): pl.pallas_call(functools.partial(attention_kernel, scale, 4), out_shape=j...  26.1 us
    pallas_call x1, Pallas kernels, project(): pl.pallas_call(project_kernel, grid=(steps,), out_shape=(jax.ShapeDtypeSt...  10.6 us
  transfers between devices with their start and end apart: 1, of which 0 were waited for; matrix products, arithmetic and copies ran while one was open for 6% of the time, Pallas kernels for 65%

profile of v19, /device:TPU:165, one launch (start us, length us, event | category | flops | bytes accessed | tf_op | source)
XLA Modules:
  0.0 152.3 jit_solution(9124682491032363981)
XLA Ops:
  7.2 1.5 %pad_maximum_fusion.2 = bf16[256,256]{1,0:T(8,128)(2,1)} fusion(bf16[256,128]{1,0:T(8,128)(2,1)} %param.17, bf16[256,128]{1,0:T(8,128)(2,1)} %param.16), kind=kLoop, calls=%fused_computation.8 | loop fusion | flops 262144 | bytes 262144 | tf_op jit(solution)/shard_map/concatenate | solution.py:522
  8.8 0.7 copy.17
  9.6 0.1 reduce
  9.7 0.7 sub.9
  10.4 1.0 convert_reduce_fusion
  11.3 1.0 select_reduce_fusion
  12.4 0.8 sub.10
  13.2 0.1 fusion.2
  13.4 0.1 dynamic-slice_bitcast_fusion.2
  13.5 1.5 reshape.250.q_meta
  14.9 47.6 %shard_map.130.x_ref = bf16[256,7168]{1,0:T(8,128)(2,1)} custom-call(bf16[256,896]{1,0:T(8,128)(2,1)} %x_ref.1), custom_call_target="tpu_custom_call" | custom-call | tf_op jit(solution)/shard_map/pallas_call | solution.py:311
  62.6 0.5 fusion.1
  63.1 0.8 pad_maximum_fusion
  64.0 10.6 %shard_map.131 = (bf16[2,128,512]{2,1,0:T(8,128)(2,1)}, bf16[256,128]{1,0:T(8,128)(2,1)}, bf16[256,128]{1,0:T(8,128)(2,1)}, bf16[2,256,128]{2,1,0:T(8,128)(2,1)}) custom-call(bf16[256,7168]{1,0:T(8,128)(2,1)} %shard_map.130.x_ref, bf16[7168]{0:T(1024)(128)(2,1)} %g_ref.1, bf16[7168,512]{1,0:T(8,128)(2,1)} %wq_ref.1, bf16[7168,128]{1,0:T(8,128)(2,1)} %wk_ref.1, ...), custom_call_target="tpu_custom_call" | custom-call | tf_op jit(solution)/shard_map/pallas_call | solution.py:360
  74.6 41.4 %shard_map.132 = bf16[2,4,4,2,256,128]{5,4,3,2,1,0:T(8,128)(2,1)} custom-call(bf16[2,256,128]{2,1,0:T(8,128)(2,1)} %get-tuple-element.8.x_ref), custom_call_target="tpu_custom_call" | custom-call | tf_op jit(solution)/shard_map/pallas_call | solution.py:191
  116.0 0.2 bitcast_reduce_fusion.2
  116.2 0.1 convert_reduce_fusion.2
  116.4 0.1 select_reduce_fusion.3.page_order
  116.5 0.1 bitcast_reduce_fusion.1
  116.6 0.2 convert_reduce_fusion.3
  116.8 0.1 convert_reduce_fusion.1
  116.9 0.1 select_reduce_fusion.2.s_idx
  117.1 2.2 %copy-done = bf16[8192,256]{1,0:T(8,128)(2,1)S(1)} copy-done((bf16[8192,256]{1,0:T(8,128)(2,1)S(1)}, bf16[8192,256]{1,0:T(8,128)(2,1)}, u32[]{:S(2)}) %copy-start) | copy-done | bytes 4194328
  119.3 26.1 %shard_map.133 = bf16[2,128,512]{2,1,0:T(8,128)(2,1)} custom-call(s32[2,4]{1,0:T(2,128)S(1)} %convert_element_type.19.wants, s32[4,16]{1,0:T(4,128)S(1)} %select_reduce_fusion.3.page_order, s32[2,64]{1,0:T(2,128)S(1)} %select_reduce_fusion.2.s_idx, s32[2]{0:T(128)S(1)} %get-tuple-element.17.s_cnt, bf16[2,128,512]{2,1,0:T(8,128)(2,1)S(1)} %copy-done.1, ...), custom_call_target="tpu_custom_call" | custom-call | tf_op jit(solution)/shard_map/pallas_call | solution.py:487
  (21 shorter events, 0.3 us)
Async XLA Ops:
  7.2 109.9 %all-gather.2.cloned.1.call-start = ((), (), s32[]{:S(2)}) async-start(), calls=%async_computation | async-start | bytes 4325376 | tf_op jit(solution)/shard_map/all_gather | solution.py:521
  74.6 41.4 %copy-start.2 = (s32[8192]{0:T(1024)S(1)}, s32[8192]{0:T(1024)}, u32[]{:S(2)}) copy-start(s32[8192]{0:T(1024)} %param.21) | copy-start | bytes 98308
  74.6 41.7 %copy-start.3 = (s32[64]{0:T(128)S(1)}, s32[64]{0:T(128)}, u32[]{:S(2)}) copy-start(s32[64]{0:T(128)} %param.18) | copy-start | bytes 772
  74.6 42.5 %copy-start.1 = (bf16[2,128,512]{2,1,0:T(8,128)(2,1)S(1)}, bf16[2,128,512]{2,1,0:T(8,128)(2,1)}, u32[]{:S(2)}) copy-start(bf16[2,128,512]{2,1,0:T(8,128)(2,1)} %get-tuple-element.7.q_ref) | copy-start | bytes 786436
  117.1 2.2 %copy-start = (bf16[8192,256]{1,0:T(8,128)(2,1)S(1)}, bf16[8192,256]{1,0:T(8,128)(2,1)}, u32[]{:S(2)}) copy-start(bf16[8192,256]{1,0:T(8,128)(2,1)} %all-gather.2.cloned.1.call-done) | copy-start | bytes 12582916
Sparse Core Ops, SparseCore 0:
  9.9 75.2 all-gather.1
